TPU v7x, 512 devices: a whole 4x4x16 slice. The times are simulated.
512 devices in a mesh: row: 8 (over y, core), col: 16 (over z), ch: 4 (over x).
Axes of the slice: x: 4, y: 4, z: 16, core: 2. Of those that a mesh axis runs over, the one named last changes fastest.
Arguments:
- image: bfloat16 [256, 32, 2048], P('ch', 'row', 'col'), may hold values from -6 to 6
- depth_kernel: float32 [256, 49], P('ch'), may hold values from -0.875 to 0.875
- norm_gain: float32 [256], P('ch'), may hold values from 0.25 to 1.75
- norm_shift: float32 [256], P('ch'), may hold values from -3 to 3
- expand_weight: bfloat16 [256, 1024], P(None, 'ch'), may hold values from -0.375 to 0.375
- expand_bias: float32 [1024], replicated, may hold values from -3 to 3
- reduce_weight: bfloat16 [1024, 256], P('ch'), may hold values from -0.1875 to 0.1875
- cotangent: bfloat16 [256, 32, 2048], P('ch', 'row', 'col'), may hold values from -6 to 6
Outputs:
- result: bfloat16 [256, 32, 2048], P('ch', 'row', 'col')
- grad_image: bfloat16 [256, 32, 2048], P('ch', 'row', 'col')
- grad_kernel: float32 [256, 49], P('ch')
- grad_gain: float32 [256], P('ch')
- grad_shift: float32 [256], P('ch')
- grad_expand: float32 [256, 1024], P(None, 'ch')
- grad_offset: float32 [1024], P('ch')
- grad_reduce: float32 [1024, 256], P('ch')
All inputs are finite; a program needn't handle non-finite values.
Results may differ from a plain program's by a relative error of at most 0.011.
Values may be sent and summed in bfloat16 or wider, within the bound.
No kernel may reach another device: no remote copies, remote signals or barrier semaphores. Data moves between devices by JAX's collectives and lax.ppermute only.
A program may use at most 64 MiB of HBM per device.

v0:
```python
import jax
import jax.numpy as jnp
from jax import lax
from jax.sharding import PartitionSpec as P

KSIZE = 7


epsilon = 1e-06
root_two_pi = 0.7978845608028654
cubic_coef = 0.044715


def padded_2(x, sides, width):
    for axis, dim in sides:
        size, length = (lax.axis_size(axis), x.shape[dim])
        up = [(i, (i + 1) % size) for i in range(size - 1)]
        down = [(j, i) for i, j in up]
        last = lax.slice_in_dim(x, length - width, length, axis=dim)
        leading = lax.slice_in_dim(x, 0, width, axis=dim)
        before = lax.ppermute(last, axis, up)
        after = lax.ppermute(leading, axis, down)
        x = jnp.concatenate([before, x, after], axis=dim)
    return x


def product(left, right, dims):
    return lax.dot_general(
        left.astype(jnp.float32),
        right.astype(jnp.float32),
        dims,
        preferred_element_type=jnp.float32,
    )


def gelu_pair(hidden):
    inner = root_two_pi * (hidden + cubic_coef * hidden * hidden * hidden)
    tangent = jnp.tanh(inner)
    value = 0.5 * hidden * (1.0 + tangent)
    slope = 0.5 * (1.0 + tangent) + 0.5 * hidden * (1.0 - tangent * tangent) * root_two_pi * (
        1.0 + 3.0 * cubic_coef * hidden * hidden
    )
    return (value, slope)


def tap_window(padded, kernel, tap, first, second, tile_rows, tile_cols):
    window = lax.dynamic_slice(
        padded, (jnp.int32(0), first, second), (padded.shape[0], tile_rows, tile_cols)
    )
    weight = lax.dynamic_slice_in_dim(kernel, tap, 1, 1)
    return weight[:, :, None] * window


def forward_taps(padded, kernel, span, tile_rows, tile_cols):

    def forward_step(tap, accum):
        tap = jnp.asarray(tap).astype(jnp.int32)
        first = tap // span
        second = tap % span
        return accum + tap_window(padded, kernel, tap, first, second, tile_rows, tile_cols)

    accum = jnp.zeros((padded.shape[0], tile_rows, tile_cols), jnp.float32)
    return lax.fori_loop(0, span * span, forward_step, accum)


def backward_taps(padded, kernel, span, tile_rows, tile_cols):
    reach = span - 1

    def backward_step(tap, accum):
        tap = jnp.asarray(tap).astype(jnp.int32)
        first = reach - tap // span
        second = reach - tap % span
        return accum + tap_window(padded, kernel, tap, first, second, tile_rows, tile_cols)

    accum = jnp.zeros((padded.shape[0], tile_rows, tile_cols), jnp.float32)
    return lax.fori_loop(0, span * span, backward_step, accum)


def kernel_grad(grad_mixed, padded, span, tile_rows, tile_cols):

    def kernel_step(tap, table):
        tap = jnp.asarray(tap).astype(jnp.int32)
        first = tap // span
        second = tap % span
        window = lax.dynamic_slice(
            padded, (jnp.int32(0), first, second), (padded.shape[0], tile_rows, tile_cols)
        )
        column = jnp.sum(grad_mixed * window, axis=(1, 2))
        return lax.dynamic_update_slice_in_dim(table, column[:, None], tap, 1)

    table = jnp.zeros((grad_mixed.shape[0], span * span), jnp.float32)
    return lax.fori_loop(0, span * span, kernel_step, table)


def body(
    image, depth_kernel, norm_gain, norm_shift, expand_weight, expand_bias, reduce_weight, cotangent
):
    channels, tile_rows, tile_cols = image.shape
    pixels = tile_rows * tile_cols
    all_channels = channels * lax.axis_size("ch")
    hid_local = reduce_weight.shape[0]
    half = KSIZE // 2
    padded = padded_2(image, (("row", 1), ("col", 2)), half).astype(jnp.float32)
    mixed = forward_taps(padded, depth_kernel, KSIZE, tile_rows, tile_cols)
    flat_cot = cotangent.reshape(channels, pixels)
    contract_first = (((0,), (0,)), ((), ()))
    contract_last = (((1,), (1,)), ((), ()))
    plain = (((1,), (0,)), ((), ()))
    centre = lax.psum(jnp.sum(mixed, axis=0), "ch") / all_channels
    diff = mixed - centre
    variance = lax.psum(jnp.sum(diff * diff, axis=0), "ch") / all_channels
    inverse = lax.rsqrt(variance + epsilon)
    normed = diff * inverse
    normal = (normed * norm_gain[:, None, None] + norm_shift[:, None, None]).astype(jnp.bfloat16)
    flat_normal = normal.reshape(channels, pixels)
    bias_local = lax.dynamic_slice_in_dim(expand_bias, lax.axis_index("ch") * hid_local, hid_local)
    full_normal = lax.all_gather(flat_normal, "ch", axis=0, tiled=True)
    hidden = product(expand_weight, full_normal, contract_first) + bias_local[:, None]
    value, slope = gelu_pair(hidden)
    active = value.astype(jnp.bfloat16)
    mlp_local = lax.psum_scatter(
        product(reduce_weight, active, contract_first), "ch", scatter_dimension=0, tiled=True
    )
    full_cot = lax.all_gather(flat_cot, "ch", axis=0, tiled=True)
    grad_act = product(reduce_weight, full_cot, plain)
    grad_hidden = (grad_act * slope).astype(jnp.bfloat16)
    grad_red = product(active, full_cot, contract_last)
    grad_exp = product(full_normal, grad_hidden, contract_last)
    grad_off = jnp.sum(grad_hidden.astype(jnp.float32), axis=1)
    grad_local = lax.psum_scatter(
        product(expand_weight, grad_hidden, plain).astype(jnp.bfloat16),
        "ch",
        scatter_dimension=0,
        tiled=True,
    ).astype(jnp.float32)
    grad_normal = grad_local.reshape(channels, tile_rows, tile_cols)
    grad_normed = grad_normal * norm_gain[:, None, None]
    plain_sum, cross_sum = lax.psum(
        (jnp.sum(grad_normed, axis=0), jnp.sum(grad_normed * normed, axis=0)), "ch"
    )
    grad_gain = jnp.sum(grad_normal * normed, axis=(1, 2))
    grad_shift = jnp.sum(grad_normal, axis=(1, 2))
    grad_mixed = inverse * (
        grad_normed - plain_sum / all_channels - normed * (cross_sum / all_channels)
    )
    result = (image.astype(jnp.float32) + mlp_local.reshape(channels, tile_rows, tile_cols)).astype(
        jnp.bfloat16
    )
    grad_pad = padded_2(grad_mixed.astype(jnp.bfloat16), (("row", 1), ("col", 2)), half).astype(
        grad_mixed.dtype
    )
    grad_image = (
        cotangent.astype(jnp.float32)
        + backward_taps(grad_pad, depth_kernel, KSIZE, tile_rows, tile_cols)
    ).astype(jnp.bfloat16)
    grad_kernel = kernel_grad(grad_mixed, padded, KSIZE, tile_rows, tile_cols)
    totals = lax.psum(
        (grad_kernel, grad_gain, grad_shift, grad_exp, grad_off, grad_red), ("row", "col")
    )
    pixels_all = pixels * lax.axis_size("row") * lax.axis_size("col")
    scale = float(pixels_all) ** (-0.5)
    return (
        result,
        grad_image,
        totals[0] * scale,
        totals[1] * scale,
        totals[2] * scale,
        totals[3] * scale,
        totals[4] * scale,
        totals[5] * scale,
    )


def solution(mesh):
    in_specs = (
        P("ch", "row", "col"),
        P("ch", None),
        P("ch"),
        P("ch"),
        P(None, "ch"),
        P(),
        P("ch", None),
        P("ch", "row", "col"),
    )
    out_specs = (
        P("ch", "row", "col"),
        P("ch", "row", "col"),
        P("ch", None),
        P("ch"),
        P("ch"),
        P(None, "ch"),
        P("ch"),
        P("ch", None),
    )
    return jax.shard_map(body, mesh=mesh, in_specs=in_specs, out_specs=out_specs, check_vma=False)
```

profile of v0, /device:TPU:1, one launch (start us, length us, event | category | flops | bytes accessed | tf_op | source)
XLA Modules:
  0.0 1113.7 jit_solution(2712978404241594079)
XLA Ops:
  8.1 1.0 fusion.13
  9.0 4.6 collective-permute-start
  13.6 5.5 collective-permute-start.1
  20.3 2.8 collective-permute-start.2
  23.1 1.3 collective-permute-start.3
  24.4 10.6 all_gather.7
  36.5 57.9 %while.48 = (s32[]{:T(128)}, f32[64,4,128]{2,1,0:T(4,128)S(1)}, f32[64,49]{0,1:T(8,128)}, f32[64,10,134]{2,1,0:T(8,128)S(1)}, s32[]{:T(128)}, /*index=5*/s32[]{:T(128)}, s32[]{:T(128)}, s32[]{:T(128)}, s32[]{:T(128)}, s32[]{:T(128)}) while((s32[]{:T(128)}, f32[64,4,128]{2,1,0:T(4,128)S(1)}, f32[64,49]{0,1:T(8,128)}, ...), condition=%wide.region_1.2_spmd.clone, body=%wide.region_0.1_spmd.clone.sunk | while | flops 98325 | bytes 394290 | solution.py:63
  94.4 7.8 psum.70
  102.4 6.0 psum.71
  109.3 10.1 all_gather.6
  119.6 1.1 fusion.8
  123.7 1.0 copy.25
  124.7 346.0 %all-reduce.5.cloned.1.call-done = (f32[256,256]{1,0:T(8,128)}, f32[256,256]{1,0:T(8,128)}) async-done(((f32[256,256]{1,0:T(8,128)}, f32[256,256]{1,0:T(8,128)}), (f32[256,256]{1,0:T(8,128)}, f32[256,256]{1,0:T(8,128)})) %all-reduce.5.cloned.1.call-update) | async-done | bytes 524304 | tf_op jit(solution)/shard_map/psum | solution.py:157
  470.8 1.9 broadcast_multiply_fusion
  472.6 1.0 copy.28
  474.4 8.4 all-reduce.2
  482.9 50.7 %while.47 = (s32[]{:T(128)}, f32[64,49]{0,1:T(8,128)S(1)}, f32[64,10,134]{2,1,0:T(8,128)S(1)}, f32[64,4,128]{2,1,0:T(4,128)S(1)}, s32[]{:T(128)}, /*index=5*/s32...) while((s32[]{:T(128)}, f32[64,49]{0,1:T(8,128)S(1)}, f32[64,10,134]{2,1,0:T(8,128)S(1)}, ...), condition=%wide.region_16.17_spmd, body=%wide.region_14.16_spmd.sunk | while | flops 65492 | bytes 263208 | solution.py:92
  483.0 0.9 multiply_reduce_fusion.6
  484.0 0.9 multiply_reduce_fusion.6
  485.1 0.9 multiply_reduce_fusion.6
  489.2 0.9 multiply_reduce_fusion.6
  490.2 0.9 multiply_reduce_fusion.6
  491.3 0.9 multiply_reduce_fusion.6
  496.5 0.9 multiply_reduce_fusion.6
  497.5 0.9 multiply_reduce_fusion.6
  502.7 0.9 multiply_reduce_fusion.6
  503.7 0.9 multiply_reduce_fusion.6
  504.7 0.9 multiply_reduce_fusion.6
  508.9 0.9 multiply_reduce_fusion.6
  509.9 0.9 multiply_reduce_fusion.6
  510.9 0.9 multiply_reduce_fusion.6
  516.1 0.9 multiply_reduce_fusion.6
  517.1 0.9 multiply_reduce_fusion.6
  522.3 0.9 multiply_reduce_fusion.6
  523.4 0.9 multiply_reduce_fusion.6
  524.4 0.9 multiply_reduce_fusion.6
  528.5 0.9 multiply_reduce_fusion.6
  529.6 0.9 multiply_reduce_fusion.6
  530.6 0.9 multiply_reduce_fusion.6
  533.7 477.5 %all-reduce = (f32[64,49]{0,1:T(8,128)S(1)}, f32[64]{0:T(128)S(1)}, f32[64]{0:T(128)S(1)}, f32[256]{0:T(256)S(1)}) all-reduce(f32[64,49]{0,1:T(8,128)S(1)} %get-tuple-element.351, f32[64]{0:T(128)S(1)} %get-tuple-element.382, f32[64]{0:T(128)S(1)} %get-tuple-element.384, ...), channel_id=1, replica_groups=mesh['row'=8,'col'=16,'ch'=4] {'row','col'}, use_global_device_ids=true, to_apply=%region_17.18 | all-reduce | flops 3520 | bytes 28160 | tf_op jit(solution)/shard_map/psum | solution.py:157
  1012.4 1.9 collective-permute-start.4
  1014.3 19.1 %collective-permute-start.5 = (bf16[64,3,128]{2,1,0:T(4,128)(2,1)S(1)}, bf16[64,3,128]{2,1,0:T(4,128)(2,1)S(1)}, u32[]{:S(2)}, u32[]{:S(2)}) collective-permute-start(bf16[64,3,128]{2,1,0:T(4,128)(2,1)S(1)} %get-tuple-element.425), channel_id=1, source_target_pairs={{64,0},{128,64},{192,128},{256,192},{320,256},{384,320},{448,384},... | collective-permute-start | bytes 147464 | tf_op jit(solution)/shard_map/ppermute | solution.py:22
  1034.6 1.3 collective-permute-start.6
  1035.9 1.3 collective-permute-start.7
  1037.7 3.5 collective-permute-done.6
  1041.2 3.8 collective-permute-done.7
  1045.8 57.9 %while.49 = (s32[]{:T(128)}, f32[64,4,128]{2,1,0:T(4,128)S(1)}, f32[64,49]{0,1:T(8,128)}, f32[64,10,134]{2,1,0:T(8,128)S(1)}, s32[]{:T(128)}, /*index=5*/s32[]{:...) while((s32[]{:T(128)}, f32[64,4,128]{2,1,0:T(4,128)S(1)}, ...), condition=%wide.region_13.14_spmd.clone, body=%wide.region_12.13_spmd.clone.sunk | while | flops 98327 | bytes 394322 | solution.py:76
  1104.4 1.0 copy.26
  (334 shorter events, 150.6 us)
Async XLA Ops:
  8.0 112.7 %copy-start = (bf16[256,256]{1,0:T(8,128)(2,1)S(1)}, bf16[256,256]{1,0:T(8,128)(2,1)}, u32[]{:S(2)}) copy-start(bf16[256,256]{1,0:T(8,128)(2,1)} %param.20) | copy-start | bytes 393220
  8.0 11.1 copy-start.3
  8.0 462.7 %all-reduce.5.cloned.1.call-start = ((), (), s32[]{:S(2)}) async-start(), calls=%async_computation.4 | async-start | bytes 1048576 | tf_op jit(solution)/shard_map/psum | solution.py:157
  9.0 10.1 collective-permute-start
  13.6 6.3 collective-permute-start.1
  19.1 0.9 copy-start.1
  20.3 15.5 %collective-permute-start.2 = (bf16[64,10,3]{2,1,0:T(8,128)(2,1)S(1)}, bf16[64,10,3]{2,1,0:T(8,128)(2,1)S(1)}, u32[]{:S(2)}, u32[]{:S(2)}) collective-permute-start(bf16[64,10,3]{2,1,0:T(8,128)(2,1)S(1)} %get-tuple-element.422), channel_id=1, source_target_pairs={{0,4},{4,8},{8,12},{12,16},{16,20},{20,24},{24,28},{28,32},{32,36}... | collective-permute-start | bytes 11528 | tf_op jit(solution)/shard_map/ppermute | solution.py:21
  23.1 12.7 %collective-permute-start.3 = (bf16[64,10,3]{2,1,0:T(8,128)(2,1)S(1)}, bf16[64,10,3]{2,1,0:T(8,128)(2,1)S(1)}, u32[]{:S(2)}, u32[]{:S(2)}) collective-permute-start(bf16[64,10,3]{2,1,0:T(8,128)(2,1)S(1)} %get-tuple-element.423), channel_id=1, source_target_pairs={{4,0},{8,4},{12,8},{16,12},{20,16},{24,20},{28,24},{32,28},{36,32}... | collective-permute-start | bytes 11528 | tf_op jit(solution)/shard_map/ppermute | solution.py:22
  108.4 0.7 copy-start.4
  108.4 0.7 copy-start.5
  109.3 10.1 copy-start.2
  122.1 350.5 %reduce-scatter.9.cloned.1.call-start = ((), (), s32[]{:S(2)}) async-start(), calls=%async_computation.3 | async-start | bytes 327680
  123.3 981.1 %reduce-scatter.7.cloned.1.call-start = ((), (), s32[]{:S(2)}) async-start(), calls=%async_computation.2 | async-start | bytes 655360
  1012.4 21.6 %collective-permute-start.4 = (bf16[64,3,128]{2,1,0:T(4,128)(2,1)S(1)}, bf16[64,3,128]{2,1,0:T(4,128)(2,1)S(1)}, u32[]{:S(2)}, u32[]{:S(2)}) collective-permute-start(bf16[64,3,128]{2,1,0:T(4,128)(2,1)S(1)} %get-tuple-element.424), channel_id=1, source_target_pairs={{0,64},{64,128},{128,192},{192,256},{256,320},{320,384},{384,448},... | collective-permute-start | bytes 147464 | tf_op jit(solution)/shard_map/ppermute | solution.py:21
  1014.3 20.0 %collective-permute-start.5 = (bf16[64,3,128]{2,1,0:T(4,128)(2,1)S(1)}, bf16[64,3,128]{2,1,0:T(4,128)(2,1)S(1)}, u32[]{:S(2)}, u32[]{:S(2)}) collective-permute-start(bf16[64,3,128]{2,1,0:T(4,128)(2,1)S(1)} %get-tuple-element.425), channel_id=1, source_target_pairs={{64,0},{128,64},{192,128},{256,192},{320,256},{384,320},{448,384},... | collective-permute-start | bytes 147464 | tf_op jit(solution)/shard_map/ppermute | solution.py:22
  1034.6 6.7 collective-permute-start.6
  1035.9 9.2 collective-permute-start.7
Sparse Core Ops, SparseCore 0:
  122.3 348.4 all-reduce.4
Sparse Core Ops, SparseCore 1:
  125.4 38.8 reduce-scatter.8
  167.0 28.9 reduce-scatter.6
where the time goes:
time: 1120 us; the launch traced here: 1110 us
  blocking collectives  520 us (46%)
  waiting for transfers between devices  355 us (32%)
  other arithmetic  97.2 us (9%)
  local copies, waits for them, and re-layouts  76.4 us (7%)
  starting transfers between devices  37.9 us (3%)
  between operations  15.7 us (1%)
    psum x1, blocking collectives, body(): lax.psum((grad_kernel, grad_gain, grad_shift, grad_exp, grad_off, grad_re...  477 us
    psum x1, waiting for transfers between devices, body(): lax.psum((grad_kernel, grad_gain, grad_shift, grad_exp, grad_off, grad_re...  346 us
    mul x98, local copies, waits for them, and re-layouts, tap_window(): return weight[:, :, None] * window  68.2 us
    reduce_sum x49, other arithmetic, kernel_step(): column = jnp.sum(grad_mixed * window, axis=(1, 2))  46.4 us
    ppermute x4, starting transfers between devices, padded_2(): after = lax.ppermute(leading, axis, down)  27.1 us
  transfers between devices with their start and end apart: 11, of which 5 were waited for; matrix products, arithmetic and copies ran while one was open for 10% of the time, Pallas kernels for 0%

commit v1 on v0

v1 whole, which is shorter than its diff:
```python
import functools
import jax
import jax.numpy as jnp
from jax import lax
from jax.experimental import pallas as pl
from jax.experimental.pallas import tpu as pltpu
from jax.sharding import PartitionSpec as P

KSIZE = 7
HALF = 3
SPAN = KSIZE + HALF
epsilon = 1e-06
root_two_pi = 0.7978845608028654
cubic_coef = 0.044715
f32 = jnp.float32
bf16 = jnp.bfloat16
LANES = 128
CT = 16


def lane_ids(rows):
    return lax.broadcasted_iota(jnp.int32, (rows, LANES), 1)


def rolled(x, shift):
    shift = shift % LANES
    return x if shift == 0 else pltpu.roll(x, shift, 1)


def split3(x):
    hi = x.astype(bf16)
    rest = x - hi.astype(f32)
    mid = rest.astype(bf16)
    low = (rest - mid.astype(f32)).astype(bf16)
    return [hi.astype(f32), mid.astype(f32), low.astype(f32)]


def gelu_pair(hidden):
    inner = root_two_pi * (hidden + cubic_coef * hidden * hidden * hidden)
    tangent = jnp.tanh(inner)
    value = 0.5 * hidden * (1.0 + tangent)
    slope = 0.5 * (1.0 + tangent) + 0.5 * hidden * (1.0 - tangent * tangent) * root_two_pi * (
        1.0 + 3.0 * cubic_coef * hidden * hidden
    )
    return (value, slope)


def halo_rows(up, mid, down, left, right, at):
    lane = lane_ids(CT)
    l = left[at, :].astype(f32)
    r = right[at, :].astype(f32)
    rows = []
    for i in range(SPAN):
        if i < HALF:
            x = up[i, at, :]
        elif i < SPAN - HALF:
            x = mid[i - HALF, at, :]
        else:
            x = down[i - (SPAN - HALF), at, :]
        edge = jnp.where(
            lane >= 64, rolled(l, LANES - HALF - HALF * i), rolled(r, LANES - HALF * i)
        )
        rows.append((x.astype(f32), edge))
    return rows


def window(row, s):
    x, edge = row
    if s == 0:
        return x
    lane = lane_ids(CT)
    mask = (lane < -s) if s < 0 else (lane >= LANES - s)
    return jnp.where(mask, rolled(edge, -s), rolled(x, -s))


def edges_kernel(up, mid, down, first, last):
    channels = mid.shape[1]
    lane = lane_ids(CT)

    def step(t, carry):
        at = pl.ds(pl.multiple_of(t * CT, CT), CT)
        head = jnp.zeros((CT, LANES), f32)
        tail = jnp.zeros((CT, LANES), f32)
        for i in range(SPAN):
            if i < HALF:
                x = up[i, at, :]
            elif i < SPAN - HALF:
                x = mid[i - HALF, at, :]
            else:
                x = down[i - (SPAN - HALF), at, :]
            x = x.astype(f32)
            mask = (lane >= HALF * i) & (lane < HALF * i + HALF)
            head = jnp.where(mask, rolled(x, HALF * i), head)
            tail = jnp.where(mask, rolled(x, HALF * i + HALF), tail)
        first[at, :] = head.astype(bf16)
        last[at, :] = tail.astype(bf16)
        return carry

    lax.fori_loop(0, channels // CT, step, 0)


def edges(up, mid, down):
    shape = jax.ShapeDtypeStruct((mid.shape[1], LANES), bf16)
    return pl.pallas_call(edges_kernel, out_shape=(shape, shape), name="edges")(up, mid, down)


def accumulate_taps(rows, kern, at, flip):
    accum = [jnp.zeros((CT, LANES), f32) for _ in range(SPAN - KSIZE + 1)]
    weights = kern[at, :]
    for b in range(KSIZE):
        shifted = [window(row, b - HALF) for row in rows]
        for a in range(KSIZE):
            tap = a * KSIZE + b
            if flip:
                tap = KSIZE * KSIZE - 1 - tap
            w = jnp.broadcast_to(weights[:, tap : tap + 1], (CT, LANES))
            for i in range(len(accum)):
                accum[i] = accum[i] + w * shifted[i + a]
    return accum


def forward_kernel(up, mid, down, left, right, kern, gain, shift, cot, mixed, payload):
    tile_rows, channels, _ = mid.shape

    def step(t, carry):
        at = pl.ds(pl.multiple_of(t * CT, CT), CT)
        rows = halo_rows(up, mid, down, left, right, at)
        accum = accumulate_taps(rows, kern, at, False)
        for i in range(tile_rows):
            mixed[at, i * LANES : (i + 1) * LANES] = accum[i]
        return carry

    lax.fori_loop(0, channels // CT, step, 0)
    pixels = tile_rows * LANES
    for i in range(tile_rows):
        cols = slice(i * LANES, (i + 1) * LANES)
        x = mixed[:, cols]
        mean = jnp.sum(x, axis=0, keepdims=True) / channels
        dev = x - mean
        spread = jnp.sum(dev * dev, axis=0, keepdims=True)
        rows = split3(mean) + split3(spread)
        stats = jnp.concatenate(rows + [jnp.zeros((CT - 6, LANES), f32)], axis=0)
        if i == 0:
            row_id = lax.broadcasted_iota(jnp.int32, (CT, LANES), 0)
            both = jnp.concatenate([gain[...], shift[...]], axis=1)
            for k, part in enumerate(split3(both)):
                stats = jnp.where(row_id == 6 + k, jnp.broadcast_to(part, (CT, LANES)), stats)
        dev = dev.astype(bf16)
        stats = stats.astype(bf16)
        for d in range(payload.shape[0]):
            payload[d, 0:channels, cols] = dev
            payload[d, channels : 2 * channels, cols] = cot[i]
            payload[d, 2 * channels : 2 * channels + CT, cols] = stats


def forward(up, mid, down, left, right, kern, gain, shift, cot, parts):
    tile_rows, channels, _ = mid.shape
    pixels = tile_rows * LANES
    return pl.pallas_call(
        forward_kernel,
        out_shape=(
            jax.ShapeDtypeStruct((channels, pixels), f32),
            jax.ShapeDtypeStruct((parts, 2 * channels + CT, pixels), bf16),
        ),
        name="forward",
    )(up, mid, down, left, right, kern, gain, shift, cot)


def column(row, n):
    i = lax.broadcasted_iota(jnp.int32, (n, n), 0)
    j = lax.broadcasted_iota(jnp.int32, (n, n), 1)
    return jnp.sum(jnp.where(i == j, jnp.broadcast_to(row, (n, n)), 0.0), axis=1, keepdims=True)


def row_of(col, n):
    i = lax.broadcasted_iota(jnp.int32, (n, n), 0)
    j = lax.broadcasted_iota(jnp.int32, (n, n), 1)
    return jnp.sum(jnp.where(i == j, jnp.broadcast_to(col, (n, n)), 0.0), axis=0, keepdims=True)


def dot(a, b, dims):
    return lax.dot_general(a, b, (dims, ((), ())), preferred_element_type=f32)


def mlp_kernel(recv, w_exp, bias, w_red, payload, stats_out, grads, off, s_norm, s_act, s_cot, s_gh):
    parts, height, pixels = recv.shape
    ch = (height - CT) // 2
    total = parts * ch
    width = 2 * LANES
    gains, shifts = [], []
    for k in range(parts):
        head = recv[k, 2 * ch : 2 * ch + CT, 0:LANES].astype(f32)
        both = head[6:7] + head[7:8] + head[8:9]
        gains.append(column(both[:, 0:ch], ch))
        shifts.append(column(both[:, ch : 2 * ch], ch))
    bias_col = column(bias[...], bias.shape[1])
    for blk in range(pixels // width):
        cols = slice(blk * width, (blk + 1) * width)
        means, spreads = [], []
        for k in range(parts):
            st = recv[k, 2 * ch : 2 * ch + CT, cols].astype(f32)
            means.append(st[0:1] + st[1:2] + st[2:3])
            spreads.append(st[3:4] + st[4:5] + st[5:6])
        centre = sum(means) / parts
        spread = sum(spreads)
        for k in range(parts):
            gap = means[k] - centre
            spread = spread + ch * gap * gap
        inverse = lax.rsqrt(spread / total + epsilon)
        stats_out[0:1, cols] = centre
        stats_out[1:2, cols] = inverse
        for k in range(parts):
            at = slice(k * ch, (k + 1) * ch)
            dev = recv[k, 0:ch, cols].astype(f32)
            normed = (dev + (means[k] - centre)) * inverse
            s_norm[at, cols] = (normed * gains[k] + shifts[k]).astype(bf16)
            s_cot[at, cols] = recv[k, ch : 2 * ch, cols]
        hidden = dot(w_exp[...], s_norm[:, cols], ((0,), (0,))) + bias_col
        value, slope = gelu_pair(hidden)
        active = value.astype(bf16)
        s_act[:, cols] = active
        gh = (dot(w_red[...], s_cot[:, cols], ((1,), (0,))) * slope).astype(bf16)
        s_gh[:, cols] = gh
        mlp = dot(w_red[...], active, ((0,), (0,)))
        part = dot(w_exp[...], gh, ((1,), (0,)))
        plain = jnp.zeros((1, width), f32)
        cross = jnp.zeros((1, width), f32)
        for k in range(parts):
            at = slice(k * ch, (k + 1) * ch)
            dev = recv[k, 0:ch, cols].astype(f32)
            normed = (dev + (means[k] - centre)) * inverse
            scaled = part[at] * gains[k]
            plain = plain + jnp.sum(scaled, axis=0, keepdims=True)
            cross = cross + jnp.sum(scaled * normed, axis=0, keepdims=True)
            payload[k, 0:ch, cols] = mlp[at].astype(bf16)
            payload[k, ch : 2 * ch, cols] = part[at].astype(bf16)
        sums = jnp.concatenate(
            split3(plain) + split3(cross) + [jnp.zeros((CT - 6, width), f32)], axis=0
        ).astype(bf16)
        for k in range(parts):
            payload[k, 2 * ch : 2 * ch + CT, cols] = sums
    last = ((1,), (1,))
    grad_exp = dot(s_norm[...], s_gh[...], last)
    grad_red = dot(s_act[...], s_cot[...], last)
    n = grad_exp.shape[0]
    grads[0:n, :] = grad_exp[:, 0:LANES]
    grads[n : 2 * n, :] = grad_exp[:, LANES:]
    grads[2 * n : 3 * n, :] = grad_red[:, 0:LANES]
    grads[3 * n : 4 * n, :] = grad_red[:, LANES:]
    off[...] = dot(jnp.ones((8, pixels), bf16), s_gh[...], last)


def mlp(recv, w_exp, bias, w_red):
    parts, height, pixels = recv.shape
    hid = w_red.shape[0]
    total = w_exp.shape[0]
    return pl.pallas_call(
        mlp_kernel,
        out_shape=(
            jax.ShapeDtypeStruct(recv.shape, bf16),
            jax.ShapeDtypeStruct((2, pixels), f32),
            jax.ShapeDtypeStruct((4 * total, LANES), f32),
            jax.ShapeDtypeStruct((8, hid), f32),
        ),
        scratch_shapes=[
            pltpu.VMEM((total, pixels), bf16),
            pltpu.VMEM((hid, pixels), bf16),
            pltpu.VMEM((total, pixels), bf16),
            pltpu.VMEM((hid, pixels), bf16),
        ],
        name="mlp",
    )(recv, w_exp, bias, w_red)


def norm_back_kernel(recv, mixed, stats, gain, image, result, grad_mixed, rounded, small):
    parts, height, pixels = recv.shape
    ch = (height - CT) // 2
    tile_rows = image.shape[0]
    total = parts * ch
    gain_col = column(gain[...], ch)
    acc_gain = jnp.zeros((ch, LANES), f32)
    acc_shift = jnp.zeros((ch, LANES), f32)
    for i in range(tile_rows):
        cols = slice(i * LANES, (i + 1) * LANES)
        mlp_out = jnp.zeros((ch, LANES), f32)
        grad = jnp.zeros((ch, LANES), f32)
        sums = jnp.zeros((CT, LANES), f32)
        for k in range(parts):
            mlp_out = mlp_out + recv[k, 0:ch, cols].astype(f32)
            grad = grad + recv[k, ch : 2 * ch, cols].astype(f32)
            sums = sums + recv[k, 2 * ch : 2 * ch + CT, cols].astype(f32)
        result[i] = (image[i].astype(f32) + mlp_out).astype(bf16)
        plain = (sums[0:1] + sums[1:2] + sums[2:3]) / total
        cross = (sums[3:4] + sums[4:5] + sums[5:6]) / total
        inverse = stats[1:2, cols]
        normed = (mixed[:, cols] - stats[0:1, cols]) * inverse
        acc_gain = acc_gain + grad * normed
        acc_shift = acc_shift + grad
        out = inverse * (grad * gain_col - plain - normed * cross)
        grad_mixed[i] = out
        rounded[i] = out.astype(bf16)
    g = row_of(jnp.sum(acc_gain, axis=1, keepdims=True), ch)
    s = row_of(jnp.sum(acc_shift, axis=1, keepdims=True), ch)
    small[...] = jnp.broadcast_to(jnp.concatenate([g, s], axis=1), (8, LANES))


def norm_back(recv, mixed, stats, gain, image):
    tile_rows, channels, _ = image.shape
    return pl.pallas_call(
        norm_back_kernel,
        out_shape=(
            jax.ShapeDtypeStruct(image.shape, bf16),
            jax.ShapeDtypeStruct(image.shape, f32),
            jax.ShapeDtypeStruct(image.shape, bf16),
            jax.ShapeDtypeStruct((8, LANES), f32),
        ),
        name="norm_back",
    )(recv, mixed, stats, gain, image)


def tap_grad_kernel(up, mid, down, left, right, grad_mixed, small, off, out):
    tile_rows, channels, _ = mid.shape
    lane = lane_ids(CT)

    def step(t, carry):
        at = pl.ds(pl.multiple_of(t * CT, CT), CT)
        rows = halo_rows(up, mid, down, left, right, at)
        grads = [grad_mixed[i, at, :] for i in range(tile_rows)]
        table = jnp.zeros((CT, LANES), f32)
        for b in range(KSIZE):
            shifted = [window(row, b - HALF) for row in rows]
            for a in range(KSIZE):
                accum = grads[0] * shifted[a]
                for i in range(1, tile_rows):
                    accum = accum + grads[i] * shifted[a + i]
                value = jnp.sum(accum, axis=1, keepdims=True)
                table = jnp.where(lane == a * KSIZE + b, value, table)
        out[at, :] = table
        return carry

    lax.fori_loop(0, channels // CT, step, 0)
    hid = off.shape[1]
    out[channels : channels + 8, :] = small[...]
    for j in range(hid // LANES):
        out[channels + 8 * (j + 1) : channels + 8 * (j + 2), :] = off[:, j * LANES : (j + 1) * LANES]
    used = channels + 8 * (1 + hid // LANES)
    out[used:, :] = jnp.zeros((out.shape[0] - used, LANES), f32)


def tap_grad(up, mid, down, left, right, grad_mixed, small, off):
    return pl.pallas_call(
        tap_grad_kernel,
        out_shape=jax.ShapeDtypeStruct((LANES, LANES), f32),
        name="tap_grad",
    )(up, mid, down, left, right, grad_mixed, small, off)


def backward_kernel(up, mid, down, left, right, kern, cot, out):
    tile_rows, channels, _ = mid.shape

    def step(t, carry):
        at = pl.ds(pl.multiple_of(t * CT, CT), CT)
        rows = halo_rows(up, mid, down, left, right, at)
        accum = accumulate_taps(rows, kern, at, True)
        for i in range(tile_rows):
            out[i, at, :] = (cot[i, at, :].astype(f32) + accum[i]).astype(bf16)
        return carry

    lax.fori_loop(0, channels // CT, step, 0)


def backward(up, mid, down, left, right, kern, cot):
    return pl.pallas_call(
        backward_kernel,
        out_shape=jax.ShapeDtypeStruct(cot.shape, bf16),
        name="backward",
    )(up, mid, down, left, right, kern, cot)


def final_kernel(scale, flat, exp_ref, red_ref, taps_ref, vec_ref):
    n = exp_ref.shape[0]
    exp_ref[:, 0:LANES] = flat[0:n, :] * scale
    exp_ref[:, LANES:] = flat[n : 2 * n, :] * scale
    red_ref[:, 0:LANES] = flat[2 * n : 3 * n, :] * scale
    red_ref[:, LANES:] = flat[3 * n : 4 * n, :] * scale
    base = 4 * n
    channels = taps_ref.shape[0]
    taps_ref[...] = flat[base : base + channels, 0 : taps_ref.shape[1]] * scale
    vec_ref[...] = flat[base + channels : base + channels + vec_ref.shape[0], :] * scale


def final(flat, scale, total, hid, channels, taps):
    return pl.pallas_call(
        functools.partial(final_kernel, scale),
        out_shape=(
            jax.ShapeDtypeStruct((total, hid), f32),
            jax.ShapeDtypeStruct((hid, total), f32),
            jax.ShapeDtypeStruct((channels, taps), f32),
            jax.ShapeDtypeStruct((8 * (1 + hid // LANES), LANES), f32),
        ),
        name="final",
    )(flat)


def neighbours(first, last, axis):
    size = lax.axis_size(axis)
    up = [(i, i + 1) for i in range(size - 1)]
    down = [(j, i) for i, j in up]
    return lax.ppermute(last, axis, up), lax.ppermute(first, axis, down)


def halo(x):
    rows = x.shape[0]
    up, down = neighbours(x[:HALF], x[rows - HALF :], "row")
    first, last = edges(up, x, down)
    left, right = neighbours(first, last, "col")
    return up, down, left, right


def reduce_all(flat):
    rows, cols = lax.axis_size("row"), lax.axis_size("col")
    height = flat.shape[0]
    part = lax.all_to_all(flat.reshape(rows, height // rows, LANES), "row", 0, 0).sum(0)
    part = part.reshape(cols, height // rows // cols, LANES)
    part = lax.all_to_all(part, "col", 0, 0).sum(0)
    part = jnp.broadcast_to(part[None], (cols,) + part.shape)
    part = lax.all_to_all(part, "col", 0, 0).reshape(height // rows, LANES)
    return lax.all_gather(part, "row", axis=0, tiled=True)


def body(
    image, depth_kernel, norm_gain, norm_shift, expand_weight, expand_bias, reduce_weight, cotangent
):
    channels, tile_rows, tile_cols = image.shape
    pixels = tile_rows * tile_cols
    parts = lax.axis_size("ch")
    hid = reduce_weight.shape[0]
    total = expand_weight.shape[0]
    img = jnp.transpose(image, (1, 0, 2))
    cot = jnp.transpose(cotangent, (1, 0, 2))
    gain = norm_gain.reshape(1, channels)
    shift = norm_shift.reshape(1, channels)
    bias = lax.dynamic_slice_in_dim(expand_bias, lax.axis_index("ch") * hid, hid).reshape(1, hid)
    up, down, left, right = halo(img)
    mixed, send = forward(up, img, down, left, right, depth_kernel, gain, shift, cot, parts)
    recv = lax.all_to_all(send, "ch", 0, 0)
    send, stats, grads, off = mlp(recv, expand_weight, bias, reduce_weight)
    recv = lax.all_to_all(send, "ch", 0, 0)
    result, grad_mixed, rounded, small = norm_back(recv, mixed, stats, gain, img)
    g_up, g_down, g_left, g_right = halo(rounded)
    taps = tap_grad(up, img, down, left, right, grad_mixed, small, off)
    grad_image = backward(g_up, rounded, g_down, g_left, g_right, depth_kernel, cot)
    flat = reduce_all(jnp.concatenate([grads, taps], axis=0))
    pixels_all = pixels * lax.axis_size("row") * lax.axis_size("col")
    scale = float(pixels_all) ** (-0.5)
    grad_exp, grad_red, grad_taps, vec = final(
        flat, scale, total, hid, channels, depth_kernel.shape[1]
    )
    return (
        jnp.transpose(result, (1, 0, 2)),
        jnp.transpose(grad_image, (1, 0, 2)),
        grad_taps,
        vec[0, :channels],
        vec[0, channels:],
        grad_exp,
        vec[8::8].reshape(hid),
        grad_red,
    )


def solution(mesh):
    in_specs = (
        P("ch", "row", "col"),
        P("ch", None),
        P("ch"),
        P("ch"),
        P(None, "ch"),
        P(),
        P("ch", None),
        P("ch", "row", "col"),
    )
    out_specs = (
        P("ch", "row", "col"),
        P("ch", "row", "col"),
        P("ch", None),
        P("ch"),
        P("ch"),
        P(None, "ch"),
        P("ch"),
        P("ch", None),
    )
    return jax.shard_map(body, mesh=mesh, in_specs=in_specs, out_specs=out_specs, check_vma=False)
```

time: 1120 us -> 159 us (0.14)
  blocking collectives: 520 us -> 71 us
  waiting for transfers between devices: 355 us -> 14.4 us
  other arithmetic: 97.2 us -> 0.93 us
  local copies, waits for them, and re-layouts: 76.4 us -> 14.4 us
  Pallas kernels: 0 us -> 22.2 us
  between operations: 15.7 us -> 0.86 us
    psum x4 -> x0, blocking collectives: 500 us -> none  [the longest x1 477 us: body(): lax.psum((grad_kernel, grad_gain, grad_shift, grad_exp, grad_off, grad_re...]
    psum x1 -> x0, waiting for transfers between devices: 346 us -> none  [body(): lax.psum((grad_kernel, grad_gain, grad_shift, grad_exp, grad_off, grad_re...]
    mul x98 -> x0, local copies, waits for them, and re-layouts: 68.2 us -> none  [tap_window(): return weight[:, :, None] * window]
    all_to_all x0 -> x3, blocking collectives: none -> 55 us  [the longest x1 26.5 us: reduce_all(): part = lax.all_to_all(part, 'col', 0, 0).sum(0)]
    reduce_sum x53 -> x2, other arithmetic: 47.3 us -> 0.05 us  [the longest x1 0.03 us: reduce_all(): lax.all_to_all(flat.reshape(rows, height // rows, LANES), 'row', 0, 0)]
    add x98 -> x0, other arithmetic: 42.4 us -> none  [the longest x49 21.2 us: forward_step(): accum + tap_window(padded, kernel, tap, first, second, tile_rows, tile_cols)]
    pallas_call x0 -> x8, Pallas kernels: none -> 22.2 us  [the longest x1 4.3 us: tap_grad(): pl.pallas_call(tap_grad_kernel, out_shape=jax.ShapeDtypeStruct((LANES, LA...]
    ppermute x8, starting transfers between devices: 37.7 us -> 23.7 us  [neighbours(): return (lax.ppermute(last, axis, up), lax.ppermute(first, axis, down))]
  transfers between devices with their start and end apart: 11 -> 10, of which waited for: 5 -> 5; matrix products, arithmetic and copies ran while one was open for 10% -> 3% of each run, Pallas kernels for 0% -> 3%
where the time goes in v1:
time: 159 us; the launch traced here: 157 us
  blocking collectives  71 us (45%)
  starting transfers between devices  33.3 us (21%)
  Pallas kernels  22.2 us (14%)
  local copies, waits for them, and re-layouts  14.4 us (9%)
  waiting for transfers between devices  14.4 us (9%)
    all_to_all x1, blocking collectives, reduce_all(): part = lax.all_to_all(part, 'col', 0, 0).sum(0)  26.5 us
    ppermute x8, starting transfers between devices, neighbours(): return (lax.ppermute(last, axis, up), lax.ppermute(first, axis, down))  23.7 us
    all_to_all x1, blocking collectives, reduce_all(): lax.all_to_all(flat.reshape(rows, height // rows, LANES), 'row', 0, 0)  16.7 us
    all_gather x1, blocking collectives, reduce_all(): return lax.all_gather(part, 'row', axis=0, tiled=True)  16 us
    all_to_all x1, blocking collectives, body(): recv = lax.all_to_all(send, 'ch', 0, 0)  11.7 us
    unnamed x36, local copies, waits for them, and re-layouts  9.74 us
    all_to_all x1, waiting for transfers between devices, body(): recv = lax.all_to_all(send, 'ch', 0, 0)  7.31 us
    ppermute x8, waiting for transfers between devices, neighbours(): return (lax.ppermute(last, axis, up), lax.ppermute(first, axis, down))  7.07 us
  transfers between devices with their start and end apart: 10, of which 5 were waited for; matrix products, arithmetic and copies ran while one was open for 3% of the time, Pallas kernels for 3%

profile of v1, /device:TPU:1, one launch (start us, length us, event | category | flops | bytes accessed | tf_op | source)
XLA Modules:
  0.0 157.1 jit_solution(545057637172232730)
XLA Ops:
  0.6 0.9 copy.33
  1.5 0.0 copy-start
  1.5 0.6 copy-done
  2.1 8.7 %collective-permute-start.1 = (bf16[3,64,128]{2,1,0:T(8,128)(2,1)S(1)}, bf16[3,64,128]{2,1,0:T(8,128)(2,1)S(1)}, u32[]{:S(2)}, u32[]{:S(2)}) collective-permute-start(bf16[3,64,128]{2,1,0:T(8,128)(2,1)S(1)} %get-tuple-element.62), channel_id=1, source_target_pairs={{64,0},{128,64},{192,128},{256,192},{320,256},{384,320},{448,384},... | collective-permute-start | bytes 147464 | tf_op jit(solution)/shard_map/ppermute | solution.py:409
  10.9 0.0 copy-start.12
  10.9 1.9 %collective-permute-start = (bf16[3,64,128]{2,1,0:T(8,128)(2,1)S(1)}, bf16[3,64,128]{2,1,0:T(8,128)(2,1)S(1)}, u32[]{:S(2)}, u32[]{:S(2)}) collective-permute-start(bf16[3,64,128]{2,1,0:T(8,128)(2,1)S(1)} %get-tuple-element.63), channel_id=1, source_target_pairs={{0,64},{64,128},{128,192},{192,256},{256,320},{320,384},{384,448},... | collective-permute-start | bytes 147464 | tf_op jit(solution)/shard_map/ppermute | solution.py:409
  12.8 0.0 collective-permute-done.1.down
  12.8 1.2 collective-permute-done.up
  14.0 0.6 copy-done.5
  14.6 1.9 %edges.2 = (bf16[64,128]{1,0:T(8,128)(2,1)}, bf16[64,128]{1,0:T(8,128)(2,1)}) custom-call(bf16[3,64,128]{2,1,0:T(8,128)(2,1)} %copy-done.5, bf16[4,64,128]{2,1,0:T(8,128)(2,1)} %bitcast.18, bf16[3,64,128]{2,1,0:T(8,128)(2,1)} %copy-done.4), custom_call_target="tpu_custom_call" | custom-call | tf_op jit(solution)/shard_map/edges/pallas_call | solution.py:104
  16.5 1.3 collective-permute-start.2
  17.8 1.3 collective-permute-start.3
  19.1 0.7 copy.25.kern
  19.8 0.6 copy.32
  20.4 2.1 %collective-permute-done.3.right = bf16[64,128]{1,0:T(8,128)(2,1)S(1)} collective-permute-done((bf16[64,128]{1,0:T(8,128)(2,1)}, bf16[64,128]{1,0:T(8,128)(2,1)S(1)}, u32[]{:S(2)}, u32[]{:S(2)}) %collective-permute-start.3) | collective-permute-done | bytes 16416 | tf_op jit(solution)/shard_map/ppermute | solution.py:409
  22.5 0.6 copy-done.9
  23.1 3.6 %forward.1 = (f32[64,512]{1,0:T(8,128)}, bf16[4,144,512]{2,1,0:T(8,128)(2,1)}) custom-call(bf16[3,64,128]{2,1,0:T(8,128)(2,1)} %copy-done.5, bf16[4,64,128]{2,1,0:T(8,128)(2,1)} %bitcast.19, bf16[3,64,128]{2,1,0:T(8,128)(2,1)} %copy-done.4, bf16[64,128]{1,0:T(8,128)(2,1)} %copy-done.8, bf16[64,128]{1,0:T(8,128)(2,1)} %copy-done.9, f32[64,49]{1,0:T(8,128)} %copy.25.kern, ...), custom_call_target="tpu_custom_call" | custom-call | tf_op jit(solution)/shard_map/forward/pallas_call | solution.py:159
  26.7 3.5 %all-to-all-start = ((bf16[4,144,512]{2,1,0:T(8,128)(2,1)}), bf16[4,144,512]{2,1,0:T(8,128)(2,1)S(1)}, u32[]{:S(2)}, u32[]{:S(2)}) async-start(bf16[4,144,512]{2,1,0:T(8,128)(2,1)} %get-tuple-element.28), calls=%async_computation | async-start | bytes 1179648 | tf_op jit(solution)/shard_map/all_to_all | solution.py:446
  30.2 1.3 dynamic_slice.3
  31.5 7.3 %all-to-all-done.recv = bf16[4,144,512]{2,1,0:T(8,128)(2,1)S(1)} async-done(((bf16[4,144,512]{2,1,0:T(8,128)(2,1)}), bf16[4,144,512]{2,1,0:T(8,128)(2,1)S(1)}, u32[]{:S(2)}, u32[]{:S(2)}) %all-to-all-start) | async-done | bytes 589856 | tf_op jit(solution)/shard_map/all_to_all | solution.py:446
  38.8 0.8 copy-done.1
  39.6 3.3 %mlp.1 = (bf16[4,144,512]{2,1,0:T(8,128)(2,1)}, f32[2,512]{1,0:T(2,128)}, f32[1024,128]{1,0:T(8,128)}, f32[8,256]{1,0:T(8,128)}) custom-call(bf16[4,144,512]{2,1,0:T(8,128)(2,1)} %copy-done.1, bf16[256,256]{1,0:T(8,128)(2,1)} %w_exp.1, f32[1,256]{1,0:T(1,128)} %bitcast.27, bf16[256,256]{1,0:T(8,128)(2,1)} %w_red.1), custom_call_target="tpu_custom_call" | custom-call | tf_op jit(solution)/shard_map/mlp/pallas_call | solution.py:257
  43.0 11.7 %all_to_all.25.recv = bf16[4,144,512]{2,1,0:T(8,128)(2,1)} all-to-all(bf16[4,144,512]{2,1,0:T(8,128)(2,1)} %get-tuple-element.29), channel_id=1, replica_groups=mesh['row'=8,'col'=16,'ch'=4] {'ch'}, dimensions={0} | all-to-all | bytes 1179648 | tf_op jit(solution)/shard_map/all_to_all | solution.py:448
  54.7 2.1 %norm_back.1 = (bf16[4,64,128]{2,1,0:T(8,128)(2,1)}, f32[4,64,128]{2,1,0:T(8,128)}, bf16[4,64,128]{2,1,0:T(8,128)(2,1)}, f32[8,128]{1,0:T(8,128)}) custom-call(bf16[4,144,512]{2,1,0:T(8,128)(2,1)} %all_to_all.25.recv, f32[64,512]{1,0:T(8,128)} %get-tuple-element.30.mixed, f32[2,512]{1,0:T(2,128)} %get-tuple-element.31.stats, f32[1,64]{1,0:T(1,128)} %bitcast.29, ...), custom_call_target="tpu_custom_call" | custom-call | tf_op jit(solution)/shard_map/norm_back/pallas_call | solution.py:309
  56.8 4.3 %tap_grad.1 = f32[128,128]{1,0:T(8,128)} custom-call(bf16[3,64,128]{2,1,0:T(8,128)(2,1)} %copy-done.5, bf16[4,64,128]{2,1,0:T(8,128)(2,1)} %bitcast.21, bf16[3,64,128]{2,1,0:T(8,128)(2,1)} %copy-done.4, bf16[64,128]{1,0:T(8,128)(2,1)} %copy-done.8, bf16[64,128]{1,0:T(8,128)(2,1)} %copy-done.9, f32[4,64,128]{2,1,0:T(8,128)} %get-tuple-element.37.grad_mixed, ...), custom_call_target="tpu_custom_call" | custom-call | tf_op jit(solution)/shard_map/tap_grad/pallas_call | solution.py:351
  61.1 0.9 pad_maximum_fusion
  61.9 16.7 %all_to_all.26 = f32[8,144,128]{2,1,0:T(8,128)S(1)} all-to-all(f32[8,144,128]{2,1,0:T(8,128)S(1)} %bitcast.22), channel_id=1, replica_groups=mesh['row'=8,'col'=16,'ch'=4] {'row'}, dimensions={0} | all-to-all | bytes 1179648 | tf_op jit(solution)/shard_map/all_to_all | solution.py:423
  78.7 26.5 %all_to_all.27 = f32[16,9,128]{2,1,0:T(8,128)S(1)} all-to-all(f32[16,9,128]{2,1,0:T(8,128)S(1)} %reshape.42), channel_id=1, replica_groups=mesh['row'=8,'col'=16,'ch'=4] {'col'}, dimensions={0} | all-to-all | bytes 147456 | tf_op jit(solution)/shard_map/all_to_all | solution.py:425
  105.3 0.7 broadcast_in_dim.2
  106.0 6.1 %all-to-all-start.4 = ((f32[16,9,128]{2,1,0:T(8,128)}), f32[16,9,128]{2,1,0:T(8,128)S(1)}, u32[]{:S(2)}, u32[]{:S(2)}) async-start(f32[16,9,128]{2,1,0:T(8,128)} %broadcast_in_dim.2), calls=%async_computation.4 | async-start | bytes 262144 | tf_op jit(solution)/shard_map/all_to_all | solution.py:427
  112.1 3.4 %collective-permute-start.5 = (bf16[3,64,128]{2,1,0:T(8,128)(2,1)S(1)}, bf16[3,64,128]{2,1,0:T(8,128)(2,1)S(1)}, u32[]{:S(2)}, u32[]{:S(2)}) collective-permute-start(bf16[3,64,128]{2,1,0:T(8,128)(2,1)S(1)} %get-tuple-element.60), channel_id=1, source_target_pairs={{64,0},{128,64},{192,128},{256,192},{320,256},{384,320},{448,384},... | collective-permute-start | bytes 147464 | tf_op jit(solution)/shard_map/ppermute | solution.py:409
  115.6 0.0 copy-start.11
  115.6 2.3 %collective-permute-start.4 = (bf16[3,64,128]{2,1,0:T(8,128)(2,1)S(1)}, bf16[3,64,128]{2,1,0:T(8,128)(2,1)S(1)}, u32[]{:S(2)}, u32[]{:S(2)}) collective-permute-start(bf16[3,64,128]{2,1,0:T(8,128)(2,1)S(1)} %get-tuple-element.61), channel_id=1, source_target_pairs={{0,64},{64,128},{128,192},{192,256},{256,320},{320,384},{384,448},... | collective-permute-start | bytes 147464 | tf_op jit(solution)/shard_map/ppermute | solution.py:409
  117.9 1.1 collective-permute-done.4.up
  119.0 0.6 copy-done.7
  119.6 1.8 %edges.3 = (bf16[64,128]{1,0:T(8,128)(2,1)}, bf16[64,128]{1,0:T(8,128)(2,1)}) custom-call(bf16[3,64,128]{2,1,0:T(8,128)(2,1)} %copy-done.7, bf16[4,64,128]{2,1,0:T(8,128)(2,1)} %get-tuple-element.33.mid, bf16[3,64,128]{2,1,0:T(8,128)(2,1)} %copy-done.6), custom_call_target="tpu_custom_call" | custom-call | tf_op jit(solution)/shard_map/edges/pallas_call | solution.py:104
  121.5 3.5 %collective-permute-start.6 = (bf16[64,128]{1,0:T(8,128)(2,1)}, bf16[64,128]{1,0:T(8,128)(2,1)S(1)}, u32[]{:S(2)}, u32[]{:S(2)}) collective-permute-start(bf16[64,128]{1,0:T(8,128)(2,1)} %get-tuple-element.34), channel_id=1, source_target_pairs={{0,4},{4,8},{8,12},{12,16},{16,20},{20,24},{24,28},{28,32},{32,36}... | collective-permute-start | bytes 49160 | tf_op jit(solution)/shard_map/ppermute | solution.py:409
  125.0 1.3 collective-permute-start.7
  126.3 0.7 copy.27
  127.0 2.7 %collective-permute-done.7.right = bf16[64,128]{1,0:T(8,128)(2,1)S(1)} collective-permute-done((bf16[64,128]{1,0:T(8,128)(2,1)}, bf16[64,128]{1,0:T(8,128)(2,1)S(1)}, u32[]{:S(2)}, u32[]{:S(2)}) %collective-permute-start.7) | collective-permute-done | bytes 16416 | tf_op jit(solution)/shard_map/ppermute | solution.py:409
  129.7 0.6 copy-done.14
  130.3 3.3 %backward.1 = bf16[4,64,128]{2,1,0:T(8,128)(2,1)} custom-call(bf16[3,64,128]{2,1,0:T(8,128)(2,1)} %copy-done.7, bf16[4,64,128]{2,1,0:T(8,128)(2,1)} %get-tuple-element.33.mid, bf16[3,64,128]{2,1,0:T(8,128)(2,1)} %copy-done.6, bf16[64,128]{1,0:T(8,128)(2,1)} %copy-done.13, bf16[64,128]{1,0:T(8,128)(2,1)} %copy-done.14, f32[64,49]{1,0:T(8,128)} %copy.25.kern, ...), custom_call_target="tpu_custom_call" | custom-call | tf_op jit(solution)/shard_map/backward/pallas_call | solution.py:373
  133.5 1.5 copy.28
  135.1 16.0 %all_gather.3.flat = f32[1152,128]{1,0:T(8,128)} all-gather(f32[144,128]{1,0:T(8,128)S(1)} %reshape.43), channel_id=1, replica_groups=mesh['row'=8,'col'=16,'ch'=4] {'row'}, dimensions={0}, use_global_device_ids=true | all-gather | bytes 663552 | tf_op jit(solution)/shard_map/all_gather | solution.py:428
  151.1 1.9 %final.1 = (f32[256,256]{1,0:T(8,128)}, f32[256,256]{1,0:T(8,128)}, f32[64,49]{1,0:T(8,128)}, f32[24,128]{1,0:T(8,128)}) custom-call(f32[1152,128]{1,0:T(8,128)} %all_gather.3.flat), custom_call_target="tpu_custom_call" | custom-call | tf_op jit(solution)/shard_map/final/pallas_call | solution.py:393
  153.0 1.3 slice.27
  154.3 1.3 slice_bitcast_fusion
  155.6 1.5 copy.29
  (31 shorter events, 0.2 us)
Async XLA Ops:
  1.5 0.6 copy-start
  2.1 10.7 %collective-permute-start.1 = (bf16[3,64,128]{2,1,0:T(8,128)(2,1)S(1)}, bf16[3,64,128]{2,1,0:T(8,128)(2,1)S(1)}, u32[]{:S(2)}, u32[]{:S(2)}) collective-permute-start(bf16[3,64,128]{2,1,0:T(8,128)(2,1)S(1)} %get-tuple-element.62), channel_id=1, source_target_pairs={{64,0},{128,64},{192,128},{256,192},{320,256},{384,320},{448,384},... | collective-permute-start | bytes 147464 | tf_op jit(solution)/shard_map/ppermute | solution.py:409
  10.9 8.2 %copy-start.12 = (f32[64,49]{0,1:T(8,128)S(1)}, f32[64,49]{0,1:T(8,128)}, u32[]{:S(2)}) copy-start(f32[64,49]{0,1:T(8,128)} %param.9) | copy-start | bytes 37636
  10.9 3.1 %collective-permute-start = (bf16[3,64,128]{2,1,0:T(8,128)(2,1)S(1)}, bf16[3,64,128]{2,1,0:T(8,128)(2,1)S(1)}, u32[]{:S(2)}, u32[]{:S(2)}) collective-permute-start(bf16[3,64,128]{2,1,0:T(8,128)(2,1)S(1)} %get-tuple-element.63), channel_id=1, source_target_pairs={{0,64},{64,128},{128,192},{192,256},{256,320},{320,384},{384,448},... | collective-permute-start | bytes 147464 | tf_op jit(solution)/shard_map/ppermute | solution.py:409
  12.8 1.2 copy-start.4
  14.0 0.6 copy-start.5
  14.6 5.2 %copy-start.10 = (bf16[64,4,128]{2,1,0:T(4,128)(2,1)S(1)}, bf16[64,4,128]{2,1,0:T(4,128)(2,1)}, u32[]{:S(2)}) copy-start(bf16[64,4,128]{2,1,0:T(4,128)(2,1)} %param.15) | copy-start | bytes 196612
  16.5 3.9 %collective-permute-start.2 = (bf16[64,128]{1,0:T(8,128)(2,1)}, bf16[64,128]{1,0:T(8,128)(2,1)S(1)}, u32[]{:S(2)}, u32[]{:S(2)}) collective-permute-start(bf16[64,128]{1,0:T(8,128)(2,1)} %get-tuple-element.26), channel_id=1, source_target_pairs={{0,4},{4,8},{8,12},{12,16},{16,20},{20,24},{24,28},{28,32},{32,36}... | collective-permute-start | bytes 49160 | tf_op jit(solution)/shard_map/ppermute | solution.py:409
  17.8 4.7 %collective-permute-start.3 = (bf16[64,128]{1,0:T(8,128)(2,1)}, bf16[64,128]{1,0:T(8,128)(2,1)S(1)}, u32[]{:S(2)}, u32[]{:S(2)}) collective-permute-start(bf16[64,128]{1,0:T(8,128)(2,1)} %get-tuple-element.27), channel_id=1, source_target_pairs={{4,0},{8,4},{12,8},{16,12},{20,16},{24,20},{28,24},{32,28},{36,32}... | collective-permute-start | bytes 49160 | tf_op jit(solution)/shard_map/ppermute | solution.py:409
  20.4 2.1 %copy-start.8 = (bf16[64,128]{1,0:T(8,128)(2,1)}, bf16[64,128]{1,0:T(8,128)(2,1)S(1)}, u32[]{:S(2)}) copy-start(bf16[64,128]{1,0:T(8,128)(2,1)S(1)} %collective-permute-done.2.left) | copy-start | bytes 49156
  22.5 0.6 copy-start.9
  26.7 12.1 %all-to-all-start = ((bf16[4,144,512]{2,1,0:T(8,128)(2,1)}), bf16[4,144,512]{2,1,0:T(8,128)(2,1)S(1)}, u32[]{:S(2)}, u32[]{:S(2)}) async-start(bf16[4,144,512]{2,1,0:T(8,128)(2,1)} %get-tuple-element.28), calls=%async_computation | async-start | bytes 1179648 | tf_op jit(solution)/shard_map/all_to_all | solution.py:446
  38.8 0.8 copy-start.1
  54.7 6.4 %copy-start.3 = (f32[1024,128]{1,0:T(8,128)S(1)}, f32[1024,128]{1,0:T(8,128)}, u32[]{:S(2)}) copy-start(f32[1024,128]{1,0:T(8,128)} %get-tuple-element.36) | copy-start | bytes 1572868
  106.0 6.1 %copy-start.2 = (bf16[4,64,128]{2,1,0:T(8,128)(2,1)S(1)}, bf16[4,64,128]{2,1,0:T(8,128)(2,1)}, u32[]{:S(2)}) copy-start(bf16[4,64,128]{2,1,0:T(8,128)(2,1)} %get-tuple-element.33.mid) | copy-start | bytes 196612
  106.0 29.1 %all-to-all-start.4 = ((f32[16,9,128]{2,1,0:T(8,128)}), f32[16,9,128]{2,1,0:T(8,128)S(1)}, u32[]{:S(2)}, u32[]{:S(2)}) async-start(f32[16,9,128]{2,1,0:T(8,128)} %broadcast_in_dim.2), calls=%async_computation.4 | async-start | bytes 262144 | tf_op jit(solution)/shard_map/all_to_all | solution.py:427
  112.1 5.7 %collective-permute-start.5 = (bf16[3,64,128]{2,1,0:T(8,128)(2,1)S(1)}, bf16[3,64,128]{2,1,0:T(8,128)(2,1)S(1)}, u32[]{:S(2)}, u32[]{:S(2)}) collective-permute-start(bf16[3,64,128]{2,1,0:T(8,128)(2,1)S(1)} %get-tuple-element.60), channel_id=1, source_target_pairs={{64,0},{128,64},{192,128},{256,192},{320,256},{384,320},{448,384},... | collective-permute-start | bytes 147464 | tf_op jit(solution)/shard_map/ppermute | solution.py:409
  115.6 10.7 %copy-start.11 = (bf16[4,64,128]{2,1,0:T(8,128)(2,1)S(1)}, bf16[4,64,128]{2,1,0:T(8,128)(2,1)}, u32[]{:S(2)}) copy-start(bf16[4,64,128]{2,1,0:T(8,128)(2,1)} %get-tuple-element.32) | copy-start | bytes 196612
  115.6 3.4 %collective-permute-start.4 = (bf16[3,64,128]{2,1,0:T(8,128)(2,1)S(1)}, bf16[3,64,128]{2,1,0:T(8,128)(2,1)S(1)}, u32[]{:S(2)}, u32[]{:S(2)}) collective-permute-start(bf16[3,64,128]{2,1,0:T(8,128)(2,1)S(1)} %get-tuple-element.61), channel_id=1, source_target_pairs={{0,64},{64,128},{128,192},{192,256},{256,320},{320,384},{384,448},... | collective-permute-start | bytes 147464 | tf_op jit(solution)/shard_map/ppermute | solution.py:409
  117.9 1.1 copy-start.6
  119.0 0.6 copy-start.7
  121.5 5.5 %collective-permute-start.6 = (bf16[64,128]{1,0:T(8,128)(2,1)}, bf16[64,128]{1,0:T(8,128)(2,1)S(1)}, u32[]{:S(2)}, u32[]{:S(2)}) collective-permute-start(bf16[64,128]{1,0:T(8,128)(2,1)} %get-tuple-element.34), channel_id=1, source_target_pairs={{0,4},{4,8},{8,12},{12,16},{16,20},{20,24},{24,28},{28,32},{32,36}... | collective-permute-start | bytes 49160 | tf_op jit(solution)/shard_map/ppermute | solution.py:409
  125.0 4.7 %collective-permute-start.7 = (bf16[64,128]{1,0:T(8,128)(2,1)}, bf16[64,128]{1,0:T(8,128)(2,1)S(1)}, u32[]{:S(2)}, u32[]{:S(2)}) collective-permute-start(bf16[64,128]{1,0:T(8,128)(2,1)} %get-tuple-element.35), channel_id=1, source_target_pairs={{4,0},{8,4},{12,8},{16,12},{20,16},{24,20},{28,24},{32,28},{36,32}... | collective-permute-start | bytes 49160 | tf_op jit(solution)/shard_map/ppermute | solution.py:409
  127.0 2.7 %copy-start.13 = (bf16[64,128]{1,0:T(8,128)(2,1)}, bf16[64,128]{1,0:T(8,128)(2,1)S(1)}, u32[]{:S(2)}) copy-start(bf16[64,128]{1,0:T(8,128)(2,1)S(1)} %collective-permute-done.6.left) | copy-start | bytes 49156
  129.7 0.6 copy-start.14

commit v2 on v1

--- a/solution.py
+++ b/solution.py
@@ -16,6 +16,25 @@
 bf16 = jnp.bfloat16
 LANES = 128
 CT = 16
+GAIN = KSIZE * KSIZE
+SHIFT = GAIN + 1
+OFFSET = GAIN + 2
+
+
+def vcall(kernel, out_shape, **kw):
+    spec = pl.BlockSpec(memory_space=pltpu.VMEM)
+
+    def call(*args):
+        return pl.pallas_call(
+            kernel,
+            out_shape=out_shape,
+            in_specs=[spec] * len(args),
+            out_specs=jax.tree.map(lambda _: spec, out_shape),
+            compiler_params=pltpu.CompilerParams(vmem_limit_bytes=8 << 20),
+            **kw,
+        )(*args)
+
+    return call
 
 
 def lane_ids(rows):
@@ -101,7 +120,7 @@
 
 def edges(up, mid, down):
     shape = jax.ShapeDtypeStruct((mid.shape[1], LANES), bf16)
-    return pl.pallas_call(edges_kernel, out_shape=(shape, shape), name="edges")(up, mid, down)
+    return vcall(edges_kernel, out_shape=(shape, shape), name="edges")(up, mid, down)
 
 
 def accumulate_taps(rows, kern, at, flip):
@@ -156,7 +175,7 @@
 def forward(up, mid, down, left, right, kern, gain, shift, cot, parts):
     tile_rows, channels, _ = mid.shape
     pixels = tile_rows * LANES
-    return pl.pallas_call(
+    return vcall(
         forward_kernel,
         out_shape=(
             jax.ShapeDtypeStruct((channels, pixels), f32),
@@ -170,12 +189,6 @@
     i = lax.broadcasted_iota(jnp.int32, (n, n), 0)
     j = lax.broadcasted_iota(jnp.int32, (n, n), 1)
     return jnp.sum(jnp.where(i == j, jnp.broadcast_to(row, (n, n)), 0.0), axis=1, keepdims=True)
-
-
-def row_of(col, n):
-    i = lax.broadcasted_iota(jnp.int32, (n, n), 0)
-    j = lax.broadcasted_iota(jnp.int32, (n, n), 1)
-    return jnp.sum(jnp.where(i == j, jnp.broadcast_to(col, (n, n)), 0.0), axis=0, keepdims=True)
 
 
 def dot(a, b, dims):
@@ -247,20 +260,25 @@
     grads[n : 2 * n, :] = grad_exp[:, LANES:]
     grads[2 * n : 3 * n, :] = grad_red[:, 0:LANES]
     grads[3 * n : 4 * n, :] = grad_red[:, LANES:]
-    off[...] = dot(jnp.ones((8, pixels), bf16), s_gh[...], last)
+    sums = dot(s_gh[...], jnp.ones((pixels, LANES), bf16), ((1,), (0,)))
+    table = jnp.zeros((ch, LANES), f32)
+    lane = lane_ids(ch)
+    for j in range(sums.shape[0] // ch):
+        table = jnp.where(lane == OFFSET + j, sums[j * ch : (j + 1) * ch], table)
+    off[...] = table
 
 
 def mlp(recv, w_exp, bias, w_red):
     parts, height, pixels = recv.shape
     hid = w_red.shape[0]
     total = w_exp.shape[0]
-    return pl.pallas_call(
+    return vcall(
         mlp_kernel,
         out_shape=(
             jax.ShapeDtypeStruct(recv.shape, bf16),
             jax.ShapeDtypeStruct((2, pixels), f32),
             jax.ShapeDtypeStruct((4 * total, LANES), f32),
-            jax.ShapeDtypeStruct((8, hid), f32),
+            jax.ShapeDtypeStruct(((recv.shape[1] - CT) // 2, LANES), f32),
         ),
         scratch_shapes=[
             pltpu.VMEM((total, pixels), bf16),
@@ -272,7 +290,7 @@
     )(recv, w_exp, bias, w_red)
 
 
-def norm_back_kernel(recv, mixed, stats, gain, image, result, grad_mixed, rounded, small):
+def norm_back_kernel(recv, mixed, stats, gain, image, off, result, grad_mixed, rounded, small):
     parts, height, pixels = recv.shape
     ch = (height - CT) // 2
     tile_rows = image.shape[0]
@@ -299,26 +317,27 @@
         out = inverse * (grad * gain_col - plain - normed * cross)
         grad_mixed[i] = out
         rounded[i] = out.astype(bf16)
-    g = row_of(jnp.sum(acc_gain, axis=1, keepdims=True), ch)
-    s = row_of(jnp.sum(acc_shift, axis=1, keepdims=True), ch)
-    small[...] = jnp.broadcast_to(jnp.concatenate([g, s], axis=1), (8, LANES))
-
-
-def norm_back(recv, mixed, stats, gain, image):
+    g = jnp.sum(acc_gain, axis=1, keepdims=True)
+    s = jnp.sum(acc_shift, axis=1, keepdims=True)
+    lane = lane_ids(ch)
+    small[...] = jnp.where(lane == GAIN, g, jnp.where(lane == SHIFT, s, off[...]))
+
+
+def norm_back(recv, mixed, stats, gain, image, off):
     tile_rows, channels, _ = image.shape
-    return pl.pallas_call(
+    return vcall(
         norm_back_kernel,
         out_shape=(
             jax.ShapeDtypeStruct(image.shape, bf16),
             jax.ShapeDtypeStruct(image.shape, f32),
             jax.ShapeDtypeStruct(image.shape, bf16),
-            jax.ShapeDtypeStruct((8, LANES), f32),
+            jax.ShapeDtypeStruct((channels, LANES), f32),
         ),
         name="norm_back",
-    )(recv, mixed, stats, gain, image)
-
-
-def tap_grad_kernel(up, mid, down, left, right, grad_mixed, small, off, out):
+    )(recv, mixed, stats, gain, image, off)
+
+
+def tap_grad_kernel(up, mid, down, left, right, grad_mixed, small, out, table_ref):
     tile_rows, channels, _ = mid.shape
     lane = lane_ids(CT)
 
@@ -326,7 +345,7 @@
         at = pl.ds(pl.multiple_of(t * CT, CT), CT)
         rows = halo_rows(up, mid, down, left, right, at)
         grads = [grad_mixed[i, at, :] for i in range(tile_rows)]
-        table = jnp.zeros((CT, LANES), f32)
+        table = small[at, :]
         for b in range(KSIZE):
             shifted = [window(row, b - HALF) for row in rows]
             for a in range(KSIZE):
@@ -335,24 +354,22 @@
                     accum = accum + grads[i] * shifted[a + i]
                 value = jnp.sum(accum, axis=1, keepdims=True)
                 table = jnp.where(lane == a * KSIZE + b, value, table)
-        out[at, :] = table
+        table_ref[at, :] = table
         return carry
 
     lax.fori_loop(0, channels // CT, step, 0)
-    hid = off.shape[1]
-    out[channels : channels + 8, :] = small[...]
-    for j in range(hid // LANES):
-        out[channels + 8 * (j + 1) : channels + 8 * (j + 2), :] = off[:, j * LANES : (j + 1) * LANES]
-    used = channels + 8 * (1 + hid // LANES)
-    out[used:, :] = jnp.zeros((out.shape[0] - used, LANES), f32)
-
-
-def tap_grad(up, mid, down, left, right, grad_mixed, small, off):
-    return pl.pallas_call(
+    half = channels // 2
+    out[...] = table_ref[0:half, :] + rolled(table_ref[half:channels, :], LANES // 2)
+
+
+def tap_grad(up, mid, down, left, right, grad_mixed, small):
+    channels = mid.shape[1]
+    return vcall(
         tap_grad_kernel,
-        out_shape=jax.ShapeDtypeStruct((LANES, LANES), f32),
+        out_shape=jax.ShapeDtypeStruct((channels // 2, LANES), f32),
+        scratch_shapes=[pltpu.VMEM((channels, LANES), f32)],
         name="tap_grad",
-    )(up, mid, down, left, right, grad_mixed, small, off)
+    )(up, mid, down, left, right, grad_mixed, small)
 
 
 def backward_kernel(up, mid, down, left, right, kern, cot, out):
@@ -370,34 +387,82 @@
 
 
 def backward(up, mid, down, left, right, kern, cot):
-    return pl.pallas_call(
+    return vcall(
         backward_kernel,
         out_shape=jax.ShapeDtypeStruct(cot.shape, bf16),
         name="backward",
     )(up, mid, down, left, right, kern, cot)
 
 
-def final_kernel(scale, flat, exp_ref, red_ref, taps_ref, vec_ref):
+def gather_kernel(recv, out):
+    cols = recv.shape[0]
+    total = recv[0]
+    for c in range(1, cols):
+        total = total + recv[c]
+    n = total.shape[0] // 2
+    big, tail = total[0:n], total[n:]
+    hi = tail.astype(bf16).astype(f32)
+    low = tail - hi
+    row = lax.broadcasted_iota(jnp.int32, tail.shape, 0)
+    extra = jnp.where(row < n // 2, hi, jnp.roll(low, n // 2, 0))
+    tile = jnp.concatenate([big, extra], axis=0).astype(bf16)
+    for c in range(cols):
+        out[c] = tile
+
+
+def gather_sum(recv):
+    return vcall(gather_kernel, out_shape=jax.ShapeDtypeStruct(recv.shape, bf16), name="gather_sum")(
+        recv
+    )
+
+
+def final_kernel(scale, flat, exp_ref, red_ref, taps_ref, gain_ref, shift_ref, off_ref, small):
+    rows, cols, height, _ = flat.shape
     n = exp_ref.shape[0]
-    exp_ref[:, 0:LANES] = flat[0:n, :] * scale
-    exp_ref[:, LANES:] = flat[n : 2 * n, :] * scale
-    red_ref[:, 0:LANES] = flat[2 * n : 3 * n, :] * scale
-    red_ref[:, LANES:] = flat[3 * n : 4 * n, :] * scale
-    base = 4 * n
-    channels = taps_ref.shape[0]
-    taps_ref[...] = flat[base : base + channels, 0 : taps_ref.shape[1]] * scale
-    vec_ref[...] = flat[base + channels : base + channels + vec_ref.shape[0], :] * scale
+    part = height // 2
+    per = small.shape[0] // cols
+    for r in range(rows):
+        x = flat[r].astype(f32)
+        block = x[:, 0:part, :].reshape(cols * part, LANES) * scale
+        start = r * cols * part
+        lo = 0
+        while lo < cols * part:
+            which, at = divmod(start + lo, n)
+            size = min(cols * part - lo, n - at)
+            ref = (exp_ref, red_ref)[which // 2]
+            lane = (which % 2) * LANES
+            ref[at : at + size, lane : lane + LANES] = block[lo : lo + size]
+            lo += size
+    sums = flat[0].astype(f32)[:, part:, :]
+    for r in range(1, rows):
+        sums = sums + flat[r].astype(f32)[:, part:, :]
+    for c in range(cols):
+        x = sums[c]
+        small[c * per : (c + 1) * per, :] = x[0:per] + x[part // 2 : part // 2 + per]
+    x = small[...] * scale
+    both = jnp.concatenate([x, rolled(x, LANES // 2)], axis=0)
+    wide = jnp.concatenate([both, jnp.zeros((LANES - both.shape[0], LANES), f32)], axis=0)
+    flip = jnp.transpose(wide)[:, 0 : both.shape[0]]
+    taps_ref[...] = flip[0 : taps_ref.shape[0], :]
+    gain_ref[...] = flip[GAIN : GAIN + 1]
+    shift_ref[...] = flip[SHIFT : SHIFT + 1]
+    channels = flip.shape[1]
+    for j in range(off_ref.shape[1] // channels):
+        off_ref[:, j * channels : (j + 1) * channels] = flip[OFFSET + j : OFFSET + j + 1]
 
 
 def final(flat, scale, total, hid, channels, taps):
-    return pl.pallas_call(
+    return vcall(
         functools.partial(final_kernel, scale),
         out_shape=(
             jax.ShapeDtypeStruct((total, hid), f32),
             jax.ShapeDtypeStruct((hid, total), f32),
-            jax.ShapeDtypeStruct((channels, taps), f32),
-            jax.ShapeDtypeStruct((8 * (1 + hid // LANES), LANES), f32),
+            jax.ShapeDtypeStruct((taps, channels), f32),
+            jax.ShapeDtypeStruct((1, channels), f32),
+            jax.ShapeDtypeStruct((1, channels), f32),
+            jax.ShapeDtypeStruct((1, hid), f32),
         ),
+        scratch_shapes=[pltpu.VMEM((channels // 2, LANES), f32)],
         name="final",
     )(flat)
 
@@ -417,15 +482,20 @@
     return up, down, left, right
 
 
-def reduce_all(flat):
+def row_sum(grads):
+    rows = lax.axis_size("row")
+    part = grads.reshape(rows, grads.shape[0] // rows, LANES)
+    return lax.all_to_all(part, "row", 0, 0).sum(0)
+
+
+def col_sum(part, taps):
     rows, cols = lax.axis_size("row"), lax.axis_size("col")
-    height = flat.shape[0]
-    part = lax.all_to_all(flat.reshape(rows, height // rows, LANES), "row", 0, 0).sum(0)
-    part = part.reshape(cols, height // rows // cols, LANES)
-    part = lax.all_to_all(part, "col", 0, 0).sum(0)
-    part = jnp.broadcast_to(part[None], (cols,) + part.shape)
-    part = lax.all_to_all(part, "col", 0, 0).reshape(height // rows, LANES)
-    return lax.all_gather(part, "row", axis=0, tiled=True)
+    part = part.reshape(cols, part.shape[0] // cols, LANES)
+    taps = taps.reshape(cols, taps.shape[0] // cols, LANES)
+    pad = jnp.zeros((cols, part.shape[1] - taps.shape[1], LANES), f32)
+    part = lax.all_to_all(jnp.concatenate([part, taps, pad], axis=1), "col", 0, 0)
+    part = lax.all_to_all(gather_sum(part), "col", 0, 0)
+    return lax.all_gather(part, "row", axis=0)
 
 
 def body(
@@ -446,24 +516,25 @@
     recv = lax.all_to_all(send, "ch", 0, 0)
     send, stats, grads, off = mlp(recv, expand_weight, bias, reduce_weight)
     recv = lax.all_to_all(send, "ch", 0, 0)
-    result, grad_mixed, rounded, small = norm_back(recv, mixed, stats, gain, img)
+    part = row_sum(grads)
+    result, grad_mixed, rounded, small = norm_back(recv, mixed, stats, gain, img, off)
     g_up, g_down, g_left, g_right = halo(rounded)
-    taps = tap_grad(up, img, down, left, right, grad_mixed, small, off)
+    taps = tap_grad(up, img, down, left, right, grad_mixed, small)
     grad_image = backward(g_up, rounded, g_down, g_left, g_right, depth_kernel, cot)
-    flat = reduce_all(jnp.concatenate([grads, taps], axis=0))
+    flat = col_sum(part, taps)
     pixels_all = pixels * lax.axis_size("row") * lax.axis_size("col")
     scale = float(pixels_all) ** (-0.5)
-    grad_exp, grad_red, grad_taps, vec = final(
+    grad_exp, grad_red, grad_taps, grad_gain, grad_shift, grad_off = final(
         flat, scale, total, hid, channels, depth_kernel.shape[1]
     )
     return (
         jnp.transpose(result, (1, 0, 2)),
         jnp.transpose(grad_image, (1, 0, 2)),
-        grad_taps,
-        vec[0, :channels],
-        vec[0, channels:],
+        jnp.transpose(grad_taps),
+        grad_gain.reshape(channels),
+        grad_shift.reshape(channels),
         grad_exp,
-        vec[8::8].reshape(hid),
+        grad_off.reshape(hid),
         grad_red,
     )
 

time: 159 us -> 134 us (0.84)
  blocking collectives: 71 us -> 50.3 us
  waiting for transfers between devices: 14.4 us -> 26.5 us
  local copies, waits for them, and re-layouts: 14.4 us -> 3.87 us
  Pallas kernels: 22.2 us -> 11.7 us
  starting transfers between devices: 33.3 us -> 39.5 us
    all_to_all x2 -> x1, blocking collectives: 43.3 us -> 26.4 us  [col_sum(): lax.all_to_all(jnp.concatenate([part, taps, pad], axis=1), 'col', 0, 0)]
    pallas_call x8 -> x9, Pallas kernels: 22.2 us -> 11.7 us  [call(): pl.pallas_call(kernel, out_shape=out_shape, in_specs=[spec] * len(args),...]
    unnamed x36 -> x17, local copies, waits for them, and re-layouts: 9.74 us -> 3 us
    all_to_all x1 -> x2, waiting for transfers between devices: 0.01 us -> 6.39 us  [the longest x1 6.38 us: row_sum(): return lax.all_to_all(part, 'row', 0, 0).sum(0)]
    all_to_all x1 -> x2, starting transfers between devices: 6.14 us -> 10.6 us  [the longest x1 5.64 us: col_sum(): part = lax.all_to_all(gather_sum(part), 'col', 0, 0)]
    all_gather x1, blocking collectives: 16 us -> 12 us  [col_sum(): return lax.all_gather(part, 'row', axis=0)]
    ppermute x8, waiting for transfers between devices: 7.07 us -> 10.4 us  [neighbours(): return (lax.ppermute(last, axis, up), lax.ppermute(first, axis, down))]
    all_to_all x1, waiting for transfers between devices: 7.31 us -> 9.72 us  [body(): recv = lax.all_to_all(send, 'ch', 0, 0)]
  transfers between devices with their start and end apart: 10 -> 11, of which waited for: 5 -> 6; matrix products, arithmetic and copies ran while one was open for 3% -> 2% of each run, Pallas kernels for 3% -> 4%
where the time goes in v2:
time: 134 us; the launch traced here: 133 us
  blocking collectives  50.3 us (38%)
  starting transfers between devices  39.5 us (29%)
  waiting for transfers between devices  26.5 us (20%)
  Pallas kernels  11.7 us (9%)
  local copies, waits for them, and re-layouts  3.87 us (3%)
    all_to_all x1, blocking collectives, col_sum(): lax.all_to_all(jnp.concatenate([part, taps, pad], axis=1), 'col', 0, 0)  26.4 us
    ppermute x8, starting transfers between devices, neighbours(): return (lax.ppermute(last, axis, up), lax.ppermute(first, axis, down))  24.8 us
    all_to_all x1, blocking collectives, body(): recv = lax.all_to_all(send, 'ch', 0, 0)  12 us
    all_gather x1, blocking collectives, col_sum(): return lax.all_gather(part, 'row', axis=0)  12 us
    pallas_call x9, Pallas kernels, call(): pl.pallas_call(kernel, out_shape=out_shape, in_specs=[spec] * len(args),...  11.7 us
    ppermute x8, waiting for transfers between devices, neighbours(): return (lax.ppermute(last, axis, up), lax.ppermute(first, axis, down))  10.4 us
    all_to_all x1, waiting for transfers between devices, body(): recv = lax.all_to_all(send, 'ch', 0, 0)  9.72 us
    all_to_all x1, waiting for transfers between devices, row_sum(): return lax.all_to_all(part, 'row', 0, 0).sum(0)  6.38 us
  transfers between devices with their start and end apart: 11, of which 6 were waited for; matrix products, arithmetic and copies ran while one was open for 2% of the time, Pallas kernels for 4%

profile of v2, /device:TPU:1, one launch (start us, length us, event | category | flops | bytes accessed | tf_op | source)
XLA Modules:
  0.0 132.8 jit_solution(252052328707664534)
XLA Ops:
  0.6 0.9 copy.31
  1.5 4.6 %collective-permute-start = (bf16[3,64,128]{2,1,0:T(8,128)(2,1)S(1)}, bf16[3,64,128]{2,1,0:T(8,128)(2,1)S(1)}, u32[]{:S(2)}, u32[]{:S(2)}) collective-permute-start(bf16[3,64,128]{2,1,0:T(8,128)(2,1)S(1)} %get-tuple-element.67), channel_id=1, source_target_pairs={{0,64},{64,128},{128,192},{192,256},{256,320},{320,384},{384,448},... | collective-permute-start | bytes 147464 | tf_op jit(solution)/shard_map/ppermute | solution.py:474
  6.1 0.0 copy-start.4
  6.1 5.6 %collective-permute-start.1 = (bf16[3,64,128]{2,1,0:T(8,128)(2,1)S(1)}, bf16[3,64,128]{2,1,0:T(8,128)(2,1)S(1)}, u32[]{:S(2)}, u32[]{:S(2)}) collective-permute-start(bf16[3,64,128]{2,1,0:T(8,128)(2,1)S(1)} %get-tuple-element.66), channel_id=1, source_target_pairs={{64,0},{128,64},{192,128},{256,192},{320,256},{384,320},{448,384},... | collective-permute-start | bytes 147464 | tf_op jit(solution)/shard_map/ppermute | solution.py:474
  11.7 0.0 collective-permute-done.up
  11.7 0.8 collective-permute-done.1.down
  12.6 0.4 edges.2
  12.9 2.6 %collective-permute-start.2 = (bf16[64,128]{1,0:T(8,128)(2,1)S(1)}, bf16[64,128]{1,0:T(8,128)(2,1)S(1)}, u32[]{:S(2)}, u32[]{:S(2)}) collective-permute-start(bf16[64,128]{1,0:T(8,128)(2,1)S(1)} %get-tuple-element.28), channel_id=1, source_target_pairs={{0,4},{4,8},{8,12},{12,16},{16,20},{20,24},{24,28},{28,32},{32,36}... | collective-permute-start | bytes 49160 | tf_op jit(solution)/shard_map/ppermute | solution.py:474
  15.6 0.0 copy-start.5
  15.6 1.3 collective-permute-start.3
  16.9 0.0 copy-done.4
  16.9 0.0 copy-done.5
  16.9 0.1 copy.24.kern
  17.0 0.0 collective-permute-done.2.left
  17.0 3.2 %collective-permute-done.3.right = bf16[64,128]{1,0:T(8,128)(2,1)S(1)} collective-permute-done((bf16[64,128]{1,0:T(8,128)(2,1)S(1)}, bf16[64,128]{1,0:T(8,128)(2,1)S(1)}, u32[]{:S(2)}, u32[]{:S(2)}) %collective-permute-start.3) | collective-permute-done | bytes 16416 | tf_op jit(solution)/shard_map/ppermute | solution.py:474
  20.3 0.7 copy-done.2
  20.9 0.0 copy-done.3
  20.9 2.6 %forward.1 = (f32[64,512]{1,0:T(8,128)S(1)}, bf16[4,144,512]{2,1,0:T(8,128)(2,1)}) custom-call(bf16[3,64,128]{2,1,0:T(8,128)(2,1)S(1)} %collective-permute-done.up, bf16[4,64,128]{2,1,0:T(8,128)(2,1)S(1)} %bitcast.21, bf16[3,64,128]{2,1,0:T(8,128)(2,1)S(1)} %collective-permute-done.1.down, bf16[64,128]{1,0:T(8,128)(2,1)S(1)} %collective-permute-done.2.left, ...), custom_call_target="tpu_custom_call" | custom-call | tf_op jit(solution)/shard_map/forward/pallas_call | solution.py:28
  23.6 4.1 %all-to-all-start = ((bf16[4,144,512]{2,1,0:T(8,128)(2,1)}), bf16[4,144,512]{2,1,0:T(8,128)(2,1)S(1)}, u32[]{:S(2)}, u32[]{:S(2)}) async-start(bf16[4,144,512]{2,1,0:T(8,128)(2,1)} %get-tuple-element.30), calls=%async_computation | async-start | bytes 1179648 | tf_op jit(solution)/shard_map/all_to_all | solution.py:516
  27.7 0.8 dynamic_slice.3
  28.5 9.7 %all-to-all-done.recv = bf16[4,144,512]{2,1,0:T(8,128)(2,1)S(1)} async-done(((bf16[4,144,512]{2,1,0:T(8,128)(2,1)}), bf16[4,144,512]{2,1,0:T(8,128)(2,1)S(1)}, u32[]{:S(2)}, u32[]{:S(2)}) %all-to-all-start) | async-done | bytes 589856 | tf_op jit(solution)/shard_map/all_to_all | solution.py:516
  38.2 0.0 copy-done
  38.2 2.1 %mlp.1 = (bf16[4,144,512]{2,1,0:T(8,128)(2,1)S(1)}, f32[2,512]{1,0:T(2,128)S(1)}, f32[1024,128]{1,0:T(8,128)}, f32[64,128]{1,0:T(8,128)S(1)}) custom-call(bf16[4,144,512]{2,1,0:T(8,128)(2,1)S(1)} %all-to-all-done.recv, bf16[256,256]{1,0:T(8,128)(2,1)S(1)} %copy-done, f32[1,256]{1,0:T(1,128)S(1)} %bitcast.30, bf16[256,256]{1,0:T(8,128)(2,1)S(1)} %copy-done.1), custom_call_target="tpu_custom_call" | custom-call | tf_op jit(solution)/shard_map/mlp/pallas_call | solution.py:28
  40.3 12.0 %all_to_all.25.recv = bf16[4,144,512]{2,1,0:T(8,128)(2,1)S(1)} all-to-all(bf16[4,144,512]{2,1,0:T(8,128)(2,1)S(1)} %get-tuple-element.31), channel_id=1, replica_groups=mesh['row'=8,'col'=16,'ch'=4] {'ch'}, dimensions={0} | all-to-all | bytes 1179648 | tf_op jit(solution)/shard_map/all_to_all | solution.py:518
  52.2 4.9 %all-to-all-start.2 = ((f32[8,128,128]{2,1,0:T(8,128)}), f32[8,128,128]{2,1,0:T(8,128)S(1)}, u32[]{:S(2)}, u32[]{:S(2)}) async-start(f32[8,128,128]{2,1,0:T(8,128)} %bitcast.7), calls=%async_computation.2 | async-start | bytes 1048576 | tf_op jit(solution)/shard_map/all_to_all | solution.py:488
  57.2 0.1 pad.2.clone
  57.2 0.1 norm_back.1
  57.4 2.8 %tap_grad.1 = f32[32,128]{1,0:T(8,128)S(1)} custom-call(bf16[3,64,128]{2,1,0:T(8,128)(2,1)S(1)} %collective-permute-done.up, bf16[4,64,128]{2,1,0:T(8,128)(2,1)S(1)} %bitcast.23, bf16[3,64,128]{2,1,0:T(8,128)(2,1)S(1)} %collective-permute-done.1.down, bf16[64,128]{1,0:T(8,128)(2,1)S(1)} %collective-permute-done.2.left, ...), custom_call_target="tpu_custom_call" | custom-call | tf_op jit(solution)/shard_map/tap_grad/pallas_call | solution.py:28
  60.1 6.4 %all-to-all-done.2 = f32[8,128,128]{2,1,0:T(8,128)S(1)} async-done(((f32[8,128,128]{2,1,0:T(8,128)}), f32[8,128,128]{2,1,0:T(8,128)S(1)}, u32[]{:S(2)}, u32[]{:S(2)}) %all-to-all-start.2) | async-done | bytes 524320 | tf_op jit(solution)/shard_map/all_to_all | solution.py:488
  66.6 0.1 maximum_maximum_fusion
  66.6 26.4 %all_to_all.26.recv = f32[16,16,128]{2,1,0:T(8,128)S(1)} all-to-all(f32[16,16,128]{2,1,0:T(8,128)S(1)} %maximum_maximum_fusion), channel_id=1, replica_groups=mesh['row'=8,'col'=16,'ch'=4] {'col'}, dimensions={0} | all-to-all | bytes 262144 | tf_op jit(solution)/shard_map/all_to_all | solution.py:496
  93.1 0.7 gather_sum.1
  93.7 5.6 %all-to-all-start.4 = ((bf16[16,16,128]{2,1,0:T(8,128)(2,1)}), bf16[16,16,128]{2,1,0:T(8,128)(2,1)S(1)}, u32[]{:S(2)}, u32[]{:S(2)}) async-start(bf16[16,16,128]{2,1,0:T(8,128)(2,1)} %gather_sum.1), calls=%async_computation.4 | async-start | bytes 131072 | tf_op jit(solution)/shard_map/all_to_all | solution.py:497
  99.4 4.0 %collective-permute-start.4 = (bf16[3,64,128]{2,1,0:T(8,128)(2,1)S(1)}, bf16[3,64,128]{2,1,0:T(8,128)(2,1)S(1)}, u32[]{:S(2)}, u32[]{:S(2)}) collective-permute-start(bf16[3,64,128]{2,1,0:T(8,128)(2,1)S(1)} %get-tuple-element.65), channel_id=1, source_target_pairs={{0,64},{64,128},{128,192},{192,256},{256,320},{320,384},{384,448},... | collective-permute-start | bytes 147464 | tf_op jit(solution)/shard_map/ppermute | solution.py:474
  103.4 1.9 %collective-permute-start.5 = (bf16[3,64,128]{2,1,0:T(8,128)(2,1)S(1)}, bf16[3,64,128]{2,1,0:T(8,128)(2,1)S(1)}, u32[]{:S(2)}, u32[]{:S(2)}) collective-permute-start(bf16[3,64,128]{2,1,0:T(8,128)(2,1)S(1)} %get-tuple-element.64), channel_id=1, source_target_pairs={{64,0},{128,64},{192,128},{256,192},{320,256},{384,320},{448,384},... | collective-permute-start | bytes 147464 | tf_op jit(solution)/shard_map/ppermute | solution.py:474
  105.3 0.0 collective-permute-done.4.up
  105.3 3.8 %collective-permute-done.5.down = bf16[3,64,128]{2,1,0:T(8,128)(2,1)S(1)} collective-permute-done((bf16[3,64,128]{2,1,0:T(8,128)(2,1)S(1)}, bf16[3,64,128]{2,1,0:T(8,128)(2,1)S(1)}, u32[]{:S(2)}, u32[]{:S(2)}) %collective-permute-start.5) | collective-permute-done | bytes 49184 | tf_op jit(solution)/shard_map/ppermute | solution.py:474
  109.1 0.4 edges.3
  109.5 3.5 %collective-permute-start.6 = (bf16[64,128]{1,0:T(8,128)(2,1)S(1)}, bf16[64,128]{1,0:T(8,128)(2,1)S(1)}, u32[]{:S(2)}, u32[]{:S(2)}) collective-permute-start(bf16[64,128]{1,0:T(8,128)(2,1)S(1)} %get-tuple-element.37), channel_id=1, source_target_pairs={{0,4},{4,8},{8,12},{12,16},{16,20},{20,24},{24,28},{28,32},{32,36}... | collective-permute-start | bytes 49160 | tf_op jit(solution)/shard_map/ppermute | solution.py:474
  113.0 1.3 collective-permute-start.7
  114.3 0.7 copy.26
  115.0 0.0 collective-permute-done.6.left
  115.0 2.5 %collective-permute-done.7.right = bf16[64,128]{1,0:T(8,128)(2,1)S(1)} collective-permute-done((bf16[64,128]{1,0:T(8,128)(2,1)S(1)}, bf16[64,128]{1,0:T(8,128)(2,1)S(1)}, u32[]{:S(2)}, u32[]{:S(2)}) %collective-permute-start.7) | collective-permute-done | bytes 16416 | tf_op jit(solution)/shard_map/ppermute | solution.py:474
  117.5 1.7 %backward.1 = bf16[4,64,128]{2,1,0:T(8,128)(2,1)S(1)} custom-call(bf16[3,64,128]{2,1,0:T(8,128)(2,1)S(1)} %collective-permute-done.4.up, bf16[4,64,128]{2,1,0:T(8,128)(2,1)S(1)} %get-tuple-element.36.mid, bf16[3,64,128]{2,1,0:T(8,128)(2,1)S(1)} %collective-permute-done.5.down, bf16[64,128]{1,0:T(8,128)(2,1)S(1)} %collective-permute-done.6.left, ...), custom_call_target="tpu_custom_call" | custom-call | tf_op jit(solution)/shard_map/backward/pallas_call | solution.py:28
  119.2 0.7 copy.27
  119.9 0.0 all-to-all-done.4
  119.9 12.0 %all-gather = bf16[128,16,128]{2,1,0:T(8,128)(2,1)S(1)} all-gather(bf16[16,16,128]{2,1,0:T(8,128)(2,1)S(1)} %all-to-all-done.4), channel_id=2, replica_groups=mesh['row'=8,'col'=16,'ch'=4] {'row'}, dimensions={0}, use_global_device_ids=true | all-gather | bytes 589824 | tf_op jit(solution)/shard_map/all_gather | solution.py:498
  131.8 1.0 final.1
  (10 shorter events, 0.1 us)
Async XLA Ops:
  1.5 10.2 %collective-permute-start = (bf16[3,64,128]{2,1,0:T(8,128)(2,1)S(1)}, bf16[3,64,128]{2,1,0:T(8,128)(2,1)S(1)}, u32[]{:S(2)}, u32[]{:S(2)}) collective-permute-start(bf16[3,64,128]{2,1,0:T(8,128)(2,1)S(1)} %get-tuple-element.67), channel_id=1, source_target_pairs={{0,64},{64,128},{128,192},{192,256},{256,320},{320,384},{384,448},... | collective-permute-start | bytes 147464 | tf_op jit(solution)/shard_map/ppermute | solution.py:474
  6.1 10.8 %copy-start.4 = (bf16[64,4,128]{2,1,0:T(4,128)(2,1)S(1)}, bf16[64,4,128]{2,1,0:T(4,128)(2,1)}, u32[]{:S(2)}) copy-start(bf16[64,4,128]{2,1,0:T(4,128)(2,1)} %param.15) | copy-start | bytes 196612
  6.1 6.5 %collective-permute-start.1 = (bf16[3,64,128]{2,1,0:T(8,128)(2,1)S(1)}, bf16[3,64,128]{2,1,0:T(8,128)(2,1)S(1)}, u32[]{:S(2)}, u32[]{:S(2)}) collective-permute-start(bf16[3,64,128]{2,1,0:T(8,128)(2,1)S(1)} %get-tuple-element.66), channel_id=1, source_target_pairs={{64,0},{128,64},{192,128},{256,192},{320,256},{384,320},{448,384},... | collective-permute-start | bytes 147464 | tf_op jit(solution)/shard_map/ppermute | solution.py:474
  12.9 4.1 %collective-permute-start.2 = (bf16[64,128]{1,0:T(8,128)(2,1)S(1)}, bf16[64,128]{1,0:T(8,128)(2,1)S(1)}, u32[]{:S(2)}, u32[]{:S(2)}) collective-permute-start(bf16[64,128]{1,0:T(8,128)(2,1)S(1)} %get-tuple-element.28), channel_id=1, source_target_pairs={{0,4},{4,8},{8,12},{12,16},{16,20},{20,24},{24,28},{28,32},{32,36}... | collective-permute-start | bytes 49160 | tf_op jit(solution)/shard_map/ppermute | solution.py:474
  15.6 1.3 %copy-start.5 = (f32[64,49]{0,1:T(8,128)S(1)}, f32[64,49]{0,1:T(8,128)}, u32[]{:S(2)}) copy-start(f32[64,49]{0,1:T(8,128)} %param.9) | copy-start | bytes 37636
  15.6 4.7 %collective-permute-start.3 = (bf16[64,128]{1,0:T(8,128)(2,1)S(1)}, bf16[64,128]{1,0:T(8,128)(2,1)S(1)}, u32[]{:S(2)}, u32[]{:S(2)}) collective-permute-start(bf16[64,128]{1,0:T(8,128)(2,1)S(1)} %get-tuple-element.29), channel_id=1, source_target_pairs={{4,0},{8,4},{12,8},{16,12},{20,16},{24,20},{28,24},{32,28},{36,32}... | collective-permute-start | bytes 49160 | tf_op jit(solution)/shard_map/ppermute | solution.py:474
  20.3 0.7 copy-start.2
  20.3 0.7 copy-start.3
  23.6 14.6 %copy-start = (bf16[256,256]{1,0:T(8,128)(2,1)S(1)}, bf16[256,256]{1,0:T(8,128)(2,1)}, u32[]{:S(2)}) copy-start(bf16[256,256]{1,0:T(8,128)(2,1)} %w_exp.1) | copy-start | bytes 393220
  23.6 14.6 %copy-start.1 = (bf16[256,256]{1,0:T(8,128)(2,1)S(1)}, bf16[256,256]{1,0:T(8,128)(2,1)}, u32[]{:S(2)}) copy-start(bf16[256,256]{1,0:T(8,128)(2,1)} %w_red.1) | copy-start | bytes 393220
  23.6 14.6 %all-to-all-start = ((bf16[4,144,512]{2,1,0:T(8,128)(2,1)}), bf16[4,144,512]{2,1,0:T(8,128)(2,1)S(1)}, u32[]{:S(2)}, u32[]{:S(2)}) async-start(bf16[4,144,512]{2,1,0:T(8,128)(2,1)} %get-tuple-element.30), calls=%async_computation | async-start | bytes 1179648 | tf_op jit(solution)/shard_map/all_to_all | solution.py:516
  52.2 14.3 %all-to-all-start.2 = ((f32[8,128,128]{2,1,0:T(8,128)}), f32[8,128,128]{2,1,0:T(8,128)S(1)}, u32[]{:S(2)}, u32[]{:S(2)}) async-start(f32[8,128,128]{2,1,0:T(8,128)} %bitcast.7), calls=%async_computation.2 | async-start | bytes 1048576 | tf_op jit(solution)/shard_map/all_to_all | solution.py:488
  93.7 26.2 %all-to-all-start.4 = ((bf16[16,16,128]{2,1,0:T(8,128)(2,1)}), bf16[16,16,128]{2,1,0:T(8,128)(2,1)S(1)}, u32[]{:S(2)}, u32[]{:S(2)}) async-start(bf16[16,16,128]{2,1,0:T(8,128)(2,1)} %gather_sum.1), calls=%async_computation.4 | async-start | bytes 131072 | tf_op jit(solution)/shard_map/all_to_all | solution.py:497
  99.4 5.9 %collective-permute-start.4 = (bf16[3,64,128]{2,1,0:T(8,128)(2,1)S(1)}, bf16[3,64,128]{2,1,0:T(8,128)(2,1)S(1)}, u32[]{:S(2)}, u32[]{:S(2)}) collective-permute-start(bf16[3,64,128]{2,1,0:T(8,128)(2,1)S(1)} %get-tuple-element.65), channel_id=1, source_target_pairs={{0,64},{64,128},{128,192},{192,256},{256,320},{320,384},{384,448},... | collective-permute-start | bytes 147464 | tf_op jit(solution)/shard_map/ppermute | solution.py:474
  103.4 5.7 %collective-permute-start.5 = (bf16[3,64,128]{2,1,0:T(8,128)(2,1)S(1)}, bf16[3,64,128]{2,1,0:T(8,128)(2,1)S(1)}, u32[]{:S(2)}, u32[]{:S(2)}) collective-permute-start(bf16[3,64,128]{2,1,0:T(8,128)(2,1)S(1)} %get-tuple-element.64), channel_id=1, source_target_pairs={{64,0},{128,64},{192,128},{256,192},{320,256},{384,320},{448,384},... | collective-permute-start | bytes 147464 | tf_op jit(solution)/shard_map/ppermute | solution.py:474
  109.5 5.5 %collective-permute-start.6 = (bf16[64,128]{1,0:T(8,128)(2,1)S(1)}, bf16[64,128]{1,0:T(8,128)(2,1)S(1)}, u32[]{:S(2)}, u32[]{:S(2)}) collective-permute-start(bf16[64,128]{1,0:T(8,128)(2,1)S(1)} %get-tuple-element.37), channel_id=1, source_target_pairs={{0,4},{4,8},{8,12},{12,16},{16,20},{20,24},{24,28},{28,32},{32,36}... | collective-permute-start | bytes 49160 | tf_op jit(solution)/shard_map/ppermute | solution.py:474
  113.0 4.5 %collective-permute-start.7 = (bf16[64,128]{1,0:T(8,128)(2,1)S(1)}, bf16[64,128]{1,0:T(8,128)(2,1)S(1)}, u32[]{:S(2)}, u32[]{:S(2)}) collective-permute-start(bf16[64,128]{1,0:T(8,128)(2,1)S(1)} %get-tuple-element.38), channel_id=1, source_target_pairs={{4,0},{8,4},{12,8},{16,12},{20,16},{24,20},{28,24},{32,28},{36,32}... | collective-permute-start | bytes 49160 | tf_op jit(solution)/shard_map/ppermute | solution.py:474

commit v3 on v2

--- a/solution.py
+++ b/solution.py
@@ -150,7 +150,6 @@
         return carry
 
     lax.fori_loop(0, channels // CT, step, 0)
-    pixels = tile_rows * LANES
     for i in range(tile_rows):
         cols = slice(i * LANES, (i + 1) * LANES)
         x = mixed[:, cols]
@@ -195,7 +194,59 @@
     return lax.dot_general(a, b, (dims, ((), ())), preferred_element_type=f32)
 
 
-def mlp_kernel(recv, w_exp, bias, w_red, payload, stats_out, grads, off, s_norm, s_act, s_cot, s_gh):
+def row_masks(size):
+    return {8: (1, 2, 6), 4: (1, 2), 2: (1,)}[size]
+
+
+def row_bits(r, size):
+    if size == 8:
+        return (r % 2, (r // 2 + r // 4) % 2, r // 4)
+    return (r % 2, r // 2)[: size.bit_length() - 1]
+
+
+def row_chunk(r, size):
+    chunk = 0
+    for bit in row_bits(r, size):
+        chunk = 2 * chunk + bit
+    return chunk
+
+
+def row_bit(step):
+    return row_bits(lax.axis_index("row"), lax.axis_size("row"))[step]
+
+
+def halves(ref, step, send, keep):
+    n = send.shape[0]
+    bit = row_bit(step)
+    send[...] = ref[pl.ds(pl.multiple_of((1 - bit) * n, n), n), :]
+    keep[...] = ref[pl.ds(pl.multiple_of(bit * n, n), n), :]
+
+
+def halve_kernel(step, x, recv, send, keep, total):
+    total[...] = x[...] + recv[...]
+    halves(total, step, send, keep)
+
+
+def halve(step, x, recv, name):
+    shape = jax.ShapeDtypeStruct((x.shape[0] // 2, LANES), f32)
+    return vcall(
+        functools.partial(halve_kernel, step),
+        out_shape=(shape, shape),
+        scratch_shapes=[pltpu.VMEM(x.shape, f32)],
+        name=name,
+    )(x, recv)
+
+
+def reduce_rows(send, keep):
+    size = lax.axis_size("row")
+    for step, mask in enumerate(row_masks(size)):
+        recv = lax.ppermute(send, "row", [(i, i ^ mask) for i in range(size)])
+        if step + 1 < len(row_masks(size)):
+            send, keep = halve(step + 1, keep, recv, "halve")
+    return keep, recv
+
+
+def mlp_kernel(recv, w_exp, bias, w_red, payload, stats_out, send, keep, off, grads, s_norm, s_act, s_cot, s_gh):
     parts, height, pixels = recv.shape
     ch = (height - CT) // 2
     total = parts * ch
@@ -260,6 +311,7 @@
     grads[n : 2 * n, :] = grad_exp[:, LANES:]
     grads[2 * n : 3 * n, :] = grad_red[:, 0:LANES]
     grads[3 * n : 4 * n, :] = grad_red[:, LANES:]
+    halves(grads, 0, send, keep)
     sums = dot(s_gh[...], jnp.ones((pixels, LANES), bf16), ((1,), (0,)))
     table = jnp.zeros((ch, LANES), f32)
     lane = lane_ids(ch)
@@ -269,7 +321,7 @@
 
 
 def mlp(recv, w_exp, bias, w_red):
-    parts, height, pixels = recv.shape
+    _, _, pixels = recv.shape
     hid = w_red.shape[0]
     total = w_exp.shape[0]
     return vcall(
@@ -277,10 +329,12 @@
         out_shape=(
             jax.ShapeDtypeStruct(recv.shape, bf16),
             jax.ShapeDtypeStruct((2, pixels), f32),
-            jax.ShapeDtypeStruct((4 * total, LANES), f32),
+            jax.ShapeDtypeStruct((2 * total, LANES), f32),
+            jax.ShapeDtypeStruct((2 * total, LANES), f32),
             jax.ShapeDtypeStruct(((recv.shape[1] - CT) // 2, LANES), f32),
         ),
         scratch_shapes=[
+            pltpu.VMEM((4 * total, LANES), f32),
             pltpu.VMEM((total, pixels), bf16),
             pltpu.VMEM((hid, pixels), bf16),
             pltpu.VMEM((total, pixels), bf16),
@@ -291,7 +345,7 @@
 
 
 def norm_back_kernel(recv, mixed, stats, gain, image, off, result, grad_mixed, rounded, small):
-    parts, height, pixels = recv.shape
+    parts, height, _ = recv.shape
     ch = (height - CT) // 2
     tile_rows = image.shape[0]
     total = parts * ch
@@ -324,7 +378,7 @@
 
 
 def norm_back(recv, mixed, stats, gain, image, off):
-    tile_rows, channels, _ = image.shape
+    _, channels, _ = image.shape
     return vcall(
         norm_back_kernel,
         out_shape=(
@@ -337,7 +391,7 @@
     )(recv, mixed, stats, gain, image, off)
 
 
-def tap_grad_kernel(up, mid, down, left, right, grad_mixed, small, out, table_ref):
+def tap_grad_kernel(up, mid, down, left, right, grad_mixed, small, send, keep, table_ref, total):
     tile_rows, channels, _ = mid.shape
     lane = lane_ids(CT)
 
@@ -359,15 +413,17 @@
 
     lax.fori_loop(0, channels // CT, step, 0)
     half = channels // 2
-    out[...] = table_ref[0:half, :] + rolled(table_ref[half:channels, :], LANES // 2)
+    total[...] = table_ref[0:half, :] + rolled(table_ref[half:channels, :], LANES // 2)
+    halves(total, 0, send, keep)
 
 
 def tap_grad(up, mid, down, left, right, grad_mixed, small):
     channels = mid.shape[1]
+    shape = jax.ShapeDtypeStruct((channels // 4, LANES), f32)
     return vcall(
         tap_grad_kernel,
-        out_shape=jax.ShapeDtypeStruct((channels // 2, LANES), f32),
-        scratch_shapes=[pltpu.VMEM((channels, LANES), f32)],
+        out_shape=(shape, shape),
+        scratch_shapes=[pltpu.VMEM((channels, LANES), f32), pltpu.VMEM((channels // 2, LANES), f32)],
         name="tap_grad",
     )(up, mid, down, left, right, grad_mixed, small)
 
@@ -394,52 +450,76 @@
     )(up, mid, down, left, right, kern, cot)
 
 
-def gather_kernel(recv, out):
-    cols = recv.shape[0]
-    total = recv[0]
+def hi_lo(x):
+    hi = x.astype(bf16).astype(f32)
+    return jnp.concatenate([hi, x - hi], axis=0)
+
+
+def col_pack_kernel(big, small, more, out):
+    total = big[0]
+    for c in range(1, big.shape[0]):
+        total = total + big[c]
+    tail = small[...] + more[...]
+    tile = jnp.concatenate([total, hi_lo(tail)], axis=0).astype(bf16)
+    for c in range(out.shape[0]):
+        out[c] = tile
+
+
+def col_pack(big, small, more):
+    cols, part, _ = big.shape
+    shape = (cols, part + 2 * small.shape[0], LANES)
+    return vcall(col_pack_kernel, out_shape=jax.ShapeDtypeStruct(shape, bf16), name="col_pack")(
+        big, small, more
+    )
+
+
+def row_pack_kernel(per, recv, out):
+    cols, height, _ = recv.shape
+    part = height - 2 * per
+    x = recv[...].astype(f32)
+    big = x[:, 0:part, :].reshape(cols * part, LANES)
+    tail = x[0, part:, :]
     for c in range(1, cols):
-        total = total + recv[c]
-    n = total.shape[0] // 2
-    big, tail = total[0:n], total[n:]
-    hi = tail.astype(bf16).astype(f32)
-    low = tail - hi
-    row = lax.broadcasted_iota(jnp.int32, tail.shape, 0)
-    extra = jnp.where(row < n // 2, hi, jnp.roll(low, n // 2, 0))
-    tile = jnp.concatenate([big, extra], axis=0).astype(bf16)
-    for c in range(cols):
-        out[c] = tile
-
-
-def gather_sum(recv):
-    return vcall(gather_kernel, out_shape=jax.ShapeDtypeStruct(recv.shape, bf16), name="gather_sum")(
-        recv
-    )
+        tail = tail + x[c, part:, :]
+    extra = hi_lo(tail[0:per] + tail[per:])
+    pad = jnp.zeros((CT - 2 * per % CT, LANES), f32) if 2 * per % CT else None
+    pieces = [big, extra] if pad is None else [big, extra, pad]
+    tile = jnp.concatenate(pieces, axis=0).astype(bf16)
+    for r in range(out.shape[0]):
+        out[r] = tile
+
+
+def row_pack(recv, rows, per):
+    cols, height, _ = recv.shape
+    tall = cols * (height - 2 * per) + -(-2 * per // CT) * CT
+    return vcall(
+        functools.partial(row_pack_kernel, per),
+        out_shape=jax.ShapeDtypeStruct((rows, tall, LANES), bf16),
+        name="row_pack",
+    )(recv)
 
 
 def final_kernel(scale, flat, exp_ref, red_ref, taps_ref, gain_ref, shift_ref, off_ref, small):
-    rows, cols, height, _ = flat.shape
+    rows = flat.shape[0]
     n = exp_ref.shape[0]
-    part = height // 2
-    per = small.shape[0] // cols
+    per = small.shape[0] // rows
+    size_all = 4 * n // rows
     for r in range(rows):
-        x = flat[r].astype(f32)
-        block = x[:, 0:part, :].reshape(cols * part, LANES) * scale
-        start = r * cols * part
+        x = flat[r].astype(f32) * scale
+        block = x[0:size_all]
+        tail = x[size_all : size_all + per] + x[size_all + per : size_all + 2 * per]
+        chunk = row_chunk(r, rows)
+        small[chunk * per : (chunk + 1) * per, :] = tail
+        start = chunk * size_all
         lo = 0
-        while lo < cols * part:
+        while lo < size_all:
             which, at = divmod(start + lo, n)
-            size = min(cols * part - lo, n - at)
+            size = min(size_all - lo, n - at)
             ref = (exp_ref, red_ref)[which // 2]
             lane = (which % 2) * LANES
             ref[at : at + size, lane : lane + LANES] = block[lo : lo + size]
             lo += size
-    sums = flat[0].astype(f32)[:, part:, :]
-    for r in range(1, rows):
-        sums = sums + flat[r].astype(f32)[:, part:, :]
-    for c in range(cols):
-        x = sums[c]
-        small[c * per : (c + 1) * per, :] = x[0:per] + x[part // 2 : part // 2 + per]
-    x = small[...] * scale
+    x = small[...]
     both = jnp.concatenate([x, rolled(x, LANES // 2)], axis=0)
     wide = jnp.concatenate([both, jnp.zeros((LANES - both.shape[0], LANES), f32)], axis=0)
     flip = jnp.transpose(wide)[:, 0 : both.shape[0]]
@@ -482,20 +562,21 @@
     return up, down, left, right
 
 
-def row_sum(grads):
-    rows = lax.axis_size("row")
-    part = grads.reshape(rows, grads.shape[0] // rows, LANES)
-    return lax.all_to_all(part, "row", 0, 0).sum(0)
-
-
-def col_sum(part, taps):
-    rows, cols = lax.axis_size("row"), lax.axis_size("col")
-    part = part.reshape(cols, part.shape[0] // cols, LANES)
-    taps = taps.reshape(cols, taps.shape[0] // cols, LANES)
-    pad = jnp.zeros((cols, part.shape[1] - taps.shape[1], LANES), f32)
-    part = lax.all_to_all(jnp.concatenate([part, taps, pad], axis=1), "col", 0, 0)
-    part = lax.all_to_all(gather_sum(part), "col", 0, 0)
-    return lax.all_gather(part, "row", axis=0)
+def exchange(x, axis):
+    return lax.all_to_all(x, axis, 0, 0)
+
+
+def reduce_big(send, keep):
+    cols = lax.axis_size("col")
+    keep, recv = reduce_rows(send, keep)
+    part = keep + recv
+    return exchange(part.reshape(cols, part.shape[0] // cols, LANES), "col")
+
+
+def reduce_rest(big, send, keep):
+    keep, recv = reduce_rows(send, keep)
+    flat = exchange(col_pack(big, keep, recv), "col")
+    return exchange(row_pack(flat, lax.axis_size("row"), keep.shape[0]), "row")
 
 
 def body(
@@ -513,15 +594,15 @@
     bias = lax.dynamic_slice_in_dim(expand_bias, lax.axis_index("ch") * hid, hid).reshape(1, hid)
     up, down, left, right = halo(img)
     mixed, send = forward(up, img, down, left, right, depth_kernel, gain, shift, cot, parts)
-    recv = lax.all_to_all(send, "ch", 0, 0)
-    send, stats, grads, off = mlp(recv, expand_weight, bias, reduce_weight)
-    recv = lax.all_to_all(send, "ch", 0, 0)
-    part = row_sum(grads)
+    recv = exchange(send, "ch")
+    send, stats, give, keep, off = mlp(recv, expand_weight, bias, reduce_weight)
+    recv = exchange(send, "ch")
+    big = reduce_big(give, keep)
     result, grad_mixed, rounded, small = norm_back(recv, mixed, stats, gain, img, off)
     g_up, g_down, g_left, g_right = halo(rounded)
-    taps = tap_grad(up, img, down, left, right, grad_mixed, small)
+    give, keep = tap_grad(up, img, down, left, right, grad_mixed, small)
     grad_image = backward(g_up, rounded, g_down, g_left, g_right, depth_kernel, cot)
-    flat = col_sum(part, taps)
+    flat = reduce_rest(big, give, keep)
     pixels_all = pixels * lax.axis_size("row") * lax.axis_size("col")
     scale = float(pixels_all) ** (-0.5)
     grad_exp, grad_red, grad_taps, grad_gain, grad_shift, grad_off = final(
@@ -560,4 +641,5 @@
         P("ch"),
         P("ch", None),
     )
+
     return jax.shard_map(body, mesh=mesh, in_specs=in_specs, out_specs=out_specs, check_vma=False)

time: 134 us -> 143 us (1.067)
  starting transfers between devices: 39.5 us -> 73.4 us
  blocking collectives: 50.3 us -> 22.8 us
    ppermute x0 -> x6, starting transfers between devices: none -> 21.5 us  [reduce_rows(): recv = lax.ppermute(send, 'row', [(i, i ^ mask) for i in range(size)])]
    all_to_all x2 -> x1, blocking collectives: 38.4 us -> 22.8 us  [exchange(): return lax.all_to_all(x, axis, 0, 0)]
    all_to_all x3 -> x4, starting transfers between devices: 14.7 us -> 29.2 us  [exchange(): return lax.all_to_all(x, axis, 0, 0)]
    all_gather x1 -> x0, blocking collectives: 12 us -> none  [col_sum(): return lax.all_gather(part, 'row', axis=0)]
    ppermute x0 -> x6, waiting for transfers between devices: none -> 11.2 us  [reduce_rows(): recv = lax.ppermute(send, 'row', [(i, i ^ mask) for i in range(size)])]
    all_to_all x3 -> x4, waiting for transfers between devices: 16.1 us -> 7.88 us  [exchange(): return lax.all_to_all(x, axis, 0, 0)]
    ppermute x8, waiting for transfers between devices: 10.4 us -> 7.9 us  [neighbours(): return (lax.ppermute(last, axis, up), lax.ppermute(first, axis, down))]
    ppermute x8, starting transfers between devices: 24.8 us -> 22.7 us  [neighbours(): return (lax.ppermute(last, axis, up), lax.ppermute(first, axis, down))]
  transfers between devices with their start and end apart: 11 -> 18, of which waited for: 6 -> 11; matrix products, arithmetic and copies ran while one was open for 2% -> 2% of each run, Pallas kernels for 4% -> 4%
where the time goes in v3:
time: 143 us; the launch traced here: 140 us
  starting transfers between devices  73.4 us (51%)
  waiting for transfers between devices  26.9 us (19%)
  blocking collectives  22.8 us (16%)
  Pallas kernels  12 us (8%)
  local copies, waits for them, and re-layouts  3.79 us (3%)
    all_to_all x4, starting transfers between devices, exchange(): return lax.all_to_all(x, axis, 0, 0)  29.2 us
    all_to_all x1, blocking collectives, exchange(): return lax.all_to_all(x, axis, 0, 0)  22.8 us
    ppermute x8, starting transfers between devices, neighbours(): return (lax.ppermute(last, axis, up), lax.ppermute(first, axis, down))  22.7 us
    ppermute x6, starting transfers between devices, reduce_rows(): recv = lax.ppermute(send, 'row', [(i, i ^ mask) for i in range(size)])  21.5 us
    pallas_call x14, Pallas kernels, call(): pl.pallas_call(kernel, out_shape=out_shape, in_specs=[spec] * len(args),...  12 us
    ppermute x6, waiting for transfers between devices, reduce_rows(): recv = lax.ppermute(send, 'row', [(i, i ^ mask) for i in range(size)])  11.2 us
    ppermute x8, waiting for transfers between devices, neighbours(): return (lax.ppermute(last, axis, up), lax.ppermute(first, axis, down))  7.9 us
    all_to_all x4, waiting for transfers between devices, exchange(): return lax.all_to_all(x, axis, 0, 0)  7.88 us
  transfers between devices with their start and end apart: 18, of which 11 were waited for; matrix products, arithmetic and copies ran while one was open for 2% of the time, Pallas kernels for 4%

profile of v3, /device:TPU:1, one launch (start us, length us, event | category | flops | bytes accessed | tf_op | source)
XLA Modules:
  0.0 140.5 jit_solution(16691118453720722314)
XLA Ops:
  0.6 0.9 copy.25
  1.5 8.7 %collective-permute-start.1 = (bf16[3,64,128]{2,1,0:T(8,128)(2,1)S(1)}, bf16[3,64,128]{2,1,0:T(8,128)(2,1)S(1)}, u32[]{:S(2)}, u32[]{:S(2)}) collective-permute-start(bf16[3,64,128]{2,1,0:T(8,128)(2,1)S(1)} %get-tuple-element.80), channel_id=1, source_target_pairs={{64,0},{128,64},{192,128},{256,192},{320,256},{384,320},{448,384},... | collective-permute-start | bytes 147464 | tf_op jit(solution)/shard_map/ppermute | solution.py:554
  10.3 0.0 copy-start.5
  10.3 1.9 %collective-permute-start = (bf16[3,64,128]{2,1,0:T(8,128)(2,1)S(1)}, bf16[3,64,128]{2,1,0:T(8,128)(2,1)S(1)}, u32[]{:S(2)}, u32[]{:S(2)}) collective-permute-start(bf16[3,64,128]{2,1,0:T(8,128)(2,1)S(1)} %get-tuple-element.81), channel_id=1, source_target_pairs={{0,64},{64,128},{128,192},{192,256},{256,320},{320,384},{384,448},... | collective-permute-start | bytes 147464 | tf_op jit(solution)/shard_map/ppermute | solution.py:554
  12.2 1.2 collective-permute-done.up
  13.4 0.4 edges.2
  13.8 1.3 collective-permute-start.2
  15.1 1.3 collective-permute-start.3
  16.4 0.1 copy.18.kern
  16.5 3.1 %collective-permute-done.3.right = bf16[64,128]{1,0:T(8,128)(2,1)S(1)} collective-permute-done((bf16[64,128]{1,0:T(8,128)(2,1)S(1)}, bf16[64,128]{1,0:T(8,128)(2,1)S(1)}, u32[]{:S(2)}, u32[]{:S(2)}) %collective-permute-start.3) | collective-permute-done | bytes 16416 | tf_op jit(solution)/shard_map/ppermute | solution.py:554
  19.6 0.7 copy-done.2
  20.2 0.0 copy-done.3
  20.2 2.6 %forward.1 = (f32[64,512]{1,0:T(8,128)S(1)}, bf16[4,144,512]{2,1,0:T(8,128)(2,1)}) custom-call(bf16[3,64,128]{2,1,0:T(8,128)(2,1)S(1)} %collective-permute-done.up, bf16[4,64,128]{2,1,0:T(8,128)(2,1)S(1)} %bitcast.19, bf16[3,64,128]{2,1,0:T(8,128)(2,1)S(1)} %collective-permute-done.1.down, bf16[64,128]{1,0:T(8,128)(2,1)S(1)} %collective-permute-done.2.left, ...), custom_call_target="tpu_custom_call" | custom-call | tf_op jit(solution)/shard_map/forward/pallas_call | solution.py:28
  22.9 3.6 %all-to-all-start = ((bf16[4,144,512]{2,1,0:T(8,128)(2,1)}), bf16[4,144,512]{2,1,0:T(8,128)(2,1)S(1)}, u32[]{:S(2)}, u32[]{:S(2)}) async-start(bf16[4,144,512]{2,1,0:T(8,128)(2,1)} %get-tuple-element.41), calls=%async_computation | async-start | bytes 1179648 | tf_op jit(solution)/shard_map/all_to_all | solution.py:566
  26.5 0.8 dynamic_slice.3
  27.2 7.9 %all-to-all-done.recv = bf16[4,144,512]{2,1,0:T(8,128)(2,1)S(1)} async-done(((bf16[4,144,512]{2,1,0:T(8,128)(2,1)}), bf16[4,144,512]{2,1,0:T(8,128)(2,1)S(1)}, u32[]{:S(2)}, u32[]{:S(2)}) %all-to-all-start) | async-done | bytes 589856 | tf_op jit(solution)/shard_map/all_to_all | solution.py:566
  35.1 2.2 %mlp.1 = (bf16[4,144,512]{2,1,0:T(8,128)(2,1)}, f32[2,512]{1,0:T(2,128)S(1)}, f32[512,128]{1,0:T(8,128)S(1)}, f32[512,128]{1,0:T(8,128)S(1)}, f32[64,128]{1,0:T(8,128)S(1)}) custom-call(bf16[4,144,512]{2,1,0:T(8,128)(2,1)S(1)} %all-to-all-done.recv, bf16[256,256]{1,0:T(8,128)(2,1)S(1)} %copy-done, f32[1,256]{1,0:T(1,128)S(1)} %bitcast.26, ...), custom_call_target="tpu_custom_call" | custom-call | tf_op jit(solution)/shard_map/mlp/pallas_call | solution.py:28
  37.3 4.4 %collective-permute-start.8 = (f32[512,128]{1,0:T(8,128)S(1)}, f32[512,128]{1,0:T(8,128)S(1)}, u32[]{:S(2)}, u32[]{:S(2)}) collective-permute-start(f32[512,128]{1,0:T(8,128)S(1)} %get-tuple-element.51), channel_id=1, source_target_pairs={{0,64},{64,0},{128,192},{192,128},{256,320},{320,256},{384,448},{4... | collective-permute-start | bytes 786440 | tf_op jit(solution)/shard_map/ppermute | solution.py:243
  41.6 3.5 %all-to-all-start.1 = ((bf16[4,144,512]{2,1,0:T(8,128)(2,1)}), bf16[4,144,512]{2,1,0:T(8,128)(2,1)S(1)}, u32[]{:S(2)}, u32[]{:S(2)}) async-start(bf16[4,144,512]{2,1,0:T(8,128)(2,1)} %get-tuple-element.42), calls=%async_computation.1 | async-start | bytes 1179648 | tf_op jit(solution)/shard_map/all_to_all | solution.py:566
  45.2 2.8 %collective-permute-start.9 = (f32[256,128]{1,0:T(8,128)S(1)}, f32[256,128]{1,0:T(8,128)S(1)}, u32[]{:S(2)}, u32[]{:S(2)}) collective-permute-start(f32[256,128]{1,0:T(8,128)S(1)} %get-tuple-element.53), channel_id=1, source_target_pairs={{0,128},{64,192},{128,0},{192,64},{256,384},{320,448},{384,256},{4... | collective-permute-start | bytes 393224 | tf_op jit(solution)/shard_map/ppermute | solution.py:243
  48.0 4.2 %collective-permute-done.9.recv = f32[256,128]{1,0:T(8,128)S(1)} collective-permute-done((f32[256,128]{1,0:T(8,128)S(1)}, f32[256,128]{1,0:T(8,128)S(1)}, u32[]{:S(2)}, u32[]{:S(2)}) %collective-permute-start.9) | collective-permute-done | bytes 131104 | tf_op jit(solution)/shard_map/ppermute | solution.py:243
  52.2 3.6 %collective-permute-start.10 = (f32[128,128]{1,0:T(8,128)S(1)}, f32[128,128]{1,0:T(8,128)S(1)}, u32[]{:S(2)}, u32[]{:S(2)}) collective-permute-start(f32[128,128]{1,0:T(8,128)S(1)} %get-tuple-element.55), channel_id=1, source_target_pairs={{0,384},{64,448},{128,256},{192,320},{256,128},{320,192},{384,0},{... | collective-permute-start | bytes 196616 | tf_op jit(solution)/shard_map/ppermute | solution.py:243
  55.8 2.6 %collective-permute-done.10 = f32[128,128]{1,0:T(8,128)S(1)} collective-permute-done((f32[128,128]{1,0:T(8,128)S(1)}, f32[128,128]{1,0:T(8,128)S(1)}, u32[]{:S(2)}, u32[]{:S(2)}) %collective-permute-start.10) | collective-permute-done | bytes 65568 | tf_op jit(solution)/shard_map/ppermute | solution.py:243
  58.4 0.6 add_bitcast_fusion
  59.0 13.8 %all-to-all-start.2 = ((f32[16,8,128]{2,1,0:T(8,128)}), f32[16,8,128]{2,1,0:T(8,128)S(1)}, u32[]{:S(2)}, u32[]{:S(2)}) async-start(f32[16,8,128]{2,1,0:T(8,128)} %add_bitcast_fusion), calls=%async_computation.2 | async-start | bytes 131072 | tf_op jit(solution)/shard_map/all_to_all | solution.py:566
  72.8 0.1 norm_back.1
  73.0 2.8 %tap_grad.1 = (f32[16,128]{1,0:T(8,128)S(1)}, f32[16,128]{1,0:T(8,128)S(1)}) custom-call(bf16[3,64,128]{2,1,0:T(8,128)(2,1)S(1)} %collective-permute-done.up, bf16[4,64,128]{2,1,0:T(8,128)(2,1)S(1)} %bitcast.21, bf16[3,64,128]{2,1,0:T(8,128)(2,1)S(1)} %collective-permute-done.1.down, bf16[64,128]{1,0:T(8,128)(2,1)S(1)} %collective-permute-done.2.left, ...), custom_call_target="tpu_custom_call" | custom-call | tf_op jit(solution)/shard_map/tap_grad/pallas_call | solution.py:28
  75.8 3.9 %collective-permute-start.11 = (f32[16,128]{1,0:T(8,128)S(1)}, f32[16,128]{1,0:T(8,128)S(1)}, u32[]{:S(2)}, u32[]{:S(2)}) collective-permute-start(f32[16,128]{1,0:T(8,128)S(1)} %get-tuple-element.59), channel_id=1, source_target_pairs={{0,64},{64,0},{128,192},{192,128},{256,320},{320,256},{384,448},{4... | collective-permute-start | bytes 24584 | tf_op jit(solution)/shard_map/ppermute | solution.py:243
  79.7 0.8 collective-permute-done.11.recv
  80.5 2.0 %collective-permute-start.12 = (f32[8,128]{1,0:T(8,128)S(1)}, f32[8,128]{1,0:T(8,128)S(1)}, u32[]{:S(2)}, u32[]{:S(2)}) collective-permute-start(f32[8,128]{1,0:T(8,128)S(1)} %get-tuple-element.61), channel_id=1, source_target_pairs={{0,128},{64,192},{128,0},{192,64},{256,384},{320,448},{384,256},{4... | collective-permute-start | bytes 12296 | tf_op jit(solution)/shard_map/ppermute | solution.py:243
  82.5 2.6 %collective-permute-done.12.recv = f32[8,128]{1,0:T(8,128)S(1)} collective-permute-done((f32[8,128]{1,0:T(8,128)S(1)}, f32[8,128]{1,0:T(8,128)S(1)}, u32[]{:S(2)}, u32[]{:S(2)}) %collective-permute-start.12) | collective-permute-done | bytes 4128 | tf_op jit(solution)/shard_map/ppermute | solution.py:243
  85.1 4.8 %collective-permute-start.13 = (f32[4,128]{1,0:T(4,128)S(1)}, f32[4,128]{1,0:T(4,128)S(1)}, u32[]{:S(2)}, u32[]{:S(2)}) collective-permute-start(f32[4,128]{1,0:T(4,128)S(1)} %get-tuple-element.63), channel_id=1, source_target_pairs={{0,384},{64,448},{128,256},{192,320},{256,128},{320,192},{384,0},{... | collective-permute-start | bytes 6152 | tf_op jit(solution)/shard_map/ppermute | solution.py:243
  90.0 1.0 collective-permute-done.13.more
  91.0 22.8 %all_to_all.25.recv = bf16[16,16,128]{2,1,0:T(8,128)(2,1)S(1)} all-to-all(bf16[16,16,128]{2,1,0:T(8,128)(2,1)S(1)} %col_pack.1), channel_id=1, replica_groups=mesh['row'=8,'col'=16,'ch'=4] {'col'}, dimensions={0} | all-to-all | bytes 131072 | tf_op jit(solution)/shard_map/all_to_all | solution.py:566
  113.8 0.8 row_pack.1
  114.6 8.3 %all-to-all-start.4 = ((bf16[8,144,128]{2,1,0:T(8,128)(2,1)}), bf16[8,144,128]{2,1,0:T(8,128)(2,1)S(1)}, u32[]{:S(2)}, u32[]{:S(2)}) async-start(bf16[8,144,128]{2,1,0:T(8,128)(2,1)} %row_pack.1), calls=%async_computation.4 | async-start | bytes 589824 | tf_op jit(solution)/shard_map/all_to_all | solution.py:566
  122.9 1.9 %collective-permute-start.5 = (bf16[3,64,128]{2,1,0:T(8,128)(2,1)S(1)}, bf16[3,64,128]{2,1,0:T(8,128)(2,1)S(1)}, u32[]{:S(2)}, u32[]{:S(2)}) collective-permute-start(bf16[3,64,128]{2,1,0:T(8,128)(2,1)S(1)} %get-tuple-element.78), channel_id=1, source_target_pairs={{64,0},{128,64},{192,128},{256,192},{320,256},{384,320},{448,384},... | collective-permute-start | bytes 147464 | tf_op jit(solution)/shard_map/ppermute | solution.py:554
  124.9 3.6 %collective-permute-start.4 = (bf16[3,64,128]{2,1,0:T(8,128)(2,1)S(1)}, bf16[3,64,128]{2,1,0:T(8,128)(2,1)S(1)}, u32[]{:S(2)}, u32[]{:S(2)}) collective-permute-start(bf16[3,64,128]{2,1,0:T(8,128)(2,1)S(1)} %get-tuple-element.79), channel_id=1, source_target_pairs={{0,64},{64,128},{128,192},{192,256},{256,320},{320,384},{384,448},... | collective-permute-start | bytes 147464 | tf_op jit(solution)/shard_map/ppermute | solution.py:554
  128.5 0.9 collective-permute-done.5.down
  129.4 0.3 collective-permute-done.4.up
  129.7 0.4 edges.3
  130.0 2.6 %collective-permute-start.6 = (bf16[64,128]{1,0:T(8,128)(2,1)S(1)}, bf16[64,128]{1,0:T(8,128)(2,1)S(1)}, u32[]{:S(2)}, u32[]{:S(2)}) collective-permute-start(bf16[64,128]{1,0:T(8,128)(2,1)S(1)} %get-tuple-element.48), channel_id=1, source_target_pairs={{0,4},{4,8},{8,12},{12,16},{16,20},{20,24},{24,28},{28,32},{32,36}... | collective-permute-start | bytes 49160 | tf_op jit(solution)/shard_map/ppermute | solution.py:554
  132.7 1.3 collective-permute-start.7
  134.0 0.7 copy.20
  134.6 2.5 %collective-permute-done.7.right = bf16[64,128]{1,0:T(8,128)(2,1)S(1)} collective-permute-done((bf16[64,128]{1,0:T(8,128)(2,1)S(1)}, bf16[64,128]{1,0:T(8,128)(2,1)S(1)}, u32[]{:S(2)}, u32[]{:S(2)}) %collective-permute-start.7) | collective-permute-done | bytes 16416 | tf_op jit(solution)/shard_map/ppermute | solution.py:554
  137.1 1.7 %backward.1 = bf16[4,64,128]{2,1,0:T(8,128)(2,1)S(1)} custom-call(bf16[3,64,128]{2,1,0:T(8,128)(2,1)S(1)} %collective-permute-done.4.up, bf16[4,64,128]{2,1,0:T(8,128)(2,1)S(1)} %get-tuple-element.47.mid, bf16[3,64,128]{2,1,0:T(8,128)(2,1)S(1)} %collective-permute-done.5.down, bf16[64,128]{1,0:T(8,128)(2,1)S(1)} %collective-permute-done.6.left, ...), custom_call_target="tpu_custom_call" | custom-call | tf_op jit(solution)/shard_map/backward/pallas_call | solution.py:28
  138.8 0.7 copy.21
  139.5 1.0 final.1
  (24 shorter events, 0.2 us)
Async XLA Ops:
  1.5 10.7 %collective-permute-start.1 = (bf16[3,64,128]{2,1,0:T(8,128)(2,1)S(1)}, bf16[3,64,128]{2,1,0:T(8,128)(2,1)S(1)}, u32[]{:S(2)}, u32[]{:S(2)}) collective-permute-start(bf16[3,64,128]{2,1,0:T(8,128)(2,1)S(1)} %get-tuple-element.80), channel_id=1, source_target_pairs={{64,0},{128,64},{192,128},{256,192},{320,256},{384,320},{448,384},... | collective-permute-start | bytes 147464 | tf_op jit(solution)/shard_map/ppermute | solution.py:554
  10.3 6.1 %copy-start.5 = (f32[64,49]{0,1:T(8,128)S(1)}, f32[64,49]{0,1:T(8,128)}, u32[]{:S(2)}) copy-start(f32[64,49]{0,1:T(8,128)} %param.9) | copy-start | bytes 37636
  10.3 3.1 %collective-permute-start = (bf16[3,64,128]{2,1,0:T(8,128)(2,1)S(1)}, bf16[3,64,128]{2,1,0:T(8,128)(2,1)S(1)}, u32[]{:S(2)}, u32[]{:S(2)}) collective-permute-start(bf16[3,64,128]{2,1,0:T(8,128)(2,1)S(1)} %get-tuple-element.81), channel_id=1, source_target_pairs={{0,64},{64,128},{128,192},{192,256},{256,320},{320,384},{384,448},... | collective-permute-start | bytes 147464 | tf_op jit(solution)/shard_map/ppermute | solution.py:554
  13.4 3.1 %copy-start.4 = (bf16[64,4,128]{2,1,0:T(4,128)(2,1)S(1)}, bf16[64,4,128]{2,1,0:T(4,128)(2,1)}, u32[]{:S(2)}) copy-start(bf16[64,4,128]{2,1,0:T(4,128)(2,1)} %param.15) | copy-start | bytes 196612
  13.8 2.7 %collective-permute-start.2 = (bf16[64,128]{1,0:T(8,128)(2,1)S(1)}, bf16[64,128]{1,0:T(8,128)(2,1)S(1)}, u32[]{:S(2)}, u32[]{:S(2)}) collective-permute-start(bf16[64,128]{1,0:T(8,128)(2,1)S(1)} %get-tuple-element.39), channel_id=1, source_target_pairs={{0,4},{4,8},{8,12},{12,16},{16,20},{20,24},{24,28},{28,32},{32,36}... | collective-permute-start | bytes 49160 | tf_op jit(solution)/shard_map/ppermute | solution.py:554
  15.1 4.5 %collective-permute-start.3 = (bf16[64,128]{1,0:T(8,128)(2,1)S(1)}, bf16[64,128]{1,0:T(8,128)(2,1)S(1)}, u32[]{:S(2)}, u32[]{:S(2)}) collective-permute-start(bf16[64,128]{1,0:T(8,128)(2,1)S(1)} %get-tuple-element.40), channel_id=1, source_target_pairs={{4,0},{8,4},{12,8},{16,12},{20,16},{24,20},{28,24},{32,28},{36,32}... | collective-permute-start | bytes 49160 | tf_op jit(solution)/shard_map/ppermute | solution.py:554
  19.6 0.7 copy-start.2
  19.6 0.7 copy-start.3
  22.8 12.3 %copy-start = (bf16[256,256]{1,0:T(8,128)(2,1)S(1)}, bf16[256,256]{1,0:T(8,128)(2,1)}, u32[]{:S(2)}) copy-start(bf16[256,256]{1,0:T(8,128)(2,1)} %w_exp.1) | copy-start | bytes 393220
  22.8 12.3 %copy-start.1 = (bf16[256,256]{1,0:T(8,128)(2,1)S(1)}, bf16[256,256]{1,0:T(8,128)(2,1)}, u32[]{:S(2)}) copy-start(bf16[256,256]{1,0:T(8,128)(2,1)} %w_red.1) | copy-start | bytes 393220
  22.9 12.3 %all-to-all-start = ((bf16[4,144,512]{2,1,0:T(8,128)(2,1)}), bf16[4,144,512]{2,1,0:T(8,128)(2,1)S(1)}, u32[]{:S(2)}, u32[]{:S(2)}) async-start(bf16[4,144,512]{2,1,0:T(8,128)(2,1)} %get-tuple-element.41), calls=%async_computation | async-start | bytes 1179648 | tf_op jit(solution)/shard_map/all_to_all | solution.py:566
  37.3 7.9 %collective-permute-start.8 = (f32[512,128]{1,0:T(8,128)S(1)}, f32[512,128]{1,0:T(8,128)S(1)}, u32[]{:S(2)}, u32[]{:S(2)}) collective-permute-start(f32[512,128]{1,0:T(8,128)S(1)} %get-tuple-element.51), channel_id=1, source_target_pairs={{0,64},{64,0},{128,192},{192,128},{256,320},{320,256},{384,448},{4... | collective-permute-start | bytes 786440 | tf_op jit(solution)/shard_map/ppermute | solution.py:243
  41.6 17.4 %all-to-all-start.1 = ((bf16[4,144,512]{2,1,0:T(8,128)(2,1)}), bf16[4,144,512]{2,1,0:T(8,128)(2,1)S(1)}, u32[]{:S(2)}, u32[]{:S(2)}) async-start(bf16[4,144,512]{2,1,0:T(8,128)(2,1)} %get-tuple-element.42), calls=%async_computation.1 | async-start | bytes 1179648 | tf_op jit(solution)/shard_map/all_to_all | solution.py:566
  45.2 6.9 %collective-permute-start.9 = (f32[256,128]{1,0:T(8,128)S(1)}, f32[256,128]{1,0:T(8,128)S(1)}, u32[]{:S(2)}, u32[]{:S(2)}) collective-permute-start(f32[256,128]{1,0:T(8,128)S(1)} %get-tuple-element.53), channel_id=1, source_target_pairs={{0,128},{64,192},{128,0},{192,64},{256,384},{320,448},{384,256},{4... | collective-permute-start | bytes 393224 | tf_op jit(solution)/shard_map/ppermute | solution.py:243
  52.2 6.2 %collective-permute-start.10 = (f32[128,128]{1,0:T(8,128)S(1)}, f32[128,128]{1,0:T(8,128)S(1)}, u32[]{:S(2)}, u32[]{:S(2)}) collective-permute-start(f32[128,128]{1,0:T(8,128)S(1)} %get-tuple-element.55), channel_id=1, source_target_pairs={{0,384},{64,448},{128,256},{192,320},{256,128},{320,192},{384,0},{... | collective-permute-start | bytes 196616 | tf_op jit(solution)/shard_map/ppermute | solution.py:243
  59.0 31.9 %all-to-all-start.2 = ((f32[16,8,128]{2,1,0:T(8,128)}), f32[16,8,128]{2,1,0:T(8,128)S(1)}, u32[]{:S(2)}, u32[]{:S(2)}) async-start(f32[16,8,128]{2,1,0:T(8,128)} %add_bitcast_fusion), calls=%async_computation.2 | async-start | bytes 131072 | tf_op jit(solution)/shard_map/all_to_all | solution.py:566
  75.8 4.7 %collective-permute-start.11 = (f32[16,128]{1,0:T(8,128)S(1)}, f32[16,128]{1,0:T(8,128)S(1)}, u32[]{:S(2)}, u32[]{:S(2)}) collective-permute-start(f32[16,128]{1,0:T(8,128)S(1)} %get-tuple-element.59), channel_id=1, source_target_pairs={{0,64},{64,0},{128,192},{192,128},{256,320},{320,256},{384,448},{4... | collective-permute-start | bytes 24584 | tf_op jit(solution)/shard_map/ppermute | solution.py:243
  80.5 4.6 %collective-permute-start.12 = (f32[8,128]{1,0:T(8,128)S(1)}, f32[8,128]{1,0:T(8,128)S(1)}, u32[]{:S(2)}, u32[]{:S(2)}) collective-permute-start(f32[8,128]{1,0:T(8,128)S(1)} %get-tuple-element.61), channel_id=1, source_target_pairs={{0,128},{64,192},{128,0},{192,64},{256,384},{320,448},{384,256},{4... | collective-permute-start | bytes 12296 | tf_op jit(solution)/shard_map/ppermute | solution.py:243
  85.1 5.8 %collective-permute-start.13 = (f32[4,128]{1,0:T(4,128)S(1)}, f32[4,128]{1,0:T(4,128)S(1)}, u32[]{:S(2)}, u32[]{:S(2)}) collective-permute-start(f32[4,128]{1,0:T(4,128)S(1)} %get-tuple-element.63), channel_id=1, source_target_pairs={{0,384},{64,448},{128,256},{192,320},{256,128},{320,192},{384,0},{... | collective-permute-start | bytes 6152 | tf_op jit(solution)/shard_map/ppermute | solution.py:243
  114.6 24.9 %all-to-all-start.4 = ((bf16[8,144,128]{2,1,0:T(8,128)(2,1)}), bf16[8,144,128]{2,1,0:T(8,128)(2,1)S(1)}, u32[]{:S(2)}, u32[]{:S(2)}) async-start(bf16[8,144,128]{2,1,0:T(8,128)(2,1)} %row_pack.1), calls=%async_computation.4 | async-start | bytes 589824 | tf_op jit(solution)/shard_map/all_to_all | solution.py:566
  122.9 6.5 %collective-permute-start.5 = (bf16[3,64,128]{2,1,0:T(8,128)(2,1)S(1)}, bf16[3,64,128]{2,1,0:T(8,128)(2,1)S(1)}, u32[]{:S(2)}, u32[]{:S(2)}) collective-permute-start(bf16[3,64,128]{2,1,0:T(8,128)(2,1)S(1)} %get-tuple-element.78), channel_id=1, source_target_pairs={{64,0},{128,64},{192,128},{256,192},{320,256},{384,320},{448,384},... | collective-permute-start | bytes 147464 | tf_op jit(solution)/shard_map/ppermute | solution.py:554
  124.9 4.8 %collective-permute-start.4 = (bf16[3,64,128]{2,1,0:T(8,128)(2,1)S(1)}, bf16[3,64,128]{2,1,0:T(8,128)(2,1)S(1)}, u32[]{:S(2)}, u32[]{:S(2)}) collective-permute-start(bf16[3,64,128]{2,1,0:T(8,128)(2,1)S(1)} %get-tuple-element.79), channel_id=1, source_target_pairs={{0,64},{64,128},{128,192},{192,256},{256,320},{320,384},{384,448},... | collective-permute-start | bytes 147464 | tf_op jit(solution)/shard_map/ppermute | solution.py:554
  130.0 4.6 %collective-permute-start.6 = (bf16[64,128]{1,0:T(8,128)(2,1)S(1)}, bf16[64,128]{1,0:T(8,128)(2,1)S(1)}, u32[]{:S(2)}, u32[]{:S(2)}) collective-permute-start(bf16[64,128]{1,0:T(8,128)(2,1)S(1)} %get-tuple-element.48), channel_id=1, source_target_pairs={{0,4},{4,8},{8,12},{12,16},{16,20},{20,24},{24,28},{28,32},{32,36}... | collective-permute-start | bytes 49160 | tf_op jit(solution)/shard_map/ppermute | solution.py:554
  132.7 4.5 %collective-permute-start.7 = (bf16[64,128]{1,0:T(8,128)(2,1)S(1)}, bf16[64,128]{1,0:T(8,128)(2,1)S(1)}, u32[]{:S(2)}, u32[]{:S(2)}) collective-permute-start(bf16[64,128]{1,0:T(8,128)(2,1)S(1)} %get-tuple-element.49), channel_id=1, source_target_pairs={{4,0},{8,4},{12,8},{16,12},{20,16},{24,20},{28,24},{32,28},{36,32}... | collective-permute-start | bytes 49160 | tf_op jit(solution)/shard_map/ppermute | solution.py:554

commit v4 on v3

--- a/solution.py
+++ b/solution.py
@@ -391,7 +391,7 @@
     )(recv, mixed, stats, gain, image, off)
 
 
-def tap_grad_kernel(up, mid, down, left, right, grad_mixed, small, send, keep, table_ref, total):
+def tap_grad_kernel(up, mid, down, left, right, grad_mixed, small, keep, recv, out, table_ref, total):
     tile_rows, channels, _ = mid.shape
     lane = lane_ids(CT)
 
@@ -414,18 +414,26 @@
     lax.fori_loop(0, channels // CT, step, 0)
     half = channels // 2
     total[...] = table_ref[0:half, :] + rolled(table_ref[half:channels, :], LANES // 2)
-    halves(total, 0, send, keep)
-
-
-def tap_grad(up, mid, down, left, right, grad_mixed, small):
+    cols, height, _ = out.shape
+    part = keep.shape[0] // cols
+    per = total.shape[0] // cols
+    for c in range(cols):
+        at = slice(c * part, (c + 1) * part)
+        out[c, 0:part, :] = keep[at, :] + recv[at, :]
+        out[c, part : part + per, :] = total[c * per : (c + 1) * per, :]
+        out[c, part + per :, :] = jnp.zeros((height - part - per, LANES), f32)
+
+
+def tap_grad(up, mid, down, left, right, grad_mixed, small, keep, recv, cols):
     channels = mid.shape[1]
-    shape = jax.ShapeDtypeStruct((channels // 4, LANES), f32)
+    part, per = keep.shape[0] // cols, channels // 2 // cols
+    height = part + -(-2 * per // 8) * 8
     return vcall(
         tap_grad_kernel,
-        out_shape=(shape, shape),
+        out_shape=jax.ShapeDtypeStruct((cols, height, LANES), f32),
         scratch_shapes=[pltpu.VMEM((channels, LANES), f32), pltpu.VMEM((channels // 2, LANES), f32)],
         name="tap_grad",
-    )(up, mid, down, left, right, grad_mixed, small)
+    )(up, mid, down, left, right, grad_mixed, small, keep, recv)
 
 
 def backward_kernel(up, mid, down, left, right, kern, cot, out):
@@ -455,62 +463,64 @@
     return jnp.concatenate([hi, x - hi], axis=0)
 
 
-def col_pack_kernel(big, small, more, out):
-    total = big[0]
-    for c in range(1, big.shape[0]):
-        total = total + big[c]
-    tail = small[...] + more[...]
-    tile = jnp.concatenate([total, hi_lo(tail)], axis=0).astype(bf16)
+def col_pack_kernel(per, recv, out):
+    total = recv[0]
+    for c in range(1, recv.shape[0]):
+        total = total + recv[c]
+    part = total.shape[0] - -(-2 * per // 8) * 8
+    tail = hi_lo(total[part : part + per])
+    pad = total.shape[0] - part - 2 * per
+    pieces = [total[0:part], tail] + ([jnp.zeros((pad, LANES), f32)] if pad else [])
+    tile = jnp.concatenate(pieces, axis=0).astype(bf16)
     for c in range(out.shape[0]):
         out[c] = tile
 
 
-def col_pack(big, small, more):
-    cols, part, _ = big.shape
-    shape = (cols, part + 2 * small.shape[0], LANES)
-    return vcall(col_pack_kernel, out_shape=jax.ShapeDtypeStruct(shape, bf16), name="col_pack")(
-        big, small, more
-    )
-
-
-def row_pack_kernel(per, recv, out):
+def col_pack(recv, per):
+    return vcall(
+        functools.partial(col_pack_kernel, per),
+        out_shape=jax.ShapeDtypeStruct(recv.shape, bf16),
+        name="col_pack",
+    )(recv)
+
+
+def row_pack_kernel(per, recv, out, tile):
     cols, height, _ = recv.shape
-    part = height - 2 * per
-    x = recv[...].astype(f32)
-    big = x[:, 0:part, :].reshape(cols * part, LANES)
-    tail = x[0, part:, :]
-    for c in range(1, cols):
-        tail = tail + x[c, part:, :]
-    extra = hi_lo(tail[0:per] + tail[per:])
-    pad = jnp.zeros((CT - 2 * per % CT, LANES), f32) if 2 * per % CT else None
-    pieces = [big, extra] if pad is None else [big, extra, pad]
-    tile = jnp.concatenate(pieces, axis=0).astype(bf16)
+    part = height - -(-2 * per // 8) * 8
+    base, size = cols * part, cols * per
+    for c in range(cols):
+        x = recv[c].astype(f32)
+        tile[c * part : (c + 1) * part, :] = x[0:part]
+        tile[base + c * per : base + (c + 1) * per, :] = x[part : part + per]
+        low = base + size + c * per
+        tile[low : low + per, :] = x[part + per : part + 2 * per]
+    x = tile[...].astype(bf16)
     for r in range(out.shape[0]):
-        out[r] = tile
+        out[r] = x
 
 
 def row_pack(recv, rows, per):
     cols, height, _ = recv.shape
-    tall = cols * (height - 2 * per) + -(-2 * per // CT) * CT
+    tall = cols * (height - -(-2 * per // 8) * 8 + 2 * per)
     return vcall(
         functools.partial(row_pack_kernel, per),
         out_shape=jax.ShapeDtypeStruct((rows, tall, LANES), bf16),
+        scratch_shapes=[pltpu.VMEM((tall, LANES), f32)],
         name="row_pack",
     )(recv)
 
 
-def final_kernel(scale, flat, exp_ref, red_ref, taps_ref, gain_ref, shift_ref, off_ref, small):
+def final_kernel(scale, flat, exp_ref, red_ref, taps_ref, gain_ref, shift_ref, off_ref):
     rows = flat.shape[0]
     n = exp_ref.shape[0]
-    per = small.shape[0] // rows
+    per = taps_ref.shape[1] // 2
     size_all = 4 * n // rows
     for r in range(rows):
         x = flat[r].astype(f32) * scale
         block = x[0:size_all]
         tail = x[size_all : size_all + per] + x[size_all + per : size_all + 2 * per]
-        chunk = row_chunk(r, rows)
-        small[chunk * per : (chunk + 1) * per, :] = tail
-        start = chunk * size_all
+        total = tail if r == 0 else total + tail
+        start = row_chunk(r, rows) * size_all
         lo = 0
         while lo < size_all:
             which, at = divmod(start + lo, n)
@@ -519,7 +529,7 @@
             lane = (which % 2) * LANES
             ref[at : at + size, lane : lane + LANES] = block[lo : lo + size]
             lo += size
-    x = small[...]
+    x = total
     both = jnp.concatenate([x, rolled(x, LANES // 2)], axis=0)
     wide = jnp.concatenate([both, jnp.zeros((LANES - both.shape[0], LANES), f32)], axis=0)
     flip = jnp.transpose(wide)[:, 0 : both.shape[0]]
@@ -542,7 +552,6 @@
             jax.ShapeDtypeStruct((1, channels), f32),
             jax.ShapeDtypeStruct((1, hid), f32),
         ),
-        scratch_shapes=[pltpu.VMEM((channels // 2, LANES), f32)],
         name="final",
     )(flat)
 
@@ -566,17 +575,10 @@
     return lax.all_to_all(x, axis, 0, 0)
 
 
-def reduce_big(send, keep):
-    cols = lax.axis_size("col")
-    keep, recv = reduce_rows(send, keep)
-    part = keep + recv
-    return exchange(part.reshape(cols, part.shape[0] // cols, LANES), "col")
-
-
-def reduce_rest(big, send, keep):
-    keep, recv = reduce_rows(send, keep)
-    flat = exchange(col_pack(big, keep, recv), "col")
-    return exchange(row_pack(flat, lax.axis_size("row"), keep.shape[0]), "row")
+def reduce_cols(part, per):
+    part = exchange(part, "col")
+    flat = exchange(col_pack(part, per), "col")
+    return exchange(row_pack(flat, lax.axis_size("row"), per), "row")
 
 
 def body(
@@ -597,12 +599,13 @@
     recv = exchange(send, "ch")
     send, stats, give, keep, off = mlp(recv, expand_weight, bias, reduce_weight)
     recv = exchange(send, "ch")
-    big = reduce_big(give, keep)
+    keep, part = reduce_rows(give, keep)
     result, grad_mixed, rounded, small = norm_back(recv, mixed, stats, gain, img, off)
     g_up, g_down, g_left, g_right = halo(rounded)
-    give, keep = tap_grad(up, img, down, left, right, grad_mixed, small)
+    cols = lax.axis_size("col")
+    part = tap_grad(up, img, down, left, right, grad_mixed, small, keep, part, cols)
     grad_image = backward(g_up, rounded, g_down, g_left, g_right, depth_kernel, cot)
-    flat = reduce_rest(big, give, keep)
+    flat = reduce_cols(part, channels // 2 // cols)
     pixels_all = pixels * lax.axis_size("row") * lax.axis_size("col")
     scale = float(pixels_all) ** (-0.5)
     grad_exp, grad_red, grad_taps, grad_gain, grad_shift, grad_off = final(

time: 143 us -> 134 us (0.937)
  starting transfers between devices: 73.4 us -> 48.8 us
  blocking collectives: 22.8 us -> 41.7 us
    all_to_all x1 -> x2, blocking collectives: 22.8 us -> 41.7 us  [exchange(): return lax.all_to_all(x, axis, 0, 0)]
    all_to_all x4 -> x3, starting transfers between devices: 29.2 us -> 16 us  [exchange(): return lax.all_to_all(x, axis, 0, 0)]
    ppermute x6 -> x3, starting transfers between devices: 21.5 us -> 9.55 us  [reduce_rows(): recv = lax.ppermute(send, 'row', [(i, i ^ mask) for i in range(size)])]
    ppermute x6 -> x3, waiting for transfers between devices: 11.2 us -> 5.85 us  [reduce_rows(): recv = lax.ppermute(send, 'row', [(i, i ^ mask) for i in range(size)])]
    ppermute x8, waiting for transfers between devices: 7.9 us -> 10.1 us  [neighbours(): return (lax.ppermute(last, axis, up), lax.ppermute(first, axis, down))]
    all_to_all x4 -> x3, waiting for transfers between devices: 7.88 us -> 9.72 us  [exchange(): return lax.all_to_all(x, axis, 0, 0)]
    pallas_call x14 -> x12, Pallas kernels: 12 us -> 12 us  [call(): pl.pallas_call(kernel, out_shape=out_shape, in_specs=[spec] * len(args),...]
  transfers between devices with their start and end apart: 18 -> 14, of which waited for: 11 -> 7; matrix products, arithmetic and copies ran while one was open for 2% -> 2% of each run, Pallas kernels for 4% -> 2%
where the time goes in v4:
time: 134 us; the launch traced here: 133 us
  starting transfers between devices  48.8 us (36%)
  blocking collectives  41.7 us (31%)
  waiting for transfers between devices  25.7 us (19%)
  Pallas kernels  12 us (9%)
  local copies, waits for them, and re-layouts  3.79 us (3%)
    all_to_all x2, blocking collectives, exchange(): return lax.all_to_all(x, axis, 0, 0)  41.7 us
    ppermute x8, starting transfers between devices, neighbours(): return (lax.ppermute(last, axis, up), lax.ppermute(first, axis, down))  23.3 us
    all_to_all x3, starting transfers between devices, exchange(): return lax.all_to_all(x, axis, 0, 0)  16 us
    pallas_call x12, Pallas kernels, call(): pl.pallas_call(kernel, out_shape=out_shape, in_specs=[spec] * len(args),...  12 us
    ppermute x8, waiting for transfers between devices, neighbours(): return (lax.ppermute(last, axis, up), lax.ppermute(first, axis, down))  10.1 us
    all_to_all x3, waiting for transfers between devices, exchange(): return lax.all_to_all(x, axis, 0, 0)  9.72 us
    ppermute x3, starting transfers between devices, reduce_rows(): recv = lax.ppermute(send, 'row', [(i, i ^ mask) for i in range(size)])  9.55 us
    ppermute x3, waiting for transfers between devices, reduce_rows(): recv = lax.ppermute(send, 'row', [(i, i ^ mask) for i in range(size)])  5.85 us
  transfers between devices with their start and end apart: 14, of which 7 were waited for; matrix products, arithmetic and copies ran while one was open for 2% of the time, Pallas kernels for 2%

profile of v4, /device:TPU:1, one launch (start us, length us, event | category | flops | bytes accessed | tf_op | source)
XLA Modules:
  0.0 132.8 jit_solution(10114676142703180856)
XLA Ops:
  0.6 0.9 copy.25
  1.5 4.6 %collective-permute-start = (bf16[3,64,128]{2,1,0:T(8,128)(2,1)S(1)}, bf16[3,64,128]{2,1,0:T(8,128)(2,1)S(1)}, u32[]{:S(2)}, u32[]{:S(2)}) collective-permute-start(bf16[3,64,128]{2,1,0:T(8,128)(2,1)S(1)} %get-tuple-element.69), channel_id=1, source_target_pairs={{0,64},{64,128},{128,192},{192,256},{256,320},{320,384},{384,448},... | collective-permute-start | bytes 147464 | tf_op jit(solution)/shard_map/ppermute | solution.py:563
  6.1 0.0 copy-start.4
  6.1 5.6 %collective-permute-start.1 = (bf16[3,64,128]{2,1,0:T(8,128)(2,1)S(1)}, bf16[3,64,128]{2,1,0:T(8,128)(2,1)S(1)}, u32[]{:S(2)}, u32[]{:S(2)}) collective-permute-start(bf16[3,64,128]{2,1,0:T(8,128)(2,1)S(1)} %get-tuple-element.68), channel_id=1, source_target_pairs={{64,0},{128,64},{192,128},{256,192},{320,256},{384,320},{448,384},... | collective-permute-start | bytes 147464 | tf_op jit(solution)/shard_map/ppermute | solution.py:563
  11.7 0.0 collective-permute-done.up
  11.7 0.8 collective-permute-done.1.down
  12.6 0.4 edges.2
  12.9 2.6 %collective-permute-start.2 = (bf16[64,128]{1,0:T(8,128)(2,1)S(1)}, bf16[64,128]{1,0:T(8,128)(2,1)S(1)}, u32[]{:S(2)}, u32[]{:S(2)}) collective-permute-start(bf16[64,128]{1,0:T(8,128)(2,1)S(1)} %get-tuple-element.33), channel_id=1, source_target_pairs={{0,4},{4,8},{8,12},{12,16},{16,20},{20,24},{24,28},{28,32},{32,36}... | collective-permute-start | bytes 49160 | tf_op jit(solution)/shard_map/ppermute | solution.py:563
  15.6 0.0 copy-start.5
  15.6 1.3 collective-permute-start.3
  16.9 0.1 copy.18.kern
  17.0 0.0 collective-permute-done.2.left
  17.0 3.2 %collective-permute-done.3.right = bf16[64,128]{1,0:T(8,128)(2,1)S(1)} collective-permute-done((bf16[64,128]{1,0:T(8,128)(2,1)S(1)}, bf16[64,128]{1,0:T(8,128)(2,1)S(1)}, u32[]{:S(2)}, u32[]{:S(2)}) %collective-permute-start.3) | collective-permute-done | bytes 16416 | tf_op jit(solution)/shard_map/ppermute | solution.py:563
  20.3 0.7 copy-done.2
  20.9 0.0 copy-done.3
  20.9 2.6 %forward.1 = (f32[64,512]{1,0:T(8,128)S(1)}, bf16[4,144,512]{2,1,0:T(8,128)(2,1)}) custom-call(bf16[3,64,128]{2,1,0:T(8,128)(2,1)S(1)} %collective-permute-done.up, bf16[4,64,128]{2,1,0:T(8,128)(2,1)S(1)} %bitcast.17, bf16[3,64,128]{2,1,0:T(8,128)(2,1)S(1)} %collective-permute-done.1.down, bf16[64,128]{1,0:T(8,128)(2,1)S(1)} %collective-permute-done.2.left, ...), custom_call_target="tpu_custom_call" | custom-call | tf_op jit(solution)/shard_map/forward/pallas_call | solution.py:28
  23.5 4.1 %all-to-all-start = ((bf16[4,144,512]{2,1,0:T(8,128)(2,1)}), bf16[4,144,512]{2,1,0:T(8,128)(2,1)S(1)}, u32[]{:S(2)}, u32[]{:S(2)}) async-start(bf16[4,144,512]{2,1,0:T(8,128)(2,1)} %get-tuple-element.35), calls=%async_computation | async-start | bytes 1179648 | tf_op jit(solution)/shard_map/all_to_all | solution.py:575
  27.7 0.8 dynamic_slice.3
  28.4 9.7 %all-to-all-done.recv = bf16[4,144,512]{2,1,0:T(8,128)(2,1)S(1)} async-done(((bf16[4,144,512]{2,1,0:T(8,128)(2,1)}), bf16[4,144,512]{2,1,0:T(8,128)(2,1)S(1)}, u32[]{:S(2)}, u32[]{:S(2)}) %all-to-all-start) | async-done | bytes 589856 | tf_op jit(solution)/shard_map/all_to_all | solution.py:575
  38.2 2.1 %mlp.1 = (bf16[4,144,512]{2,1,0:T(8,128)(2,1)}, f32[2,512]{1,0:T(2,128)S(1)}, f32[512,128]{1,0:T(8,128)S(1)}, f32[512,128]{1,0:T(8,128)S(1)}, f32[64,128]{1,0:T(8,128)S(1)}) custom-call(bf16[4,144,512]{2,1,0:T(8,128)(2,1)S(1)} %all-to-all-done.recv, bf16[256,256]{1,0:T(8,128)(2,1)S(1)} %copy-done, f32[1,256]{1,0:T(1,128)S(1)} %bitcast.24, ...), custom_call_target="tpu_custom_call" | custom-call | tf_op jit(solution)/shard_map/mlp/pallas_call | solution.py:28
  40.3 2.3 %collective-permute-start.8 = (f32[512,128]{1,0:T(8,128)S(1)}, f32[512,128]{1,0:T(8,128)S(1)}, u32[]{:S(2)}, u32[]{:S(2)}) collective-permute-start(f32[512,128]{1,0:T(8,128)S(1)} %get-tuple-element.47), channel_id=1, source_target_pairs={{0,64},{64,0},{128,192},{192,128},{256,320},{320,256},{384,448},{4... | collective-permute-start | bytes 786440 | tf_op jit(solution)/shard_map/ppermute | solution.py:243
  42.6 3.5 %all-to-all-start.1 = ((bf16[4,144,512]{2,1,0:T(8,128)(2,1)}), bf16[4,144,512]{2,1,0:T(8,128)(2,1)S(1)}, u32[]{:S(2)}, u32[]{:S(2)}) async-start(bf16[4,144,512]{2,1,0:T(8,128)(2,1)} %get-tuple-element.36), calls=%async_computation.1 | async-start | bytes 1179648 | tf_op jit(solution)/shard_map/all_to_all | solution.py:575
  46.1 0.0 collective-permute-done.8.recv
  46.2 3.5 %collective-permute-start.9 = (f32[256,128]{1,0:T(8,128)S(1)}, f32[256,128]{1,0:T(8,128)S(1)}, u32[]{:S(2)}, u32[]{:S(2)}) collective-permute-start(f32[256,128]{1,0:T(8,128)S(1)} %get-tuple-element.49), channel_id=1, source_target_pairs={{0,128},{64,192},{128,0},{192,64},{256,384},{320,448},{384,256},{4... | collective-permute-start | bytes 393224 | tf_op jit(solution)/shard_map/ppermute | solution.py:243
  49.7 3.6 %collective-permute-done.9.recv = f32[256,128]{1,0:T(8,128)S(1)} collective-permute-done((f32[256,128]{1,0:T(8,128)S(1)}, f32[256,128]{1,0:T(8,128)S(1)}, u32[]{:S(2)}, u32[]{:S(2)}) %collective-permute-start.9) | collective-permute-done | bytes 131104 | tf_op jit(solution)/shard_map/ppermute | solution.py:243
  53.3 3.8 %collective-permute-start.10 = (f32[128,128]{1,0:T(8,128)S(1)}, f32[128,128]{1,0:T(8,128)S(1)}, u32[]{:S(2)}, u32[]{:S(2)}) collective-permute-start(f32[128,128]{1,0:T(8,128)S(1)} %get-tuple-element.51), channel_id=1, source_target_pairs={{0,384},{64,448},{128,256},{192,320},{256,128},{320,192},{384,0},{... | collective-permute-start | bytes 196616 | tf_op jit(solution)/shard_map/ppermute | solution.py:243
  57.1 0.0 all-to-all-done.1.recv
  57.1 0.1 norm_back.1
  57.2 2.3 %collective-permute-done.10.recv = f32[128,128]{1,0:T(8,128)S(1)} collective-permute-done((f32[128,128]{1,0:T(8,128)S(1)}, f32[128,128]{1,0:T(8,128)S(1)}, u32[]{:S(2)}, u32[]{:S(2)}) %collective-permute-start.10) | collective-permute-done | bytes 65568 | tf_op jit(solution)/shard_map/ppermute | solution.py:243
  59.5 2.8 %tap_grad.1 = f32[16,16,128]{2,1,0:T(8,128)S(1)} custom-call(bf16[3,64,128]{2,1,0:T(8,128)(2,1)S(1)} %collective-permute-done.up, bf16[4,64,128]{2,1,0:T(8,128)(2,1)S(1)} %bitcast.19, bf16[3,64,128]{2,1,0:T(8,128)(2,1)S(1)} %collective-permute-done.1.down, bf16[64,128]{1,0:T(8,128)(2,1)S(1)} %collective-permute-done.2.left, ...), custom_call_target="tpu_custom_call" | custom-call | tf_op jit(solution)/shard_map/tap_grad/pallas_call | solution.py:28
  62.3 26.3 %all_to_all.25.recv = f32[16,16,128]{2,1,0:T(8,128)S(1)} all-to-all(f32[16,16,128]{2,1,0:T(8,128)S(1)} %tap_grad.1), channel_id=1, replica_groups=mesh['row'=8,'col'=16,'ch'=4] {'col'}, dimensions={0} | all-to-all | bytes 262144 | tf_op jit(solution)/shard_map/all_to_all | solution.py:575
  88.6 15.4 %all_to_all.26.recv = bf16[16,16,128]{2,1,0:T(8,128)(2,1)S(1)} all-to-all(bf16[16,16,128]{2,1,0:T(8,128)(2,1)S(1)} %col_pack.1), channel_id=1, replica_groups=mesh['row'=8,'col'=16,'ch'=4] {'col'}, dimensions={0} | all-to-all | bytes 131072 | tf_op jit(solution)/shard_map/all_to_all | solution.py:575
  104.0 0.8 row_pack.1
  104.8 8.3 %all-to-all-start.4 = ((bf16[8,192,128]{2,1,0:T(8,128)(2,1)}), bf16[8,192,128]{2,1,0:T(8,128)(2,1)S(1)}, u32[]{:S(2)}, u32[]{:S(2)}) async-start(bf16[8,192,128]{2,1,0:T(8,128)(2,1)} %row_pack.1), calls=%async_computation.4 | async-start | bytes 786432 | tf_op jit(solution)/shard_map/all_to_all | solution.py:575
  113.1 3.5 %collective-permute-start.4 = (bf16[3,64,128]{2,1,0:T(8,128)(2,1)S(1)}, bf16[3,64,128]{2,1,0:T(8,128)(2,1)S(1)}, u32[]{:S(2)}, u32[]{:S(2)}) collective-permute-start(bf16[3,64,128]{2,1,0:T(8,128)(2,1)S(1)} %get-tuple-element.67), channel_id=1, source_target_pairs={{0,64},{64,128},{128,192},{192,256},{256,320},{320,384},{384,448},... | collective-permute-start | bytes 147464 | tf_op jit(solution)/shard_map/ppermute | solution.py:563
  116.7 1.9 %collective-permute-start.5 = (bf16[3,64,128]{2,1,0:T(8,128)(2,1)S(1)}, bf16[3,64,128]{2,1,0:T(8,128)(2,1)S(1)}, u32[]{:S(2)}, u32[]{:S(2)}) collective-permute-start(bf16[3,64,128]{2,1,0:T(8,128)(2,1)S(1)} %get-tuple-element.66), channel_id=1, source_target_pairs={{64,0},{128,64},{192,128},{256,192},{320,256},{384,320},{448,384},... | collective-permute-start | bytes 147464 | tf_op jit(solution)/shard_map/ppermute | solution.py:563
  118.6 0.0 collective-permute-done.4.up
  118.6 3.5 %collective-permute-done.5.down = bf16[3,64,128]{2,1,0:T(8,128)(2,1)S(1)} collective-permute-done((bf16[3,64,128]{2,1,0:T(8,128)(2,1)S(1)}, bf16[3,64,128]{2,1,0:T(8,128)(2,1)S(1)}, u32[]{:S(2)}, u32[]{:S(2)}) %collective-permute-start.5) | collective-permute-done | bytes 49184 | tf_op jit(solution)/shard_map/ppermute | solution.py:563
  122.2 0.4 edges.3
  122.5 2.4 %collective-permute-start.6 = (bf16[64,128]{1,0:T(8,128)(2,1)S(1)}, bf16[64,128]{1,0:T(8,128)(2,1)S(1)}, u32[]{:S(2)}, u32[]{:S(2)}) collective-permute-start(bf16[64,128]{1,0:T(8,128)(2,1)S(1)} %get-tuple-element.42), channel_id=1, source_target_pairs={{0,4},{4,8},{8,12},{12,16},{16,20},{20,24},{24,28},{28,32},{32,36}... | collective-permute-start | bytes 49160 | tf_op jit(solution)/shard_map/ppermute | solution.py:563
  125.0 1.3 collective-permute-start.7
  126.3 0.7 copy.20
  127.0 0.0 collective-permute-done.6.left
  127.0 2.5 %collective-permute-done.7.right = bf16[64,128]{1,0:T(8,128)(2,1)S(1)} collective-permute-done((bf16[64,128]{1,0:T(8,128)(2,1)S(1)}, bf16[64,128]{1,0:T(8,128)(2,1)S(1)}, u32[]{:S(2)}, u32[]{:S(2)}) %collective-permute-start.7) | collective-permute-done | bytes 16416 | tf_op jit(solution)/shard_map/ppermute | solution.py:563
  129.5 1.7 %backward.1 = bf16[4,64,128]{2,1,0:T(8,128)(2,1)S(1)} custom-call(bf16[3,64,128]{2,1,0:T(8,128)(2,1)S(1)} %collective-permute-done.4.up, bf16[4,64,128]{2,1,0:T(8,128)(2,1)S(1)} %get-tuple-element.41.mid, bf16[3,64,128]{2,1,0:T(8,128)(2,1)S(1)} %collective-permute-done.5.down, bf16[64,128]{1,0:T(8,128)(2,1)S(1)} %collective-permute-done.6.left, ...), custom_call_target="tpu_custom_call" | custom-call | tf_op jit(solution)/shard_map/backward/pallas_call | solution.py:28
  131.2 0.7 copy.21
  131.8 0.0 all-to-all-done.4.flat
  131.8 1.0 final.1
  (14 shorter events, 0.2 us)
Async XLA Ops:
  1.5 10.2 %collective-permute-start = (bf16[3,64,128]{2,1,0:T(8,128)(2,1)S(1)}, bf16[3,64,128]{2,1,0:T(8,128)(2,1)S(1)}, u32[]{:S(2)}, u32[]{:S(2)}) collective-permute-start(bf16[3,64,128]{2,1,0:T(8,128)(2,1)S(1)} %get-tuple-element.69), channel_id=1, source_target_pairs={{0,64},{64,128},{128,192},{192,256},{256,320},{320,384},{384,448},... | collective-permute-start | bytes 147464 | tf_op jit(solution)/shard_map/ppermute | solution.py:563
  6.1 10.8 %copy-start.4 = (bf16[64,4,128]{2,1,0:T(4,128)(2,1)S(1)}, bf16[64,4,128]{2,1,0:T(4,128)(2,1)}, u32[]{:S(2)}) copy-start(bf16[64,4,128]{2,1,0:T(4,128)(2,1)} %param.15) | copy-start | bytes 196612
  6.1 6.5 %collective-permute-start.1 = (bf16[3,64,128]{2,1,0:T(8,128)(2,1)S(1)}, bf16[3,64,128]{2,1,0:T(8,128)(2,1)S(1)}, u32[]{:S(2)}, u32[]{:S(2)}) collective-permute-start(bf16[3,64,128]{2,1,0:T(8,128)(2,1)S(1)} %get-tuple-element.68), channel_id=1, source_target_pairs={{64,0},{128,64},{192,128},{256,192},{320,256},{384,320},{448,384},... | collective-permute-start | bytes 147464 | tf_op jit(solution)/shard_map/ppermute | solution.py:563
  12.9 4.1 %collective-permute-start.2 = (bf16[64,128]{1,0:T(8,128)(2,1)S(1)}, bf16[64,128]{1,0:T(8,128)(2,1)S(1)}, u32[]{:S(2)}, u32[]{:S(2)}) collective-permute-start(bf16[64,128]{1,0:T(8,128)(2,1)S(1)} %get-tuple-element.33), channel_id=1, source_target_pairs={{0,4},{4,8},{8,12},{12,16},{16,20},{20,24},{24,28},{28,32},{32,36}... | collective-permute-start | bytes 49160 | tf_op jit(solution)/shard_map/ppermute | solution.py:563
  15.6 1.3 %copy-start.5 = (f32[64,49]{0,1:T(8,128)S(1)}, f32[64,49]{0,1:T(8,128)}, u32[]{:S(2)}) copy-start(f32[64,49]{0,1:T(8,128)} %param.9) | copy-start | bytes 37636
  15.6 4.7 %collective-permute-start.3 = (bf16[64,128]{1,0:T(8,128)(2,1)S(1)}, bf16[64,128]{1,0:T(8,128)(2,1)S(1)}, u32[]{:S(2)}, u32[]{:S(2)}) collective-permute-start(bf16[64,128]{1,0:T(8,128)(2,1)S(1)} %get-tuple-element.34), channel_id=1, source_target_pairs={{4,0},{8,4},{12,8},{16,12},{20,16},{24,20},{28,24},{32,28},{36,32}... | collective-permute-start | bytes 49160 | tf_op jit(solution)/shard_map/ppermute | solution.py:563
  20.3 0.7 copy-start.2
  20.3 0.7 copy-start.3
  23.5 14.6 %copy-start = (bf16[256,256]{1,0:T(8,128)(2,1)S(1)}, bf16[256,256]{1,0:T(8,128)(2,1)}, u32[]{:S(2)}) copy-start(bf16[256,256]{1,0:T(8,128)(2,1)} %w_exp.1) | copy-start | bytes 393220
  23.5 14.6 %copy-start.1 = (bf16[256,256]{1,0:T(8,128)(2,1)S(1)}, bf16[256,256]{1,0:T(8,128)(2,1)}, u32[]{:S(2)}) copy-start(bf16[256,256]{1,0:T(8,128)(2,1)} %w_red.1) | copy-start | bytes 393220
  23.5 14.6 %all-to-all-start = ((bf16[4,144,512]{2,1,0:T(8,128)(2,1)}), bf16[4,144,512]{2,1,0:T(8,128)(2,1)S(1)}, u32[]{:S(2)}, u32[]{:S(2)}) async-start(bf16[4,144,512]{2,1,0:T(8,128)(2,1)} %get-tuple-element.35), calls=%async_computation | async-start | bytes 1179648 | tf_op jit(solution)/shard_map/all_to_all | solution.py:575
  40.3 5.8 %collective-permute-start.8 = (f32[512,128]{1,0:T(8,128)S(1)}, f32[512,128]{1,0:T(8,128)S(1)}, u32[]{:S(2)}, u32[]{:S(2)}) collective-permute-start(f32[512,128]{1,0:T(8,128)S(1)} %get-tuple-element.47), channel_id=1, source_target_pairs={{0,64},{64,0},{128,192},{192,128},{256,320},{320,256},{384,448},{4... | collective-permute-start | bytes 786440 | tf_op jit(solution)/shard_map/ppermute | solution.py:243
  42.6 14.4 %all-to-all-start.1 = ((bf16[4,144,512]{2,1,0:T(8,128)(2,1)}), bf16[4,144,512]{2,1,0:T(8,128)(2,1)S(1)}, u32[]{:S(2)}, u32[]{:S(2)}) async-start(bf16[4,144,512]{2,1,0:T(8,128)(2,1)} %get-tuple-element.36), calls=%async_computation.1 | async-start | bytes 1179648 | tf_op jit(solution)/shard_map/all_to_all | solution.py:575
  46.2 7.1 %collective-permute-start.9 = (f32[256,128]{1,0:T(8,128)S(1)}, f32[256,128]{1,0:T(8,128)S(1)}, u32[]{:S(2)}, u32[]{:S(2)}) collective-permute-start(f32[256,128]{1,0:T(8,128)S(1)} %get-tuple-element.49), channel_id=1, source_target_pairs={{0,128},{64,192},{128,0},{192,64},{256,384},{320,448},{384,256},{4... | collective-permute-start | bytes 393224 | tf_op jit(solution)/shard_map/ppermute | solution.py:243
  53.3 6.2 %collective-permute-start.10 = (f32[128,128]{1,0:T(8,128)S(1)}, f32[128,128]{1,0:T(8,128)S(1)}, u32[]{:S(2)}, u32[]{:S(2)}) collective-permute-start(f32[128,128]{1,0:T(8,128)S(1)} %get-tuple-element.51), channel_id=1, source_target_pairs={{0,384},{64,448},{128,256},{192,320},{256,128},{320,192},{384,0},{... | collective-permute-start | bytes 196616 | tf_op jit(solution)/shard_map/ppermute | solution.py:243
  104.8 27.1 %all-to-all-start.4 = ((bf16[8,192,128]{2,1,0:T(8,128)(2,1)}), bf16[8,192,128]{2,1,0:T(8,128)(2,1)S(1)}, u32[]{:S(2)}, u32[]{:S(2)}) async-start(bf16[8,192,128]{2,1,0:T(8,128)(2,1)} %row_pack.1), calls=%async_computation.4 | async-start | bytes 786432 | tf_op jit(solution)/shard_map/all_to_all | solution.py:575
  113.1 5.5 %collective-permute-start.4 = (bf16[3,64,128]{2,1,0:T(8,128)(2,1)S(1)}, bf16[3,64,128]{2,1,0:T(8,128)(2,1)S(1)}, u32[]{:S(2)}, u32[]{:S(2)}) collective-permute-start(bf16[3,64,128]{2,1,0:T(8,128)(2,1)S(1)} %get-tuple-element.67), channel_id=1, source_target_pairs={{0,64},{64,128},{128,192},{192,256},{256,320},{320,384},{384,448},... | collective-permute-start | bytes 147464 | tf_op jit(solution)/shard_map/ppermute | solution.py:563
  116.7 5.5 %collective-permute-start.5 = (bf16[3,64,128]{2,1,0:T(8,128)(2,1)S(1)}, bf16[3,64,128]{2,1,0:T(8,128)(2,1)S(1)}, u32[]{:S(2)}, u32[]{:S(2)}) collective-permute-start(bf16[3,64,128]{2,1,0:T(8,128)(2,1)S(1)} %get-tuple-element.66), channel_id=1, source_target_pairs={{64,0},{128,64},{192,128},{256,192},{320,256},{384,320},{448,384},... | collective-permute-start | bytes 147464 | tf_op jit(solution)/shard_map/ppermute | solution.py:563
  122.5 4.4 %collective-permute-start.6 = (bf16[64,128]{1,0:T(8,128)(2,1)S(1)}, bf16[64,128]{1,0:T(8,128)(2,1)S(1)}, u32[]{:S(2)}, u32[]{:S(2)}) collective-permute-start(bf16[64,128]{1,0:T(8,128)(2,1)S(1)} %get-tuple-element.42), channel_id=1, source_target_pairs={{0,4},{4,8},{8,12},{12,16},{16,20},{20,24},{24,28},{28,32},{32,36}... | collective-permute-start | bytes 49160 | tf_op jit(solution)/shard_map/ppermute | solution.py:563
  125.0 4.5 %collective-permute-start.7 = (bf16[64,128]{1,0:T(8,128)(2,1)S(1)}, bf16[64,128]{1,0:T(8,128)(2,1)S(1)}, u32[]{:S(2)}, u32[]{:S(2)}) collective-permute-start(bf16[64,128]{1,0:T(8,128)(2,1)S(1)} %get-tuple-element.43), channel_id=1, source_target_pairs={{4,0},{8,4},{12,8},{16,12},{20,16},{24,20},{28,24},{32,28},{36,32}... | collective-permute-start | bytes 49160 | tf_op jit(solution)/shard_map/ppermute | solution.py:563

commit v5 on v4

--- a/solution.py
+++ b/solution.py
@@ -92,7 +92,8 @@
     return jnp.where(mask, rolled(edge, -s), rolled(x, -s))
 
 
-def edges_kernel(up, mid, down, first, last):
+def edges_kernel(up, mid, down, gain, shift, first, last, both):
+    both[...] = jnp.concatenate([gain[...], shift[...]], axis=1)
     channels = mid.shape[1]
     lane = lane_ids(CT)
 
@@ -118,9 +119,14 @@
     lax.fori_loop(0, channels // CT, step, 0)
 
 
-def edges(up, mid, down):
-    shape = jax.ShapeDtypeStruct((mid.shape[1], LANES), bf16)
-    return vcall(edges_kernel, out_shape=(shape, shape), name="edges")(up, mid, down)
+def edges(up, mid, down, gain, shift):
+    channels = mid.shape[1]
+    shape = jax.ShapeDtypeStruct((channels, LANES), bf16)
+    return vcall(
+        edges_kernel,
+        out_shape=(shape, shape, jax.ShapeDtypeStruct((1, 2 * channels), f32)),
+        name="edges",
+    )(up, mid, down, gain, shift)
 
 
 def accumulate_taps(rows, kern, at, flip):
@@ -138,7 +144,7 @@
     return accum
 
 
-def forward_kernel(up, mid, down, left, right, kern, gain, shift, cot, mixed, payload):
+def forward_kernel(up, mid, down, left, right, kern, affine, cot, mixed, payload):
     tile_rows, channels, _ = mid.shape
 
     def step(t, carry):
@@ -160,8 +166,7 @@
         stats = jnp.concatenate(rows + [jnp.zeros((CT - 6, LANES), f32)], axis=0)
         if i == 0:
             row_id = lax.broadcasted_iota(jnp.int32, (CT, LANES), 0)
-            both = jnp.concatenate([gain[...], shift[...]], axis=1)
-            for k, part in enumerate(split3(both)):
+            for k, part in enumerate(split3(affine[...])):
                 stats = jnp.where(row_id == 6 + k, jnp.broadcast_to(part, (CT, LANES)), stats)
         dev = dev.astype(bf16)
         stats = stats.astype(bf16)
@@ -171,7 +176,7 @@
             payload[d, 2 * channels : 2 * channels + CT, cols] = stats
 
 
-def forward(up, mid, down, left, right, kern, gain, shift, cot, parts):
+def forward(up, mid, down, left, right, kern, affine, cot, parts):
     tile_rows, channels, _ = mid.shape
     pixels = tile_rows * LANES
     return vcall(
@@ -181,7 +186,7 @@
             jax.ShapeDtypeStruct((parts, 2 * channels + CT, pixels), bf16),
         ),
         name="forward",
-    )(up, mid, down, left, right, kern, gain, shift, cot)
+    )(up, mid, down, left, right, kern, affine, cot)
 
 
 def column(row, n):
@@ -194,56 +199,49 @@
     return lax.dot_general(a, b, (dims, ((), ())), preferred_element_type=f32)
 
 
-def row_masks(size):
-    return {8: (1, 2, 6), 4: (1, 2), 2: (1,)}[size]
-
-
-def row_bits(r, size):
-    if size == 8:
-        return (r % 2, (r // 2 + r // 4) % 2, r // 4)
-    return (r % 2, r // 2)[: size.bit_length() - 1]
-
-
 def row_chunk(r, size):
-    chunk = 0
-    for bit in row_bits(r, size):
-        chunk = 2 * chunk + bit
-    return chunk
-
-
-def row_bit(step):
-    return row_bits(lax.axis_index("row"), lax.axis_size("row"))[step]
-
-
-def halves(ref, step, send, keep):
+    return (r % 2) * (size // 2) + r // 2
+
+
+def halves(ref, send, keep):
     n = send.shape[0]
-    bit = row_bit(step)
+    bit = lax.axis_index("row") % 2
     send[...] = ref[pl.ds(pl.multiple_of((1 - bit) * n, n), n), :]
     keep[...] = ref[pl.ds(pl.multiple_of(bit * n, n), n), :]
 
 
-def halve_kernel(step, x, recv, send, keep, total):
+def spread_kernel(x, recv, *rest):
+    outs, total = rest[:-1], rest[-1]
     total[...] = x[...] + recv[...]
-    halves(total, step, send, keep)
-
-
-def halve(step, x, recv, name):
-    shape = jax.ShapeDtypeStruct((x.shape[0] // 2, LANES), f32)
-    return vcall(
-        functools.partial(halve_kernel, step),
-        out_shape=(shape, shape),
+    n = outs[0].shape[0]
+    y = lax.axis_index("row") // 2
+    for m, out in enumerate(outs):
+        low, high = y % 2, y // 2
+        low = 1 - low if m % 2 else low
+        high = 1 - high if m // 2 else high
+        out[...] = total[pl.ds(pl.multiple_of((2 * high + low) * n, n), n), :]
+
+
+def spread(x, recv, parts):
+    shape = jax.ShapeDtypeStruct((x.shape[0] // parts, LANES), f32)
+    return vcall(
+        spread_kernel,
+        out_shape=(shape,) * parts,
         scratch_shapes=[pltpu.VMEM(x.shape, f32)],
-        name=name,
+        name="spread",
     )(x, recv)
 
 
 def reduce_rows(send, keep):
     size = lax.axis_size("row")
-    for step, mask in enumerate(row_masks(size)):
-        recv = lax.ppermute(send, "row", [(i, i ^ mask) for i in range(size)])
-        if step + 1 < len(row_masks(size)):
-            send, keep = halve(step + 1, keep, recv, "halve")
-    return keep, recv
+    recv = lax.ppermute(send, "row", [(i, i ^ 1) for i in range(size)])
+    if size == 2:
+        return [keep, recv]
+    chunks = spread(keep, recv, size // 2)
+    return [chunks[0]] + [
+        lax.ppermute(chunks[m], "row", [(i, i ^ (2 * m)) for i in range(size)])
+        for m in range(1, size // 2)
+    ]
 
 
 def mlp_kernel(recv, w_exp, bias, w_red, payload, stats_out, send, keep, off, grads, s_norm, s_act, s_cot, s_gh):
@@ -311,7 +309,7 @@
     grads[n : 2 * n, :] = grad_exp[:, LANES:]
     grads[2 * n : 3 * n, :] = grad_red[:, 0:LANES]
     grads[3 * n : 4 * n, :] = grad_red[:, LANES:]
-    halves(grads, 0, send, keep)
+    halves(grads, send, keep)
     sums = dot(s_gh[...], jnp.ones((pixels, LANES), bf16), ((1,), (0,)))
     table = jnp.zeros((ch, LANES), f32)
     lane = lane_ids(ch)
@@ -391,7 +389,8 @@
     )(recv, mixed, stats, gain, image, off)
 
 
-def tap_grad_kernel(up, mid, down, left, right, grad_mixed, small, keep, recv, out, table_ref, total):
+def tap_grad_kernel(up, mid, down, left, right, grad_mixed, small, *rest):
+    pieces, (out, table_ref, total) = rest[:-3], rest[-3:]
     tile_rows, channels, _ = mid.shape
     lane = lane_ids(CT)
 
@@ -415,25 +414,25 @@
     half = channels // 2
     total[...] = table_ref[0:half, :] + rolled(table_ref[half:channels, :], LANES // 2)
     cols, height, _ = out.shape
-    part = keep.shape[0] // cols
+    part = pieces[0].shape[0] // cols
     per = total.shape[0] // cols
     for c in range(cols):
         at = slice(c * part, (c + 1) * part)
-        out[c, 0:part, :] = keep[at, :] + recv[at, :]
+        out[c, 0:part, :] = sum(x[at, :] for x in pieces)
         out[c, part : part + per, :] = total[c * per : (c + 1) * per, :]
         out[c, part + per :, :] = jnp.zeros((height - part - per, LANES), f32)
 
 
-def tap_grad(up, mid, down, left, right, grad_mixed, small, keep, recv, cols):
+def tap_grad(up, mid, down, left, right, grad_mixed, small, pieces, cols):
     channels = mid.shape[1]
-    part, per = keep.shape[0] // cols, channels // 2 // cols
+    part, per = pieces[0].shape[0] // cols, channels // 2 // cols
     height = part + -(-2 * per // 8) * 8
     return vcall(
         tap_grad_kernel,
         out_shape=jax.ShapeDtypeStruct((cols, height, LANES), f32),
         scratch_shapes=[pltpu.VMEM((channels, LANES), f32), pltpu.VMEM((channels // 2, LANES), f32)],
         name="tap_grad",
-    )(up, mid, down, left, right, grad_mixed, small, keep, recv)
+    )(up, mid, down, left, right, grad_mixed, small, *pieces)
 
 
 def backward_kernel(up, mid, down, left, right, kern, cot, out):
@@ -563,12 +562,12 @@
     return lax.ppermute(last, axis, up), lax.ppermute(first, axis, down)
 
 
-def halo(x):
+def halo(x, gain, shift):
     rows = x.shape[0]
     up, down = neighbours(x[:HALF], x[rows - HALF :], "row")
-    first, last = edges(up, x, down)
+    first, last, both = edges(up, x, down, gain, shift)
     left, right = neighbours(first, last, "col")
-    return up, down, left, right
+    return up, down, left, right, both
 
 
 def exchange(x, axis):
@@ -594,16 +593,16 @@
     gain = norm_gain.reshape(1, channels)
     shift = norm_shift.reshape(1, channels)
     bias = lax.dynamic_slice_in_dim(expand_bias, lax.axis_index("ch") * hid, hid).reshape(1, hid)
-    up, down, left, right = halo(img)
-    mixed, send = forward(up, img, down, left, right, depth_kernel, gain, shift, cot, parts)
+    up, down, left, right, affine = halo(img, gain, shift)
+    mixed, send = forward(up, img, down, left, right, depth_kernel, affine, cot, parts)
     recv = exchange(send, "ch")
     send, stats, give, keep, off = mlp(recv, expand_weight, bias, reduce_weight)
     recv = exchange(send, "ch")
-    keep, part = reduce_rows(give, keep)
+    pieces = reduce_rows(give, keep)
     result, grad_mixed, rounded, small = norm_back(recv, mixed, stats, gain, img, off)
-    g_up, g_down, g_left, g_right = halo(rounded)
+    g_up, g_down, g_left, g_right, _ = halo(rounded, gain, shift)
     cols = lax.axis_size("col")
-    part = tap_grad(up, img, down, left, right, grad_mixed, small, keep, part, cols)
+    part = tap_grad(up, img, down, left, right, grad_mixed, small, pieces, cols)
     grad_image = backward(g_up, rounded, g_down, g_left, g_right, depth_kernel, cot)
     flat = reduce_cols(part, channels // 2 // cols)
     pixels_all = pixels * lax.axis_size("row") * lax.axis_size("col")

time: 134 us -> 135 us (level)
  starting transfers between devices: 48.8 us -> 51 us
  waiting for transfers between devices: 25.7 us -> 23.9 us
    ppermute x3 -> x4, starting transfers between devices: 9.55 us -> 12 us  [the longest x3 9.69 us: reduce_rows(): lax.ppermute(chunks[m], 'row', [(i, i ^ 2 * m) for i in range(size)])]
    ppermute x3 -> x4, waiting for transfers between devices: 5.85 us -> 4.05 us  [the longest x3 2.91 us: reduce_rows(): lax.ppermute(chunks[m], 'row', [(i, i ^ 2 * m) for i in range(size)])]
    pallas_call x12 -> x11, Pallas kernels: 12 us -> 12.5 us  [call(): pl.pallas_call(kernel, out_shape=out_shape, in_specs=[spec] * len(args),...]
  transfers between devices with their start and end apart: 14 -> 15, of which waited for: 7 -> 8; matrix products, arithmetic and copies ran while one was open for 2% -> 2% of each run, Pallas kernels for 2% -> 2%
where the time goes in v5:
time: 135 us; the launch traced here: 134 us
  starting transfers between devices  51 us (38%)
  blocking collectives  41.8 us (31%)
  waiting for transfers between devices  23.9 us (18%)
  Pallas kernels  12.5 us (9%)
  local copies, waits for them, and re-layouts  3.79 us (3%)
    all_to_all x2, blocking collectives, exchange(): return lax.all_to_all(x, axis, 0, 0)  41.8 us
    ppermute x8, starting transfers between devices, neighbours(): return (lax.ppermute(last, axis, up), lax.ppermute(first, axis, down))  23.3 us
    all_to_all x3, starting transfers between devices, exchange(): return lax.all_to_all(x, axis, 0, 0)  15.7 us
    pallas_call x11, Pallas kernels, call(): pl.pallas_call(kernel, out_shape=out_shape, in_specs=[spec] * len(args),...  12.5 us
    ppermute x8, waiting for transfers between devices, neighbours(): return (lax.ppermute(last, axis, up), lax.ppermute(first, axis, down))  10.2 us
    all_to_all x3, waiting for transfers between devices, exchange(): return lax.all_to_all(x, axis, 0, 0)  9.72 us
    ppermute x3, starting transfers between devices, reduce_rows(): lax.ppermute(chunks[m], 'row', [(i, i ^ 2 * m) for i in range(size)])  9.69 us
    unnamed x17, local copies, waits for them, and re-layouts  3 us
  transfers between devices with their start and end apart: 15, of which 8 were waited for; matrix products, arithmetic and copies ran while one was open for 2% of the time, Pallas kernels for 2%

profile of v5, /device:TPU:1, one launch (start us, length us, event | category | flops | bytes accessed | tf_op | source)
XLA Modules:
  0.0 133.8 jit_solution(7781775284851081079)
XLA Ops:
  0.6 0.9 copy.25
  1.5 4.6 %collective-permute-start = (bf16[3,64,128]{2,1,0:T(8,128)(2,1)S(1)}, bf16[3,64,128]{2,1,0:T(8,128)(2,1)S(1)}, u32[]{:S(2)}, u32[]{:S(2)}) collective-permute-start(bf16[3,64,128]{2,1,0:T(8,128)(2,1)S(1)} %get-tuple-element.71), channel_id=1, source_target_pairs={{0,64},{64,128},{128,192},{192,256},{256,320},{320,384},{384,448},... | collective-permute-start | bytes 147464 | tf_op jit(solution)/shard_map/ppermute | solution.py:562
  6.1 5.5 %collective-permute-start.1 = (bf16[3,64,128]{2,1,0:T(8,128)(2,1)S(1)}, bf16[3,64,128]{2,1,0:T(8,128)(2,1)S(1)}, u32[]{:S(2)}, u32[]{:S(2)}) collective-permute-start(bf16[3,64,128]{2,1,0:T(8,128)(2,1)S(1)} %get-tuple-element.70), channel_id=1, source_target_pairs={{64,0},{128,64},{192,128},{256,192},{320,256},{384,320},{448,384},... | collective-permute-start | bytes 147464 | tf_op jit(solution)/shard_map/ppermute | solution.py:562
  11.6 0.0 collective-permute-done.up
  11.6 0.8 collective-permute-done.1.down
  12.4 0.7 copy-done.2
  13.1 0.0 copy-done.3
  13.1 0.4 edges.2
  13.5 2.6 %collective-permute-start.2 = (bf16[64,128]{1,0:T(8,128)(2,1)S(1)}, bf16[64,128]{1,0:T(8,128)(2,1)S(1)}, u32[]{:S(2)}, u32[]{:S(2)}) collective-permute-start(bf16[64,128]{1,0:T(8,128)(2,1)S(1)} %get-tuple-element.34), channel_id=1, source_target_pairs={{0,4},{4,8},{8,12},{12,16},{16,20},{20,24},{24,28},{28,32},{32,36}... | collective-permute-start | bytes 49160 | tf_op jit(solution)/shard_map/ppermute | solution.py:562
  16.2 0.0 copy-start.5
  16.2 1.3 collective-permute-start.3
  17.5 0.1 copy.18.kern
  17.6 0.0 collective-permute-done.2.left
  17.6 3.2 %collective-permute-done.3.right = bf16[64,128]{1,0:T(8,128)(2,1)S(1)} collective-permute-done((bf16[64,128]{1,0:T(8,128)(2,1)S(1)}, bf16[64,128]{1,0:T(8,128)(2,1)S(1)}, u32[]{:S(2)}, u32[]{:S(2)}) %collective-permute-start.3) | collective-permute-done | bytes 16416 | tf_op jit(solution)/shard_map/ppermute | solution.py:562
  20.9 2.6 %forward.1 = (f32[64,512]{1,0:T(8,128)S(1)}, bf16[4,144,512]{2,1,0:T(8,128)(2,1)}) custom-call(bf16[3,64,128]{2,1,0:T(8,128)(2,1)S(1)} %collective-permute-done.up, bf16[4,64,128]{2,1,0:T(8,128)(2,1)S(1)} %bitcast.17, bf16[3,64,128]{2,1,0:T(8,128)(2,1)S(1)} %collective-permute-done.1.down, bf16[64,128]{1,0:T(8,128)(2,1)S(1)} %collective-permute-done.2.left, ...), custom_call_target="tpu_custom_call" | custom-call | tf_op jit(solution)/shard_map/forward/pallas_call | solution.py:28
  23.5 4.1 %all-to-all-start = ((bf16[4,144,512]{2,1,0:T(8,128)(2,1)}), bf16[4,144,512]{2,1,0:T(8,128)(2,1)S(1)}, u32[]{:S(2)}, u32[]{:S(2)}) async-start(bf16[4,144,512]{2,1,0:T(8,128)(2,1)} %get-tuple-element.37), calls=%async_computation | async-start | bytes 1179648 | tf_op jit(solution)/shard_map/all_to_all | solution.py:574
  27.6 0.8 dynamic_slice.3
  28.4 9.7 %all-to-all-done.recv = bf16[4,144,512]{2,1,0:T(8,128)(2,1)S(1)} async-done(((bf16[4,144,512]{2,1,0:T(8,128)(2,1)}), bf16[4,144,512]{2,1,0:T(8,128)(2,1)S(1)}, u32[]{:S(2)}, u32[]{:S(2)}) %all-to-all-start) | async-done | bytes 589856 | tf_op jit(solution)/shard_map/all_to_all | solution.py:574
  38.1 2.1 %mlp.1 = (bf16[4,144,512]{2,1,0:T(8,128)(2,1)}, f32[2,512]{1,0:T(2,128)S(1)}, f32[512,128]{1,0:T(8,128)S(1)}, f32[512,128]{1,0:T(8,128)S(1)}, f32[64,128]{1,0:T(8,128)S(1)}) custom-call(bf16[4,144,512]{2,1,0:T(8,128)(2,1)S(1)} %all-to-all-done.recv, bf16[256,256]{1,0:T(8,128)(2,1)S(1)} %copy-done, f32[1,256]{1,0:T(1,128)S(1)} %bitcast.27, ...), custom_call_target="tpu_custom_call" | custom-call | tf_op jit(solution)/shard_map/mlp/pallas_call | solution.py:28
  40.2 3.5 %all-to-all-start.1 = ((bf16[4,144,512]{2,1,0:T(8,128)(2,1)}), bf16[4,144,512]{2,1,0:T(8,128)(2,1)S(1)}, u32[]{:S(2)}, u32[]{:S(2)}) async-start(bf16[4,144,512]{2,1,0:T(8,128)(2,1)} %get-tuple-element.38), calls=%async_computation.1 | async-start | bytes 1179648 | tf_op jit(solution)/shard_map/all_to_all | solution.py:574
  43.7 2.3 %collective-permute-start.8 = (f32[512,128]{1,0:T(8,128)S(1)}, f32[512,128]{1,0:T(8,128)S(1)}, u32[]{:S(2)}, u32[]{:S(2)}) collective-permute-start(f32[512,128]{1,0:T(8,128)S(1)} %get-tuple-element.49), channel_id=1, source_target_pairs={{0,64},{64,0},{128,192},{192,128},{256,320},{320,256},{384,448},{4... | collective-permute-start | bytes 786440 | tf_op jit(solution)/shard_map/ppermute | solution.py:237
  46.0 1.1 collective-permute-done.8.recv
  47.2 4.8 %collective-permute-start.10 = (f32[128,128]{1,0:T(8,128)S(1)}, f32[128,128]{1,0:T(8,128)S(1)}, u32[]{:S(2)}, u32[]{:S(2)}) collective-permute-start(f32[128,128]{1,0:T(8,128)S(1)} %get-tuple-element.52), channel_id=1, source_target_pairs={{0,256},{64,320},{128,384},{192,448},{256,0},{320,64},{384,128},{4... | collective-permute-start | bytes 196616 | tf_op jit(solution)/shard_map/ppermute | solution.py:242
  52.0 3.0 %collective-permute-start.11 = (f32[128,128]{1,0:T(8,128)S(1)}, f32[128,128]{1,0:T(8,128)S(1)}, u32[]{:S(2)}, u32[]{:S(2)}) collective-permute-start(f32[128,128]{1,0:T(8,128)S(1)} %get-tuple-element.53), channel_id=1, source_target_pairs={{0,384},{64,448},{128,256},{192,320},{256,128},{320,192},{384,0},{... | collective-permute-start | bytes 196616 | tf_op jit(solution)/shard_map/ppermute | solution.py:242
  55.0 1.9 %collective-permute-start.9 = (f32[128,128]{1,0:T(8,128)S(1)}, f32[128,128]{1,0:T(8,128)S(1)}, u32[]{:S(2)}, u32[]{:S(2)}) collective-permute-start(f32[128,128]{1,0:T(8,128)S(1)} %get-tuple-element.51), channel_id=1, source_target_pairs={{0,128},{64,192},{128,0},{192,64},{256,384},{320,448},{384,256},{4... | collective-permute-start | bytes 196616 | tf_op jit(solution)/shard_map/ppermute | solution.py:242
  56.9 0.0 all-to-all-done.1.recv
  56.9 0.1 norm_back.1
  57.1 0.0 collective-permute-done.10.rest_2_
  57.1 1.1 collective-permute-done.11.rest_3_
  58.2 1.8 %collective-permute-done.9.rest_1_ = f32[128,128]{1,0:T(8,128)S(1)} collective-permute-done((f32[128,128]{1,0:T(8,128)S(1)}, f32[128,128]{1,0:T(8,128)S(1)}, u32[]{:S(2)}, u32[]{:S(2)}) %collective-permute-start.9) | collective-permute-done | bytes 65568 | tf_op jit(solution)/shard_map/ppermute | solution.py:242
  60.0 2.8 %tap_grad.1 = f32[16,16,128]{2,1,0:T(8,128)S(1)} custom-call(bf16[3,64,128]{2,1,0:T(8,128)(2,1)S(1)} %collective-permute-done.up, bf16[4,64,128]{2,1,0:T(8,128)(2,1)S(1)} %bitcast.19, bf16[3,64,128]{2,1,0:T(8,128)(2,1)S(1)} %collective-permute-done.1.down, bf16[64,128]{1,0:T(8,128)(2,1)S(1)} %collective-permute-done.2.left, ...), custom_call_target="tpu_custom_call" | custom-call | tf_op jit(solution)/shard_map/tap_grad/pallas_call | solution.py:28
  62.8 26.4 %all_to_all.25.recv = f32[16,16,128]{2,1,0:T(8,128)S(1)} all-to-all(f32[16,16,128]{2,1,0:T(8,128)S(1)} %tap_grad.1), channel_id=1, replica_groups=mesh['row'=8,'col'=16,'ch'=4] {'col'}, dimensions={0} | all-to-all | bytes 262144 | tf_op jit(solution)/shard_map/all_to_all | solution.py:574
  89.2 15.4 %all_to_all.26.recv = bf16[16,16,128]{2,1,0:T(8,128)(2,1)S(1)} all-to-all(bf16[16,16,128]{2,1,0:T(8,128)(2,1)S(1)} %col_pack.1), channel_id=1, replica_groups=mesh['row'=8,'col'=16,'ch'=4] {'col'}, dimensions={0} | all-to-all | bytes 131072 | tf_op jit(solution)/shard_map/all_to_all | solution.py:574
  104.6 0.8 row_pack.1
  105.4 8.1 %all-to-all-start.4 = ((bf16[8,192,128]{2,1,0:T(8,128)(2,1)}), bf16[8,192,128]{2,1,0:T(8,128)(2,1)S(1)}, u32[]{:S(2)}, u32[]{:S(2)}) async-start(bf16[8,192,128]{2,1,0:T(8,128)(2,1)} %row_pack.1), calls=%async_computation.4 | async-start | bytes 786432 | tf_op jit(solution)/shard_map/all_to_all | solution.py:574
  113.5 3.5 %collective-permute-start.4 = (bf16[3,64,128]{2,1,0:T(8,128)(2,1)S(1)}, bf16[3,64,128]{2,1,0:T(8,128)(2,1)S(1)}, u32[]{:S(2)}, u32[]{:S(2)}) collective-permute-start(bf16[3,64,128]{2,1,0:T(8,128)(2,1)S(1)} %get-tuple-element.69), channel_id=1, source_target_pairs={{0,64},{64,128},{128,192},{192,256},{256,320},{320,384},{384,448},... | collective-permute-start | bytes 147464 | tf_op jit(solution)/shard_map/ppermute | solution.py:562
  117.1 1.9 %collective-permute-start.5 = (bf16[3,64,128]{2,1,0:T(8,128)(2,1)S(1)}, bf16[3,64,128]{2,1,0:T(8,128)(2,1)S(1)}, u32[]{:S(2)}, u32[]{:S(2)}) collective-permute-start(bf16[3,64,128]{2,1,0:T(8,128)(2,1)S(1)} %get-tuple-element.68), channel_id=1, source_target_pairs={{64,0},{128,64},{192,128},{256,192},{320,256},{384,320},{448,384},... | collective-permute-start | bytes 147464 | tf_op jit(solution)/shard_map/ppermute | solution.py:562
  119.0 0.0 collective-permute-done.4.up
  119.0 3.6 %collective-permute-done.5.down = bf16[3,64,128]{2,1,0:T(8,128)(2,1)S(1)} collective-permute-done((bf16[3,64,128]{2,1,0:T(8,128)(2,1)S(1)}, bf16[3,64,128]{2,1,0:T(8,128)(2,1)S(1)}, u32[]{:S(2)}, u32[]{:S(2)}) %collective-permute-start.5) | collective-permute-done | bytes 49184 | tf_op jit(solution)/shard_map/ppermute | solution.py:562
  122.6 0.9 edges.3
  123.4 2.5 %collective-permute-start.6 = (bf16[64,128]{1,0:T(8,128)(2,1)S(1)}, bf16[64,128]{1,0:T(8,128)(2,1)S(1)}, u32[]{:S(2)}, u32[]{:S(2)}) collective-permute-start(bf16[64,128]{1,0:T(8,128)(2,1)S(1)} %get-tuple-element.44), channel_id=1, source_target_pairs={{0,4},{4,8},{8,12},{12,16},{16,20},{20,24},{24,28},{28,32},{32,36}... | collective-permute-start | bytes 49160 | tf_op jit(solution)/shard_map/ppermute | solution.py:562
  126.0 1.3 collective-permute-start.7
  127.3 0.7 copy.20
  128.0 0.0 collective-permute-done.6.left
  128.0 2.5 %collective-permute-done.7.right = bf16[64,128]{1,0:T(8,128)(2,1)S(1)} collective-permute-done((bf16[64,128]{1,0:T(8,128)(2,1)S(1)}, bf16[64,128]{1,0:T(8,128)(2,1)S(1)}, u32[]{:S(2)}, u32[]{:S(2)}) %collective-permute-start.7) | collective-permute-done | bytes 16416 | tf_op jit(solution)/shard_map/ppermute | solution.py:562
  130.5 1.7 %backward.1 = bf16[4,64,128]{2,1,0:T(8,128)(2,1)S(1)} custom-call(bf16[3,64,128]{2,1,0:T(8,128)(2,1)S(1)} %collective-permute-done.4.up, bf16[4,64,128]{2,1,0:T(8,128)(2,1)S(1)} %get-tuple-element.43.mid, bf16[3,64,128]{2,1,0:T(8,128)(2,1)S(1)} %collective-permute-done.5.down, bf16[64,128]{1,0:T(8,128)(2,1)S(1)} %collective-permute-done.6.left, ...), custom_call_target="tpu_custom_call" | custom-call | tf_op jit(solution)/shard_map/backward/pallas_call | solution.py:28
  132.2 0.7 copy.21
  132.8 1.0 final.1
  (15 shorter events, 0.1 us)
Async XLA Ops:
  1.5 10.1 %collective-permute-start = (bf16[3,64,128]{2,1,0:T(8,128)(2,1)S(1)}, bf16[3,64,128]{2,1,0:T(8,128)(2,1)S(1)}, u32[]{:S(2)}, u32[]{:S(2)}) collective-permute-start(bf16[3,64,128]{2,1,0:T(8,128)(2,1)S(1)} %get-tuple-element.71), channel_id=1, source_target_pairs={{0,64},{64,128},{128,192},{192,256},{256,320},{320,384},{384,448},... | collective-permute-start | bytes 147464 | tf_op jit(solution)/shard_map/ppermute | solution.py:562
  6.1 6.3 %collective-permute-start.1 = (bf16[3,64,128]{2,1,0:T(8,128)(2,1)S(1)}, bf16[3,64,128]{2,1,0:T(8,128)(2,1)S(1)}, u32[]{:S(2)}, u32[]{:S(2)}) collective-permute-start(bf16[3,64,128]{2,1,0:T(8,128)(2,1)S(1)} %get-tuple-element.70), channel_id=1, source_target_pairs={{64,0},{128,64},{192,128},{256,192},{320,256},{384,320},{448,384},... | collective-permute-start | bytes 147464 | tf_op jit(solution)/shard_map/ppermute | solution.py:562
  12.4 0.7 copy-start.2
  12.4 0.7 copy-start.3
  13.1 4.4 %copy-start.4 = (bf16[64,4,128]{2,1,0:T(4,128)(2,1)S(1)}, bf16[64,4,128]{2,1,0:T(4,128)(2,1)}, u32[]{:S(2)}) copy-start(bf16[64,4,128]{2,1,0:T(4,128)(2,1)} %param.15) | copy-start | bytes 196612
  13.5 4.1 %collective-permute-start.2 = (bf16[64,128]{1,0:T(8,128)(2,1)S(1)}, bf16[64,128]{1,0:T(8,128)(2,1)S(1)}, u32[]{:S(2)}, u32[]{:S(2)}) collective-permute-start(bf16[64,128]{1,0:T(8,128)(2,1)S(1)} %get-tuple-element.34), channel_id=1, source_target_pairs={{0,4},{4,8},{8,12},{12,16},{16,20},{20,24},{24,28},{28,32},{32,36}... | collective-permute-start | bytes 49160 | tf_op jit(solution)/shard_map/ppermute | solution.py:562
  16.2 1.3 %copy-start.5 = (f32[64,49]{0,1:T(8,128)S(1)}, f32[64,49]{0,1:T(8,128)}, u32[]{:S(2)}) copy-start(f32[64,49]{0,1:T(8,128)} %param.9) | copy-start | bytes 37636
  16.2 4.7 %collective-permute-start.3 = (bf16[64,128]{1,0:T(8,128)(2,1)S(1)}, bf16[64,128]{1,0:T(8,128)(2,1)S(1)}, u32[]{:S(2)}, u32[]{:S(2)}) collective-permute-start(bf16[64,128]{1,0:T(8,128)(2,1)S(1)} %get-tuple-element.35), channel_id=1, source_target_pairs={{4,0},{8,4},{12,8},{16,12},{20,16},{24,20},{28,24},{32,28},{36,32}... | collective-permute-start | bytes 49160 | tf_op jit(solution)/shard_map/ppermute | solution.py:562
  23.5 14.6 %copy-start = (bf16[256,256]{1,0:T(8,128)(2,1)S(1)}, bf16[256,256]{1,0:T(8,128)(2,1)}, u32[]{:S(2)}) copy-start(bf16[256,256]{1,0:T(8,128)(2,1)} %w_exp.1) | copy-start | bytes 393220
  23.5 14.6 %copy-start.1 = (bf16[256,256]{1,0:T(8,128)(2,1)S(1)}, bf16[256,256]{1,0:T(8,128)(2,1)}, u32[]{:S(2)}) copy-start(bf16[256,256]{1,0:T(8,128)(2,1)} %w_red.1) | copy-start | bytes 393220
  23.5 14.6 %all-to-all-start = ((bf16[4,144,512]{2,1,0:T(8,128)(2,1)}), bf16[4,144,512]{2,1,0:T(8,128)(2,1)S(1)}, u32[]{:S(2)}, u32[]{:S(2)}) async-start(bf16[4,144,512]{2,1,0:T(8,128)(2,1)} %get-tuple-element.37), calls=%async_computation | async-start | bytes 1179648 | tf_op jit(solution)/shard_map/all_to_all | solution.py:574
  40.2 16.7 %all-to-all-start.1 = ((bf16[4,144,512]{2,1,0:T(8,128)(2,1)}), bf16[4,144,512]{2,1,0:T(8,128)(2,1)S(1)}, u32[]{:S(2)}, u32[]{:S(2)}) async-start(bf16[4,144,512]{2,1,0:T(8,128)(2,1)} %get-tuple-element.38), calls=%async_computation.1 | async-start | bytes 1179648 | tf_op jit(solution)/shard_map/all_to_all | solution.py:574
  43.7 3.5 %collective-permute-start.8 = (f32[512,128]{1,0:T(8,128)S(1)}, f32[512,128]{1,0:T(8,128)S(1)}, u32[]{:S(2)}, u32[]{:S(2)}) collective-permute-start(f32[512,128]{1,0:T(8,128)S(1)} %get-tuple-element.49), channel_id=1, source_target_pairs={{0,64},{64,0},{128,192},{192,128},{256,320},{320,256},{384,448},{4... | collective-permute-start | bytes 786440 | tf_op jit(solution)/shard_map/ppermute | solution.py:237
  47.2 9.9 %collective-permute-start.10 = (f32[128,128]{1,0:T(8,128)S(1)}, f32[128,128]{1,0:T(8,128)S(1)}, u32[]{:S(2)}, u32[]{:S(2)}) collective-permute-start(f32[128,128]{1,0:T(8,128)S(1)} %get-tuple-element.52), channel_id=1, source_target_pairs={{0,256},{64,320},{128,384},{192,448},{256,0},{320,64},{384,128},{4... | collective-permute-start | bytes 196616 | tf_op jit(solution)/shard_map/ppermute | solution.py:242
  52.0 6.2 %collective-permute-start.11 = (f32[128,128]{1,0:T(8,128)S(1)}, f32[128,128]{1,0:T(8,128)S(1)}, u32[]{:S(2)}, u32[]{:S(2)}) collective-permute-start(f32[128,128]{1,0:T(8,128)S(1)} %get-tuple-element.53), channel_id=1, source_target_pairs={{0,384},{64,448},{128,256},{192,320},{256,128},{320,192},{384,0},{... | collective-permute-start | bytes 196616 | tf_op jit(solution)/shard_map/ppermute | solution.py:242
  55.0 5.0 %collective-permute-start.9 = (f32[128,128]{1,0:T(8,128)S(1)}, f32[128,128]{1,0:T(8,128)S(1)}, u32[]{:S(2)}, u32[]{:S(2)}) collective-permute-start(f32[128,128]{1,0:T(8,128)S(1)} %get-tuple-element.51), channel_id=1, source_target_pairs={{0,128},{64,192},{128,0},{192,64},{256,384},{320,448},{384,256},{4... | collective-permute-start | bytes 196616 | tf_op jit(solution)/shard_map/ppermute | solution.py:242
  105.4 27.5 %all-to-all-start.4 = ((bf16[8,192,128]{2,1,0:T(8,128)(2,1)}), bf16[8,192,128]{2,1,0:T(8,128)(2,1)S(1)}, u32[]{:S(2)}, u32[]{:S(2)}) async-start(bf16[8,192,128]{2,1,0:T(8,128)(2,1)} %row_pack.1), calls=%async_computation.4 | async-start | bytes 786432 | tf_op jit(solution)/shard_map/all_to_all | solution.py:574
  113.5 5.5 %collective-permute-start.4 = (bf16[3,64,128]{2,1,0:T(8,128)(2,1)S(1)}, bf16[3,64,128]{2,1,0:T(8,128)(2,1)S(1)}, u32[]{:S(2)}, u32[]{:S(2)}) collective-permute-start(bf16[3,64,128]{2,1,0:T(8,128)(2,1)S(1)} %get-tuple-element.69), channel_id=1, source_target_pairs={{0,64},{64,128},{128,192},{192,256},{256,320},{320,384},{384,448},... | collective-permute-start | bytes 147464 | tf_op jit(solution)/shard_map/ppermute | solution.py:562
  117.1 5.5 %collective-permute-start.5 = (bf16[3,64,128]{2,1,0:T(8,128)(2,1)S(1)}, bf16[3,64,128]{2,1,0:T(8,128)(2,1)S(1)}, u32[]{:S(2)}, u32[]{:S(2)}) collective-permute-start(bf16[3,64,128]{2,1,0:T(8,128)(2,1)S(1)} %get-tuple-element.68), channel_id=1, source_target_pairs={{64,0},{128,64},{192,128},{256,192},{320,256},{384,320},{448,384},... | collective-permute-start | bytes 147464 | tf_op jit(solution)/shard_map/ppermute | solution.py:562
  123.4 4.5 %collective-permute-start.6 = (bf16[64,128]{1,0:T(8,128)(2,1)S(1)}, bf16[64,128]{1,0:T(8,128)(2,1)S(1)}, u32[]{:S(2)}, u32[]{:S(2)}) collective-permute-start(bf16[64,128]{1,0:T(8,128)(2,1)S(1)} %get-tuple-element.44), channel_id=1, source_target_pairs={{0,4},{4,8},{8,12},{12,16},{16,20},{20,24},{24,28},{28,32},{32,36}... | collective-permute-start | bytes 49160 | tf_op jit(solution)/shard_map/ppermute | solution.py:562
  126.0 4.5 %collective-permute-start.7 = (bf16[64,128]{1,0:T(8,128)(2,1)S(1)}, bf16[64,128]{1,0:T(8,128)(2,1)S(1)}, u32[]{:S(2)}, u32[]{:S(2)}) collective-permute-start(bf16[64,128]{1,0:T(8,128)(2,1)S(1)} %get-tuple-element.45), channel_id=1, source_target_pairs={{4,0},{8,4},{12,8},{16,12},{20,16},{24,20},{28,24},{32,28},{36,32}... | collective-permute-start | bytes 49160 | tf_op jit(solution)/shard_map/ppermute | solution.py:562

commit v6 on v5

--- a/solution.py
+++ b/solution.py
@@ -21,14 +21,15 @@
 OFFSET = GAIN + 2
 
 
-def vcall(kernel, out_shape, **kw):
+def vcall(kernel, out_shape, hbm=(), **kw):
     spec = pl.BlockSpec(memory_space=pltpu.VMEM)
+    outside = pl.BlockSpec(memory_space=pltpu.MemorySpace.HBM)
 
     def call(*args):
         return pl.pallas_call(
             kernel,
             out_shape=out_shape,
-            in_specs=[spec] * len(args),
+            in_specs=[outside if k in hbm else spec for k in range(len(args))],
             out_specs=jax.tree.map(lambda _: spec, out_shape),
             compiler_params=pltpu.CompilerParams(vmem_limit_bytes=8 << 20),
             **kw,
@@ -92,8 +93,7 @@
     return jnp.where(mask, rolled(edge, -s), rolled(x, -s))
 
 
-def edges_kernel(up, mid, down, gain, shift, first, last, both):
-    both[...] = jnp.concatenate([gain[...], shift[...]], axis=1)
+def edges_kernel(up, mid, down, first, last):
     channels = mid.shape[1]
     lane = lane_ids(CT)
 
@@ -119,14 +119,9 @@
     lax.fori_loop(0, channels // CT, step, 0)
 
 
-def edges(up, mid, down, gain, shift):
-    channels = mid.shape[1]
-    shape = jax.ShapeDtypeStruct((channels, LANES), bf16)
-    return vcall(
-        edges_kernel,
-        out_shape=(shape, shape, jax.ShapeDtypeStruct((1, 2 * channels), f32)),
-        name="edges",
-    )(up, mid, down, gain, shift)
+def edges(up, mid, down):
+    shape = jax.ShapeDtypeStruct((mid.shape[1], LANES), bf16)
+    return vcall(edges_kernel, out_shape=(shape, shape), name="edges")(up, mid, down)
 
 
 def accumulate_taps(rows, kern, at, flip):
@@ -144,8 +139,13 @@
     return accum
 
 
-def forward_kernel(up, mid, down, left, right, kern, affine, cot, mixed, payload):
+def forward_kernel(up, mid, down, left, right, kern, gain, shift, cot, mixed, payload, affine, sem):
     tile_rows, channels, _ = mid.shape
+    copies = [
+        pltpu.make_async_copy(x, affine.at[pl.ds(k, 1)], sem.at[k]) for k, x in enumerate((gain, shift))
+    ]
+    for copy in copies:
+        copy.start()
 
     def step(t, carry):
         at = pl.ds(pl.multiple_of(t * CT, CT), CT)
@@ -166,7 +166,10 @@
         stats = jnp.concatenate(rows + [jnp.zeros((CT - 6, LANES), f32)], axis=0)
         if i == 0:
             row_id = lax.broadcasted_iota(jnp.int32, (CT, LANES), 0)
-            for k, part in enumerate(split3(affine[...])):
+            for copy in copies:
+                copy.wait()
+            both = jnp.concatenate([affine[0:1], affine[1:2]], axis=1)
+            for k, part in enumerate(split3(both)):
                 stats = jnp.where(row_id == 6 + k, jnp.broadcast_to(part, (CT, LANES)), stats)
         dev = dev.astype(bf16)
         stats = stats.astype(bf16)
@@ -176,7 +179,7 @@
             payload[d, 2 * channels : 2 * channels + CT, cols] = stats
 
 
-def forward(up, mid, down, left, right, kern, affine, cot, parts):
+def forward(up, mid, down, left, right, kern, gain, shift, cot, parts):
     tile_rows, channels, _ = mid.shape
     pixels = tile_rows * LANES
     return vcall(
@@ -185,8 +188,10 @@
             jax.ShapeDtypeStruct((channels, pixels), f32),
             jax.ShapeDtypeStruct((parts, 2 * channels + CT, pixels), bf16),
         ),
+        hbm=(6, 7),
+        scratch_shapes=[pltpu.VMEM((2, channels), f32), pltpu.SemaphoreType.DMA((2,))],
         name="forward",
-    )(up, mid, down, left, right, kern, affine, cot)
+    )(up, mid, down, left, right, kern, gain, shift, cot)
 
 
 def column(row, n):
@@ -562,12 +567,12 @@
     return lax.ppermute(last, axis, up), lax.ppermute(first, axis, down)
 
 
-def halo(x, gain, shift):
+def halo(x):
     rows = x.shape[0]
     up, down = neighbours(x[:HALF], x[rows - HALF :], "row")
-    first, last, both = edges(up, x, down, gain, shift)
+    first, last = edges(up, x, down)
     left, right = neighbours(first, last, "col")
-    return up, down, left, right, both
+    return up, down, left, right
 
 
 def exchange(x, axis):
@@ -593,14 +598,14 @@
     gain = norm_gain.reshape(1, channels)
     shift = norm_shift.reshape(1, channels)
     bias = lax.dynamic_slice_in_dim(expand_bias, lax.axis_index("ch") * hid, hid).reshape(1, hid)
-    up, down, left, right, affine = halo(img, gain, shift)
-    mixed, send = forward(up, img, down, left, right, depth_kernel, affine, cot, parts)
+    up, down, left, right = halo(img)
+    mixed, send = forward(up, img, down, left, right, depth_kernel, gain, shift, cot, parts)
     recv = exchange(send, "ch")
     send, stats, give, keep, off = mlp(recv, expand_weight, bias, reduce_weight)
     recv = exchange(send, "ch")
     pieces = reduce_rows(give, keep)
     result, grad_mixed, rounded, small = norm_back(recv, mixed, stats, gain, img, off)
-    g_up, g_down, g_left, g_right, _ = halo(rounded, gain, shift)
+    g_up, g_down, g_left, g_right = halo(rounded)
     cols = lax.axis_size("col")
     part = tap_grad(up, img, down, left, right, grad_mixed, small, pieces, cols)
     grad_image = backward(g_up, rounded, g_down, g_left, g_right, depth_kernel, cot)

time: 135 us -> 134 us (level)
  no operation moved by 1% of the time
where the time goes in v6:
time: 134 us
  starting transfers between devices  51.1 us (38%)
  blocking collectives  41.8 us (31%)
  waiting for transfers between devices  23.9 us (18%)
  Pallas kernels  12 us (9%)
  local copies, waits for them, and re-layouts  3.79 us (3%)
    all_to_all x2, blocking collectives, exchange(): return lax.all_to_all(x, axis, 0, 0)  41.8 us
    ppermute x8, starting transfers between devices, neighbours(): return (lax.ppermute(last, axis, up), lax.ppermute(first, axis, down))  23.4 us
    all_to_all x3, starting transfers between devices, exchange(): return lax.all_to_all(x, axis, 0, 0)  15.7 us
    pallas_call x11, Pallas kernels, call(): pl.pallas_call(kernel, out_shape=out_shape, in_specs=[outside if k in hbm...  12 us
    ppermute x8, waiting for transfers between devices, neighbours(): return (lax.ppermute(last, axis, up), lax.ppermute(first, axis, down))  10.2 us
    all_to_all x3, waiting for transfers between devices, exchange(): return lax.all_to_all(x, axis, 0, 0)  9.72 us
    ppermute x3, starting transfers between devices, reduce_rows(): lax.ppermute(chunks[m], 'row', [(i, i ^ 2 * m) for i in range(size)])  9.69 us
    unnamed x17, local copies, waits for them, and re-layouts  3.01 us
  transfers between devices with their start and end apart: 15, of which 8 were waited for; matrix products, arithmetic and copies ran while one was open for 2% of the time, Pallas kernels for 2%

profile of v6, /device:TPU:1, one launch (start us, length us, event | category | flops | bytes accessed | tf_op | source)
XLA Modules:
  0.0 133.5 jit_solution(16980918526929766485)
XLA Ops:
  0.6 0.9 copy.25
  1.5 4.6 %collective-permute-start = (bf16[3,64,128]{2,1,0:T(8,128)(2,1)S(1)}, bf16[3,64,128]{2,1,0:T(8,128)(2,1)S(1)}, u32[]{:S(2)}, u32[]{:S(2)}) collective-permute-start(bf16[3,64,128]{2,1,0:T(8,128)(2,1)S(1)} %get-tuple-element.69), channel_id=1, source_target_pairs={{0,64},{64,128},{128,192},{192,256},{256,320},{320,384},{384,448},... | collective-permute-start | bytes 147464 | tf_op jit(solution)/shard_map/ppermute | solution.py:567
  6.1 0.0 copy-start.4
  6.1 5.6 %collective-permute-start.1 = (bf16[3,64,128]{2,1,0:T(8,128)(2,1)S(1)}, bf16[3,64,128]{2,1,0:T(8,128)(2,1)S(1)}, u32[]{:S(2)}, u32[]{:S(2)}) collective-permute-start(bf16[3,64,128]{2,1,0:T(8,128)(2,1)S(1)} %get-tuple-element.68), channel_id=1, source_target_pairs={{64,0},{128,64},{192,128},{256,192},{320,256},{384,320},{448,384},... | collective-permute-start | bytes 147464 | tf_op jit(solution)/shard_map/ppermute | solution.py:567
  11.7 0.0 collective-permute-done.up
  11.7 0.8 collective-permute-done.1.down
  12.6 0.4 edges.2
  12.9 2.6 %collective-permute-start.2 = (bf16[64,128]{1,0:T(8,128)(2,1)S(1)}, bf16[64,128]{1,0:T(8,128)(2,1)S(1)}, u32[]{:S(2)}, u32[]{:S(2)}) collective-permute-start(bf16[64,128]{1,0:T(8,128)(2,1)S(1)} %get-tuple-element.33), channel_id=1, source_target_pairs={{0,4},{4,8},{8,12},{12,16},{16,20},{20,24},{24,28},{28,32},{32,36}... | collective-permute-start | bytes 49160 | tf_op jit(solution)/shard_map/ppermute | solution.py:567
  15.6 0.0 copy-start.5
  15.6 1.3 collective-permute-start.3
  16.9 0.1 copy.18.kern
  17.0 0.0 collective-permute-done.2.left
  17.0 3.2 %collective-permute-done.3.right = bf16[64,128]{1,0:T(8,128)(2,1)S(1)} collective-permute-done((bf16[64,128]{1,0:T(8,128)(2,1)S(1)}, bf16[64,128]{1,0:T(8,128)(2,1)S(1)}, u32[]{:S(2)}, u32[]{:S(2)}) %collective-permute-start.3) | collective-permute-done | bytes 16416 | tf_op jit(solution)/shard_map/ppermute | solution.py:567
  20.3 0.7 copy-done.2
  20.9 0.0 copy-done.3
  20.9 2.7 %forward.1 = (f32[64,512]{1,0:T(8,128)S(1)}, bf16[4,144,512]{2,1,0:T(8,128)(2,1)}) custom-call(bf16[3,64,128]{2,1,0:T(8,128)(2,1)S(1)} %collective-permute-done.up, bf16[4,64,128]{2,1,0:T(8,128)(2,1)S(1)} %bitcast.17, bf16[3,64,128]{2,1,0:T(8,128)(2,1)S(1)} %collective-permute-done.1.down, bf16[64,128]{1,0:T(8,128)(2,1)S(1)} %collective-permute-done.2.left, ...), custom_call_target="tpu_custom_call" | custom-call | tf_op jit(solution)/shard_map/forward/pallas_call | solution.py:29
  23.6 0.0 copy-start
  23.6 0.0 copy-start.1
  23.6 4.2 %all-to-all-start = ((bf16[4,144,512]{2,1,0:T(8,128)(2,1)}), bf16[4,144,512]{2,1,0:T(8,128)(2,1)S(1)}, u32[]{:S(2)}, u32[]{:S(2)}) async-start(bf16[4,144,512]{2,1,0:T(8,128)(2,1)} %get-tuple-element.35), calls=%async_computation | async-start | bytes 1179648 | tf_op jit(solution)/shard_map/all_to_all | solution.py:579
  27.8 0.8 dynamic_slice.3
  28.5 9.7 %all-to-all-done.recv = bf16[4,144,512]{2,1,0:T(8,128)(2,1)S(1)} async-done(((bf16[4,144,512]{2,1,0:T(8,128)(2,1)}), bf16[4,144,512]{2,1,0:T(8,128)(2,1)S(1)}, u32[]{:S(2)}, u32[]{:S(2)}) %all-to-all-start) | async-done | bytes 589856 | tf_op jit(solution)/shard_map/all_to_all | solution.py:579
  38.3 2.1 %mlp.1 = (bf16[4,144,512]{2,1,0:T(8,128)(2,1)}, f32[2,512]{1,0:T(2,128)S(1)}, f32[512,128]{1,0:T(8,128)S(1)}, f32[512,128]{1,0:T(8,128)S(1)}, f32[64,128]{1,0:T(8,128)S(1)}) custom-call(bf16[4,144,512]{2,1,0:T(8,128)(2,1)S(1)} %all-to-all-done.recv, bf16[256,256]{1,0:T(8,128)(2,1)S(1)} %copy-done, f32[1,256]{1,0:T(1,128)S(1)} %bitcast.24, ...), custom_call_target="tpu_custom_call" | custom-call | tf_op jit(solution)/shard_map/mlp/pallas_call | solution.py:29
  40.4 3.5 %all-to-all-start.1 = ((bf16[4,144,512]{2,1,0:T(8,128)(2,1)}), bf16[4,144,512]{2,1,0:T(8,128)(2,1)S(1)}, u32[]{:S(2)}, u32[]{:S(2)}) async-start(bf16[4,144,512]{2,1,0:T(8,128)(2,1)} %get-tuple-element.36), calls=%async_computation.1 | async-start | bytes 1179648 | tf_op jit(solution)/shard_map/all_to_all | solution.py:579
  43.9 2.3 %collective-permute-start.8 = (f32[512,128]{1,0:T(8,128)S(1)}, f32[512,128]{1,0:T(8,128)S(1)}, u32[]{:S(2)}, u32[]{:S(2)}) collective-permute-start(f32[512,128]{1,0:T(8,128)S(1)} %get-tuple-element.47), channel_id=1, source_target_pairs={{0,64},{64,0},{128,192},{192,128},{256,320},{320,256},{384,448},{4... | collective-permute-start | bytes 786440 | tf_op jit(solution)/shard_map/ppermute | solution.py:242
  46.2 1.1 collective-permute-done.8.recv
  47.4 4.8 %collective-permute-start.10 = (f32[128,128]{1,0:T(8,128)S(1)}, f32[128,128]{1,0:T(8,128)S(1)}, u32[]{:S(2)}, u32[]{:S(2)}) collective-permute-start(f32[128,128]{1,0:T(8,128)S(1)} %get-tuple-element.50), channel_id=1, source_target_pairs={{0,256},{64,320},{128,384},{192,448},{256,0},{320,64},{384,128},{4... | collective-permute-start | bytes 196616 | tf_op jit(solution)/shard_map/ppermute | solution.py:247
  52.2 3.0 %collective-permute-start.11 = (f32[128,128]{1,0:T(8,128)S(1)}, f32[128,128]{1,0:T(8,128)S(1)}, u32[]{:S(2)}, u32[]{:S(2)}) collective-permute-start(f32[128,128]{1,0:T(8,128)S(1)} %get-tuple-element.51), channel_id=1, source_target_pairs={{0,384},{64,448},{128,256},{192,320},{256,128},{320,192},{384,0},{... | collective-permute-start | bytes 196616 | tf_op jit(solution)/shard_map/ppermute | solution.py:247
  55.2 1.9 %collective-permute-start.9 = (f32[128,128]{1,0:T(8,128)S(1)}, f32[128,128]{1,0:T(8,128)S(1)}, u32[]{:S(2)}, u32[]{:S(2)}) collective-permute-start(f32[128,128]{1,0:T(8,128)S(1)} %get-tuple-element.49), channel_id=1, source_target_pairs={{0,128},{64,192},{128,0},{192,64},{256,384},{320,448},{384,256},{4... | collective-permute-start | bytes 196616 | tf_op jit(solution)/shard_map/ppermute | solution.py:247
  57.1 0.1 norm_back.1
  57.3 0.0 collective-permute-done.10.rest_2_
  57.3 1.1 collective-permute-done.11.rest_3_
  58.4 1.8 %collective-permute-done.9.rest_1_ = f32[128,128]{1,0:T(8,128)S(1)} collective-permute-done((f32[128,128]{1,0:T(8,128)S(1)}, f32[128,128]{1,0:T(8,128)S(1)}, u32[]{:S(2)}, u32[]{:S(2)}) %collective-permute-start.9) | collective-permute-done | bytes 65568 | tf_op jit(solution)/shard_map/ppermute | solution.py:247
  60.2 2.8 %tap_grad.1 = f32[16,16,128]{2,1,0:T(8,128)S(1)} custom-call(bf16[3,64,128]{2,1,0:T(8,128)(2,1)S(1)} %collective-permute-done.up, bf16[4,64,128]{2,1,0:T(8,128)(2,1)S(1)} %bitcast.19, bf16[3,64,128]{2,1,0:T(8,128)(2,1)S(1)} %collective-permute-done.1.down, bf16[64,128]{1,0:T(8,128)(2,1)S(1)} %collective-permute-done.2.left, ...), custom_call_target="tpu_custom_call" | custom-call | tf_op jit(solution)/shard_map/tap_grad/pallas_call | solution.py:29
  63.0 26.4 %all_to_all.25.recv = f32[16,16,128]{2,1,0:T(8,128)S(1)} all-to-all(f32[16,16,128]{2,1,0:T(8,128)S(1)} %tap_grad.1), channel_id=1, replica_groups=mesh['row'=8,'col'=16,'ch'=4] {'col'}, dimensions={0} | all-to-all | bytes 262144 | tf_op jit(solution)/shard_map/all_to_all | solution.py:579
  89.4 15.4 %all_to_all.26.recv = bf16[16,16,128]{2,1,0:T(8,128)(2,1)S(1)} all-to-all(bf16[16,16,128]{2,1,0:T(8,128)(2,1)S(1)} %col_pack.1), channel_id=1, replica_groups=mesh['row'=8,'col'=16,'ch'=4] {'col'}, dimensions={0} | all-to-all | bytes 131072 | tf_op jit(solution)/shard_map/all_to_all | solution.py:579
  104.8 0.8 row_pack.1
  105.6 8.1 %all-to-all-start.4 = ((bf16[8,192,128]{2,1,0:T(8,128)(2,1)}), bf16[8,192,128]{2,1,0:T(8,128)(2,1)S(1)}, u32[]{:S(2)}, u32[]{:S(2)}) async-start(bf16[8,192,128]{2,1,0:T(8,128)(2,1)} %row_pack.1), calls=%async_computation.4 | async-start | bytes 786432 | tf_op jit(solution)/shard_map/all_to_all | solution.py:579
  113.7 3.5 %collective-permute-start.4 = (bf16[3,64,128]{2,1,0:T(8,128)(2,1)S(1)}, bf16[3,64,128]{2,1,0:T(8,128)(2,1)S(1)}, u32[]{:S(2)}, u32[]{:S(2)}) collective-permute-start(bf16[3,64,128]{2,1,0:T(8,128)(2,1)S(1)} %get-tuple-element.67), channel_id=1, source_target_pairs={{0,64},{64,128},{128,192},{192,256},{256,320},{320,384},{384,448},... | collective-permute-start | bytes 147464 | tf_op jit(solution)/shard_map/ppermute | solution.py:567
  117.2 1.9 %collective-permute-start.5 = (bf16[3,64,128]{2,1,0:T(8,128)(2,1)S(1)}, bf16[3,64,128]{2,1,0:T(8,128)(2,1)S(1)}, u32[]{:S(2)}, u32[]{:S(2)}) collective-permute-start(bf16[3,64,128]{2,1,0:T(8,128)(2,1)S(1)} %get-tuple-element.66), channel_id=1, source_target_pairs={{64,0},{128,64},{192,128},{256,192},{320,256},{384,320},{448,384},... | collective-permute-start | bytes 147464 | tf_op jit(solution)/shard_map/ppermute | solution.py:567
  119.2 3.6 %collective-permute-done.5.down = bf16[3,64,128]{2,1,0:T(8,128)(2,1)S(1)} collective-permute-done((bf16[3,64,128]{2,1,0:T(8,128)(2,1)S(1)}, bf16[3,64,128]{2,1,0:T(8,128)(2,1)S(1)}, u32[]{:S(2)}, u32[]{:S(2)}) %collective-permute-start.5) | collective-permute-done | bytes 49184 | tf_op jit(solution)/shard_map/ppermute | solution.py:567
  122.7 0.4 edges.3
  123.1 2.6 %collective-permute-start.6 = (bf16[64,128]{1,0:T(8,128)(2,1)S(1)}, bf16[64,128]{1,0:T(8,128)(2,1)S(1)}, u32[]{:S(2)}, u32[]{:S(2)}) collective-permute-start(bf16[64,128]{1,0:T(8,128)(2,1)S(1)} %get-tuple-element.42), channel_id=1, source_target_pairs={{0,4},{4,8},{8,12},{12,16},{16,20},{20,24},{24,28},{28,32},{32,36}... | collective-permute-start | bytes 49160 | tf_op jit(solution)/shard_map/ppermute | solution.py:567
  125.7 1.3 collective-permute-start.7
  127.0 0.7 copy.20
  127.7 2.5 %collective-permute-done.7.right = bf16[64,128]{1,0:T(8,128)(2,1)S(1)} collective-permute-done((bf16[64,128]{1,0:T(8,128)(2,1)S(1)}, bf16[64,128]{1,0:T(8,128)(2,1)S(1)}, u32[]{:S(2)}, u32[]{:S(2)}) %collective-permute-start.7) | collective-permute-done | bytes 16416 | tf_op jit(solution)/shard_map/ppermute | solution.py:567
  130.2 1.7 %backward.1 = bf16[4,64,128]{2,1,0:T(8,128)(2,1)S(1)} custom-call(bf16[3,64,128]{2,1,0:T(8,128)(2,1)S(1)} %collective-permute-done.4.up, bf16[4,64,128]{2,1,0:T(8,128)(2,1)S(1)} %get-tuple-element.41.mid, bf16[3,64,128]{2,1,0:T(8,128)(2,1)S(1)} %collective-permute-done.5.down, bf16[64,128]{1,0:T(8,128)(2,1)S(1)} %collective-permute-done.6.left, ...), custom_call_target="tpu_custom_call" | custom-call | tf_op jit(solution)/shard_map/backward/pallas_call | solution.py:29
  131.9 0.7 copy.21
  132.5 1.0 final.1
  (15 shorter events, 0.1 us)
Async XLA Ops:
  1.5 10.2 %collective-permute-start = (bf16[3,64,128]{2,1,0:T(8,128)(2,1)S(1)}, bf16[3,64,128]{2,1,0:T(8,128)(2,1)S(1)}, u32[]{:S(2)}, u32[]{:S(2)}) collective-permute-start(bf16[3,64,128]{2,1,0:T(8,128)(2,1)S(1)} %get-tuple-element.69), channel_id=1, source_target_pairs={{0,64},{64,128},{128,192},{192,256},{256,320},{320,384},{384,448},... | collective-permute-start | bytes 147464 | tf_op jit(solution)/shard_map/ppermute | solution.py:567
  6.1 10.8 %copy-start.4 = (bf16[64,4,128]{2,1,0:T(4,128)(2,1)S(1)}, bf16[64,4,128]{2,1,0:T(4,128)(2,1)}, u32[]{:S(2)}) copy-start(bf16[64,4,128]{2,1,0:T(4,128)(2,1)} %param.15) | copy-start | bytes 196612
  6.1 6.5 %collective-permute-start.1 = (bf16[3,64,128]{2,1,0:T(8,128)(2,1)S(1)}, bf16[3,64,128]{2,1,0:T(8,128)(2,1)S(1)}, u32[]{:S(2)}, u32[]{:S(2)}) collective-permute-start(bf16[3,64,128]{2,1,0:T(8,128)(2,1)S(1)} %get-tuple-element.68), channel_id=1, source_target_pairs={{64,0},{128,64},{192,128},{256,192},{320,256},{384,320},{448,384},... | collective-permute-start | bytes 147464 | tf_op jit(solution)/shard_map/ppermute | solution.py:567
  12.9 4.1 %collective-permute-start.2 = (bf16[64,128]{1,0:T(8,128)(2,1)S(1)}, bf16[64,128]{1,0:T(8,128)(2,1)S(1)}, u32[]{:S(2)}, u32[]{:S(2)}) collective-permute-start(bf16[64,128]{1,0:T(8,128)(2,1)S(1)} %get-tuple-element.33), channel_id=1, source_target_pairs={{0,4},{4,8},{8,12},{12,16},{16,20},{20,24},{24,28},{28,32},{32,36}... | collective-permute-start | bytes 49160 | tf_op jit(solution)/shard_map/ppermute | solution.py:567
  15.6 1.3 %copy-start.5 = (f32[64,49]{0,1:T(8,128)S(1)}, f32[64,49]{0,1:T(8,128)}, u32[]{:S(2)}) copy-start(f32[64,49]{0,1:T(8,128)} %param.9) | copy-start | bytes 37636
  15.6 4.7 %collective-permute-start.3 = (bf16[64,128]{1,0:T(8,128)(2,1)S(1)}, bf16[64,128]{1,0:T(8,128)(2,1)S(1)}, u32[]{:S(2)}, u32[]{:S(2)}) collective-permute-start(bf16[64,128]{1,0:T(8,128)(2,1)S(1)} %get-tuple-element.34), channel_id=1, source_target_pairs={{4,0},{8,4},{12,8},{16,12},{20,16},{24,20},{28,24},{32,28},{36,32}... | collective-permute-start | bytes 49160 | tf_op jit(solution)/shard_map/ppermute | solution.py:567
  20.3 0.7 copy-start.2
  20.3 0.7 copy-start.3
  23.6 14.7 %copy-start = (bf16[256,256]{1,0:T(8,128)(2,1)S(1)}, bf16[256,256]{1,0:T(8,128)(2,1)}, u32[]{:S(2)}) copy-start(bf16[256,256]{1,0:T(8,128)(2,1)} %w_exp.1) | copy-start | bytes 393220
  23.6 14.7 %copy-start.1 = (bf16[256,256]{1,0:T(8,128)(2,1)S(1)}, bf16[256,256]{1,0:T(8,128)(2,1)}, u32[]{:S(2)}) copy-start(bf16[256,256]{1,0:T(8,128)(2,1)} %w_red.1) | copy-start | bytes 393220
  23.6 14.6 %all-to-all-start = ((bf16[4,144,512]{2,1,0:T(8,128)(2,1)}), bf16[4,144,512]{2,1,0:T(8,128)(2,1)S(1)}, u32[]{:S(2)}, u32[]{:S(2)}) async-start(bf16[4,144,512]{2,1,0:T(8,128)(2,1)} %get-tuple-element.35), calls=%async_computation | async-start | bytes 1179648 | tf_op jit(solution)/shard_map/all_to_all | solution.py:579
  40.4 16.7 %all-to-all-start.1 = ((bf16[4,144,512]{2,1,0:T(8,128)(2,1)}), bf16[4,144,512]{2,1,0:T(8,128)(2,1)S(1)}, u32[]{:S(2)}, u32[]{:S(2)}) async-start(bf16[4,144,512]{2,1,0:T(8,128)(2,1)} %get-tuple-element.36), calls=%async_computation.1 | async-start | bytes 1179648 | tf_op jit(solution)/shard_map/all_to_all | solution.py:579
  43.9 3.5 %collective-permute-start.8 = (f32[512,128]{1,0:T(8,128)S(1)}, f32[512,128]{1,0:T(8,128)S(1)}, u32[]{:S(2)}, u32[]{:S(2)}) collective-permute-start(f32[512,128]{1,0:T(8,128)S(1)} %get-tuple-element.47), channel_id=1, source_target_pairs={{0,64},{64,0},{128,192},{192,128},{256,320},{320,256},{384,448},{4... | collective-permute-start | bytes 786440 | tf_op jit(solution)/shard_map/ppermute | solution.py:242
  47.4 9.9 %collective-permute-start.10 = (f32[128,128]{1,0:T(8,128)S(1)}, f32[128,128]{1,0:T(8,128)S(1)}, u32[]{:S(2)}, u32[]{:S(2)}) collective-permute-start(f32[128,128]{1,0:T(8,128)S(1)} %get-tuple-element.50), channel_id=1, source_target_pairs={{0,256},{64,320},{128,384},{192,448},{256,0},{320,64},{384,128},{4... | collective-permute-start | bytes 196616 | tf_op jit(solution)/shard_map/ppermute | solution.py:247
  52.2 6.2 %collective-permute-start.11 = (f32[128,128]{1,0:T(8,128)S(1)}, f32[128,128]{1,0:T(8,128)S(1)}, u32[]{:S(2)}, u32[]{:S(2)}) collective-permute-start(f32[128,128]{1,0:T(8,128)S(1)} %get-tuple-element.51), channel_id=1, source_target_pairs={{0,384},{64,448},{128,256},{192,320},{256,128},{320,192},{384,0},{... | collective-permute-start | bytes 196616 | tf_op jit(solution)/shard_map/ppermute | solution.py:247
  55.2 5.0 %collective-permute-start.9 = (f32[128,128]{1,0:T(8,128)S(1)}, f32[128,128]{1,0:T(8,128)S(1)}, u32[]{:S(2)}, u32[]{:S(2)}) collective-permute-start(f32[128,128]{1,0:T(8,128)S(1)} %get-tuple-element.49), channel_id=1, source_target_pairs={{0,128},{64,192},{128,0},{192,64},{256,384},{320,448},{384,256},{4... | collective-permute-start | bytes 196616 | tf_op jit(solution)/shard_map/ppermute | solution.py:247
  105.6 27.0 %all-to-all-start.4 = ((bf16[8,192,128]{2,1,0:T(8,128)(2,1)}), bf16[8,192,128]{2,1,0:T(8,128)(2,1)S(1)}, u32[]{:S(2)}, u32[]{:S(2)}) async-start(bf16[8,192,128]{2,1,0:T(8,128)(2,1)} %row_pack.1), calls=%async_computation.4 | async-start | bytes 786432 | tf_op jit(solution)/shard_map/all_to_all | solution.py:579
  113.7 5.5 %collective-permute-start.4 = (bf16[3,64,128]{2,1,0:T(8,128)(2,1)S(1)}, bf16[3,64,128]{2,1,0:T(8,128)(2,1)S(1)}, u32[]{:S(2)}, u32[]{:S(2)}) collective-permute-start(bf16[3,64,128]{2,1,0:T(8,128)(2,1)S(1)} %get-tuple-element.67), channel_id=1, source_target_pairs={{0,64},{64,128},{128,192},{192,256},{256,320},{320,384},{384,448},... | collective-permute-start | bytes 147464 | tf_op jit(solution)/shard_map/ppermute | solution.py:567
  117.2 5.5 %collective-permute-start.5 = (bf16[3,64,128]{2,1,0:T(8,128)(2,1)S(1)}, bf16[3,64,128]{2,1,0:T(8,128)(2,1)S(1)}, u32[]{:S(2)}, u32[]{:S(2)}) collective-permute-start(bf16[3,64,128]{2,1,0:T(8,128)(2,1)S(1)} %get-tuple-element.66), channel_id=1, source_target_pairs={{64,0},{128,64},{192,128},{256,192},{320,256},{384,320},{448,384},... | collective-permute-start | bytes 147464 | tf_op jit(solution)/shard_map/ppermute | solution.py:567
  123.1 4.5 %collective-permute-start.6 = (bf16[64,128]{1,0:T(8,128)(2,1)S(1)}, bf16[64,128]{1,0:T(8,128)(2,1)S(1)}, u32[]{:S(2)}, u32[]{:S(2)}) collective-permute-start(bf16[64,128]{1,0:T(8,128)(2,1)S(1)} %get-tuple-element.42), channel_id=1, source_target_pairs={{0,4},{4,8},{8,12},{12,16},{16,20},{20,24},{24,28},{28,32},{32,36}... | collective-permute-start | bytes 49160 | tf_op jit(solution)/shard_map/ppermute | solution.py:567
  125.7 4.5 %collective-permute-start.7 = (bf16[64,128]{1,0:T(8,128)(2,1)S(1)}, bf16[64,128]{1,0:T(8,128)(2,1)S(1)}, u32[]{:S(2)}, u32[]{:S(2)}) collective-permute-start(bf16[64,128]{1,0:T(8,128)(2,1)S(1)} %get-tuple-element.43), channel_id=1, source_target_pairs={{4,0},{8,4},{12,8},{16,12},{20,16},{24,20},{28,24},{32,28},{36,32}... | collective-permute-start | bytes 49160 | tf_op jit(solution)/shard_map/ppermute | solution.py:567

commit v7 on v5

--- a/solution.py
+++ b/solution.py
@@ -219,14 +219,14 @@
         low, high = y % 2, y // 2
         low = 1 - low if m % 2 else low
         high = 1 - high if m // 2 else high
-        out[...] = total[pl.ds(pl.multiple_of((2 * high + low) * n, n), n), :]
+        out[...] = total[pl.ds(pl.multiple_of((2 * high + low) * n, n), n), :].astype(out.dtype)
 
 
 def spread(x, recv, parts):
-    shape = jax.ShapeDtypeStruct((x.shape[0] // parts, LANES), f32)
+    shape = (x.shape[0] // parts, LANES)
     return vcall(
         spread_kernel,
-        out_shape=(shape,) * parts,
+        out_shape=tuple(jax.ShapeDtypeStruct(shape, bf16 if m else f32) for m in range(parts)),
         scratch_shapes=[pltpu.VMEM(x.shape, f32)],
         name="spread",
     )(x, recv)
@@ -418,7 +418,7 @@
     per = total.shape[0] // cols
     for c in range(cols):
         at = slice(c * part, (c + 1) * part)
-        out[c, 0:part, :] = sum(x[at, :] for x in pieces)
+        out[c, 0:part, :] = sum(x[at, :].astype(f32) for x in pieces)
         out[c, part : part + per, :] = total[c * per : (c + 1) * per, :]
         out[c, part + per :, :] = jnp.zeros((height - part - per, LANES), f32)
 

time: 135 us -> 134 us (level)
  no operation moved by 1% of the time
where the time goes in v7:
time: 134 us; the launch traced here: 133 us
  starting transfers between devices  51 us (38%)
  blocking collectives  41.8 us (31%)
  waiting for transfers between devices  23.6 us (18%)
  Pallas kernels  12.5 us (9%)
  local copies, waits for them, and re-layouts  3.79 us (3%)
    all_to_all x2, blocking collectives, exchange(): return lax.all_to_all(x, axis, 0, 0)  41.8 us
    ppermute x8, starting transfers between devices, neighbours(): return (lax.ppermute(last, axis, up), lax.ppermute(first, axis, down))  23.3 us
    all_to_all x3, starting transfers between devices, exchange(): return lax.all_to_all(x, axis, 0, 0)  15.7 us
    pallas_call x11, Pallas kernels, call(): pl.pallas_call(kernel, out_shape=out_shape, in_specs=[spec] * len(args),...  12.5 us
    ppermute x8, waiting for transfers between devices, neighbours(): return (lax.ppermute(last, axis, up), lax.ppermute(first, axis, down))  10.2 us
    all_to_all x3, waiting for transfers between devices, exchange(): return lax.all_to_all(x, axis, 0, 0)  9.72 us
    ppermute x3, starting transfers between devices, reduce_rows(): lax.ppermute(chunks[m], 'row', [(i, i ^ 2 * m) for i in range(size)])  9.69 us
    unnamed x17, local copies, waits for them, and re-layouts  3 us
  transfers between devices with their start and end apart: 15, of which 8 were waited for; matrix products, arithmetic and copies ran while one was open for 2% of the time, Pallas kernels for 2%

profile of v7, /device:TPU:1, one launch (start us, length us, event | category | flops | bytes accessed | tf_op | source)
XLA Modules:
  0.0 133.5 jit_solution(6503344868931134015)
XLA Ops:
  0.6 0.9 copy.25
  1.5 4.6 %collective-permute-start = (bf16[3,64,128]{2,1,0:T(8,128)(2,1)S(1)}, bf16[3,64,128]{2,1,0:T(8,128)(2,1)S(1)}, u32[]{:S(2)}, u32[]{:S(2)}) collective-permute-start(bf16[3,64,128]{2,1,0:T(8,128)(2,1)S(1)} %get-tuple-element.71), channel_id=1, source_target_pairs={{0,64},{64,128},{128,192},{192,256},{256,320},{320,384},{384,448},... | collective-permute-start | bytes 147464 | tf_op jit(solution)/shard_map/ppermute | solution.py:562
  6.1 5.5 %collective-permute-start.1 = (bf16[3,64,128]{2,1,0:T(8,128)(2,1)S(1)}, bf16[3,64,128]{2,1,0:T(8,128)(2,1)S(1)}, u32[]{:S(2)}, u32[]{:S(2)}) collective-permute-start(bf16[3,64,128]{2,1,0:T(8,128)(2,1)S(1)} %get-tuple-element.70), channel_id=1, source_target_pairs={{64,0},{128,64},{192,128},{256,192},{320,256},{384,320},{448,384},... | collective-permute-start | bytes 147464 | tf_op jit(solution)/shard_map/ppermute | solution.py:562
  11.6 0.0 collective-permute-done.up
  11.6 0.8 collective-permute-done.1.down
  12.4 0.7 copy-done.2
  13.1 0.0 copy-done.3
  13.1 0.4 edges.2
  13.5 2.6 %collective-permute-start.2 = (bf16[64,128]{1,0:T(8,128)(2,1)S(1)}, bf16[64,128]{1,0:T(8,128)(2,1)S(1)}, u32[]{:S(2)}, u32[]{:S(2)}) collective-permute-start(bf16[64,128]{1,0:T(8,128)(2,1)S(1)} %get-tuple-element.34), channel_id=1, source_target_pairs={{0,4},{4,8},{8,12},{12,16},{16,20},{20,24},{24,28},{28,32},{32,36}... | collective-permute-start | bytes 49160 | tf_op jit(solution)/shard_map/ppermute | solution.py:562
  16.2 0.0 copy-start.5
  16.2 1.3 collective-permute-start.3
  17.5 0.1 copy.18.kern
  17.6 0.0 collective-permute-done.2.left
  17.6 3.2 %collective-permute-done.3.right = bf16[64,128]{1,0:T(8,128)(2,1)S(1)} collective-permute-done((bf16[64,128]{1,0:T(8,128)(2,1)S(1)}, bf16[64,128]{1,0:T(8,128)(2,1)S(1)}, u32[]{:S(2)}, u32[]{:S(2)}) %collective-permute-start.3) | collective-permute-done | bytes 16416 | tf_op jit(solution)/shard_map/ppermute | solution.py:562
  20.9 2.6 %forward.1 = (f32[64,512]{1,0:T(8,128)S(1)}, bf16[4,144,512]{2,1,0:T(8,128)(2,1)}) custom-call(bf16[3,64,128]{2,1,0:T(8,128)(2,1)S(1)} %collective-permute-done.up, bf16[4,64,128]{2,1,0:T(8,128)(2,1)S(1)} %bitcast.17, bf16[3,64,128]{2,1,0:T(8,128)(2,1)S(1)} %collective-permute-done.1.down, bf16[64,128]{1,0:T(8,128)(2,1)S(1)} %collective-permute-done.2.left, ...), custom_call_target="tpu_custom_call" | custom-call | tf_op jit(solution)/shard_map/forward/pallas_call | solution.py:28
  23.5 4.1 %all-to-all-start = ((bf16[4,144,512]{2,1,0:T(8,128)(2,1)}), bf16[4,144,512]{2,1,0:T(8,128)(2,1)S(1)}, u32[]{:S(2)}, u32[]{:S(2)}) async-start(bf16[4,144,512]{2,1,0:T(8,128)(2,1)} %get-tuple-element.37), calls=%async_computation | async-start | bytes 1179648 | tf_op jit(solution)/shard_map/all_to_all | solution.py:574
  27.6 0.8 dynamic_slice.3
  28.4 9.7 %all-to-all-done.recv = bf16[4,144,512]{2,1,0:T(8,128)(2,1)S(1)} async-done(((bf16[4,144,512]{2,1,0:T(8,128)(2,1)}), bf16[4,144,512]{2,1,0:T(8,128)(2,1)S(1)}, u32[]{:S(2)}, u32[]{:S(2)}) %all-to-all-start) | async-done | bytes 589856 | tf_op jit(solution)/shard_map/all_to_all | solution.py:574
  38.1 2.1 %mlp.1 = (bf16[4,144,512]{2,1,0:T(8,128)(2,1)}, f32[2,512]{1,0:T(2,128)S(1)}, f32[512,128]{1,0:T(8,128)S(1)}, f32[512,128]{1,0:T(8,128)S(1)}, f32[64,128]{1,0:T(8,128)S(1)}) custom-call(bf16[4,144,512]{2,1,0:T(8,128)(2,1)S(1)} %all-to-all-done.recv, bf16[256,256]{1,0:T(8,128)(2,1)S(1)} %copy-done, f32[1,256]{1,0:T(1,128)S(1)} %bitcast.27, ...), custom_call_target="tpu_custom_call" | custom-call | tf_op jit(solution)/shard_map/mlp/pallas_call | solution.py:28
  40.2 3.5 %all-to-all-start.1 = ((bf16[4,144,512]{2,1,0:T(8,128)(2,1)}), bf16[4,144,512]{2,1,0:T(8,128)(2,1)S(1)}, u32[]{:S(2)}, u32[]{:S(2)}) async-start(bf16[4,144,512]{2,1,0:T(8,128)(2,1)} %get-tuple-element.38), calls=%async_computation.1 | async-start | bytes 1179648 | tf_op jit(solution)/shard_map/all_to_all | solution.py:574
  43.7 2.3 %collective-permute-start.8 = (f32[512,128]{1,0:T(8,128)S(1)}, f32[512,128]{1,0:T(8,128)S(1)}, u32[]{:S(2)}, u32[]{:S(2)}) collective-permute-start(f32[512,128]{1,0:T(8,128)S(1)} %get-tuple-element.49), channel_id=1, source_target_pairs={{0,64},{64,0},{128,192},{192,128},{256,320},{320,256},{384,448},{4... | collective-permute-start | bytes 786440 | tf_op jit(solution)/shard_map/ppermute | solution.py:237
  46.0 1.1 collective-permute-done.8.recv
  47.2 4.8 %collective-permute-start.10 = (bf16[128,128]{1,0:T(8,128)(2,1)S(1)}, bf16[128,128]{1,0:T(8,128)(2,1)S(1)}, u32[]{:S(2)}, u32[]{:S(2)}) collective-permute-start(bf16[128,128]{1,0:T(8,128)(2,1)S(1)} %get-tuple-element.52), channel_id=1, source_target_pairs={{0,256},{64,320},{128,384},{192,448},{256,0},{320,64},{384,128},{4... | collective-permute-start | bytes 98312 | tf_op jit(solution)/shard_map/ppermute | solution.py:242
  52.0 3.0 %collective-permute-start.11 = (bf16[128,128]{1,0:T(8,128)(2,1)S(1)}, bf16[128,128]{1,0:T(8,128)(2,1)S(1)}, u32[]{:S(2)}, u32[]{:S(2)}) collective-permute-start(bf16[128,128]{1,0:T(8,128)(2,1)S(1)} %get-tuple-element.53), channel_id=1, source_target_pairs={{0,384},{64,448},{128,256},{192,320},{256,128},{320,192},{384,0},{... | collective-permute-start | bytes 98312 | tf_op jit(solution)/shard_map/ppermute | solution.py:242
  55.0 1.9 %collective-permute-start.9 = (bf16[128,128]{1,0:T(8,128)(2,1)S(1)}, bf16[128,128]{1,0:T(8,128)(2,1)S(1)}, u32[]{:S(2)}, u32[]{:S(2)}) collective-permute-start(bf16[128,128]{1,0:T(8,128)(2,1)S(1)} %get-tuple-element.51), channel_id=1, source_target_pairs={{0,128},{64,192},{128,0},{192,64},{256,384},{320,448},{384,256},{4... | collective-permute-start | bytes 98312 | tf_op jit(solution)/shard_map/ppermute | solution.py:242
  56.9 0.1 norm_back.1
  57.1 0.0 collective-permute-done.10.rest_2_
  57.1 0.8 collective-permute-done.11.rest_3_
  57.9 1.8 %collective-permute-done.9.rest_1_ = bf16[128,128]{1,0:T(8,128)(2,1)S(1)} collective-permute-done((bf16[128,128]{1,0:T(8,128)(2,1)S(1)}, bf16[128,128]{1,0:T(8,128)(2,1)S(1)}, u32[]{:S(2)}, u32[]{:S(2)}) %collective-permute-start.9) | collective-permute-done | bytes 32800 | tf_op jit(solution)/shard_map/ppermute | solution.py:242
  59.7 2.8 %tap_grad.1 = f32[16,16,128]{2,1,0:T(8,128)S(1)} custom-call(bf16[3,64,128]{2,1,0:T(8,128)(2,1)S(1)} %collective-permute-done.up, bf16[4,64,128]{2,1,0:T(8,128)(2,1)S(1)} %bitcast.19, bf16[3,64,128]{2,1,0:T(8,128)(2,1)S(1)} %collective-permute-done.1.down, bf16[64,128]{1,0:T(8,128)(2,1)S(1)} %collective-permute-done.2.left, ...), custom_call_target="tpu_custom_call" | custom-call | tf_op jit(solution)/shard_map/tap_grad/pallas_call | solution.py:28
  62.4 26.4 %all_to_all.25.recv = f32[16,16,128]{2,1,0:T(8,128)S(1)} all-to-all(f32[16,16,128]{2,1,0:T(8,128)S(1)} %tap_grad.1), channel_id=1, replica_groups=mesh['row'=8,'col'=16,'ch'=4] {'col'}, dimensions={0} | all-to-all | bytes 262144 | tf_op jit(solution)/shard_map/all_to_all | solution.py:574
  88.8 15.4 %all_to_all.26.recv = bf16[16,16,128]{2,1,0:T(8,128)(2,1)S(1)} all-to-all(bf16[16,16,128]{2,1,0:T(8,128)(2,1)S(1)} %col_pack.1), channel_id=1, replica_groups=mesh['row'=8,'col'=16,'ch'=4] {'col'}, dimensions={0} | all-to-all | bytes 131072 | tf_op jit(solution)/shard_map/all_to_all | solution.py:574
  104.2 0.8 row_pack.1
  105.0 8.1 %all-to-all-start.4 = ((bf16[8,192,128]{2,1,0:T(8,128)(2,1)}), bf16[8,192,128]{2,1,0:T(8,128)(2,1)S(1)}, u32[]{:S(2)}, u32[]{:S(2)}) async-start(bf16[8,192,128]{2,1,0:T(8,128)(2,1)} %row_pack.1), calls=%async_computation.4 | async-start | bytes 786432 | tf_op jit(solution)/shard_map/all_to_all | solution.py:574
  113.1 3.5 %collective-permute-start.4 = (bf16[3,64,128]{2,1,0:T(8,128)(2,1)S(1)}, bf16[3,64,128]{2,1,0:T(8,128)(2,1)S(1)}, u32[]{:S(2)}, u32[]{:S(2)}) collective-permute-start(bf16[3,64,128]{2,1,0:T(8,128)(2,1)S(1)} %get-tuple-element.69), channel_id=1, source_target_pairs={{0,64},{64,128},{128,192},{192,256},{256,320},{320,384},{384,448},... | collective-permute-start | bytes 147464 | tf_op jit(solution)/shard_map/ppermute | solution.py:562
  116.7 1.9 %collective-permute-start.5 = (bf16[3,64,128]{2,1,0:T(8,128)(2,1)S(1)}, bf16[3,64,128]{2,1,0:T(8,128)(2,1)S(1)}, u32[]{:S(2)}, u32[]{:S(2)}) collective-permute-start(bf16[3,64,128]{2,1,0:T(8,128)(2,1)S(1)} %get-tuple-element.68), channel_id=1, source_target_pairs={{64,0},{128,64},{192,128},{256,192},{320,256},{384,320},{448,384},... | collective-permute-start | bytes 147464 | tf_op jit(solution)/shard_map/ppermute | solution.py:562
  118.6 0.0 collective-permute-done.4.up
  118.6 3.6 %collective-permute-done.5.down = bf16[3,64,128]{2,1,0:T(8,128)(2,1)S(1)} collective-permute-done((bf16[3,64,128]{2,1,0:T(8,128)(2,1)S(1)}, bf16[3,64,128]{2,1,0:T(8,128)(2,1)S(1)}, u32[]{:S(2)}, u32[]{:S(2)}) %collective-permute-start.5) | collective-permute-done | bytes 49184 | tf_op jit(solution)/shard_map/ppermute | solution.py:562
  122.2 0.9 edges.3
  123.1 2.5 %collective-permute-start.6 = (bf16[64,128]{1,0:T(8,128)(2,1)S(1)}, bf16[64,128]{1,0:T(8,128)(2,1)S(1)}, u32[]{:S(2)}, u32[]{:S(2)}) collective-permute-start(bf16[64,128]{1,0:T(8,128)(2,1)S(1)} %get-tuple-element.44), channel_id=1, source_target_pairs={{0,4},{4,8},{8,12},{12,16},{16,20},{20,24},{24,28},{28,32},{32,36}... | collective-permute-start | bytes 49160 | tf_op jit(solution)/shard_map/ppermute | solution.py:562
  125.6 1.3 collective-permute-start.7
  126.9 0.7 copy.20
  127.6 0.0 collective-permute-done.6.left
  127.6 2.5 %collective-permute-done.7.right = bf16[64,128]{1,0:T(8,128)(2,1)S(1)} collective-permute-done((bf16[64,128]{1,0:T(8,128)(2,1)S(1)}, bf16[64,128]{1,0:T(8,128)(2,1)S(1)}, u32[]{:S(2)}, u32[]{:S(2)}) %collective-permute-start.7) | collective-permute-done | bytes 16416 | tf_op jit(solution)/shard_map/ppermute | solution.py:562
  130.1 1.7 %backward.1 = bf16[4,64,128]{2,1,0:T(8,128)(2,1)S(1)} custom-call(bf16[3,64,128]{2,1,0:T(8,128)(2,1)S(1)} %collective-permute-done.4.up, bf16[4,64,128]{2,1,0:T(8,128)(2,1)S(1)} %get-tuple-element.43.mid, bf16[3,64,128]{2,1,0:T(8,128)(2,1)S(1)} %collective-permute-done.5.down, bf16[64,128]{1,0:T(8,128)(2,1)S(1)} %collective-permute-done.6.left, ...), custom_call_target="tpu_custom_call" | custom-call | tf_op jit(solution)/shard_map/backward/pallas_call | solution.py:28
  131.8 0.7 copy.21
  132.5 0.0 all-to-all-done.4.flat
  132.5 1.0 final.1
  (15 shorter events, 0.1 us)
Async XLA Ops:
  1.5 10.1 %collective-permute-start = (bf16[3,64,128]{2,1,0:T(8,128)(2,1)S(1)}, bf16[3,64,128]{2,1,0:T(8,128)(2,1)S(1)}, u32[]{:S(2)}, u32[]{:S(2)}) collective-permute-start(bf16[3,64,128]{2,1,0:T(8,128)(2,1)S(1)} %get-tuple-element.71), channel_id=1, source_target_pairs={{0,64},{64,128},{128,192},{192,256},{256,320},{320,384},{384,448},... | collective-permute-start | bytes 147464 | tf_op jit(solution)/shard_map/ppermute | solution.py:562
  6.1 6.3 %collective-permute-start.1 = (bf16[3,64,128]{2,1,0:T(8,128)(2,1)S(1)}, bf16[3,64,128]{2,1,0:T(8,128)(2,1)S(1)}, u32[]{:S(2)}, u32[]{:S(2)}) collective-permute-start(bf16[3,64,128]{2,1,0:T(8,128)(2,1)S(1)} %get-tuple-element.70), channel_id=1, source_target_pairs={{64,0},{128,64},{192,128},{256,192},{320,256},{384,320},{448,384},... | collective-permute-start | bytes 147464 | tf_op jit(solution)/shard_map/ppermute | solution.py:562
  12.4 0.7 copy-start.2
  12.4 0.7 copy-start.3
  13.1 4.4 %copy-start.4 = (bf16[64,4,128]{2,1,0:T(4,128)(2,1)S(1)}, bf16[64,4,128]{2,1,0:T(4,128)(2,1)}, u32[]{:S(2)}) copy-start(bf16[64,4,128]{2,1,0:T(4,128)(2,1)} %param.15) | copy-start | bytes 196612
  13.5 4.1 %collective-permute-start.2 = (bf16[64,128]{1,0:T(8,128)(2,1)S(1)}, bf16[64,128]{1,0:T(8,128)(2,1)S(1)}, u32[]{:S(2)}, u32[]{:S(2)}) collective-permute-start(bf16[64,128]{1,0:T(8,128)(2,1)S(1)} %get-tuple-element.34), channel_id=1, source_target_pairs={{0,4},{4,8},{8,12},{12,16},{16,20},{20,24},{24,28},{28,32},{32,36}... | collective-permute-start | bytes 49160 | tf_op jit(solution)/shard_map/ppermute | solution.py:562
  16.2 1.3 %copy-start.5 = (f32[64,49]{0,1:T(8,128)S(1)}, f32[64,49]{0,1:T(8,128)}, u32[]{:S(2)}) copy-start(f32[64,49]{0,1:T(8,128)} %param.9) | copy-start | bytes 37636
  16.2 4.7 %collective-permute-start.3 = (bf16[64,128]{1,0:T(8,128)(2,1)S(1)}, bf16[64,128]{1,0:T(8,128)(2,1)S(1)}, u32[]{:S(2)}, u32[]{:S(2)}) collective-permute-start(bf16[64,128]{1,0:T(8,128)(2,1)S(1)} %get-tuple-element.35), channel_id=1, source_target_pairs={{4,0},{8,4},{12,8},{16,12},{20,16},{24,20},{28,24},{32,28},{36,32}... | collective-permute-start | bytes 49160 | tf_op jit(solution)/shard_map/ppermute | solution.py:562
  23.5 14.6 %copy-start = (bf16[256,256]{1,0:T(8,128)(2,1)S(1)}, bf16[256,256]{1,0:T(8,128)(2,1)}, u32[]{:S(2)}) copy-start(bf16[256,256]{1,0:T(8,128)(2,1)} %w_exp.1) | copy-start | bytes 393220
  23.5 14.6 %copy-start.1 = (bf16[256,256]{1,0:T(8,128)(2,1)S(1)}, bf16[256,256]{1,0:T(8,128)(2,1)}, u32[]{:S(2)}) copy-start(bf16[256,256]{1,0:T(8,128)(2,1)} %w_red.1) | copy-start | bytes 393220
  23.5 14.6 %all-to-all-start = ((bf16[4,144,512]{2,1,0:T(8,128)(2,1)}), bf16[4,144,512]{2,1,0:T(8,128)(2,1)S(1)}, u32[]{:S(2)}, u32[]{:S(2)}) async-start(bf16[4,144,512]{2,1,0:T(8,128)(2,1)} %get-tuple-element.37), calls=%async_computation | async-start | bytes 1179648 | tf_op jit(solution)/shard_map/all_to_all | solution.py:574
  40.2 16.7 %all-to-all-start.1 = ((bf16[4,144,512]{2,1,0:T(8,128)(2,1)}), bf16[4,144,512]{2,1,0:T(8,128)(2,1)S(1)}, u32[]{:S(2)}, u32[]{:S(2)}) async-start(bf16[4,144,512]{2,1,0:T(8,128)(2,1)} %get-tuple-element.38), calls=%async_computation.1 | async-start | bytes 1179648 | tf_op jit(solution)/shard_map/all_to_all | solution.py:574
  43.7 3.5 %collective-permute-start.8 = (f32[512,128]{1,0:T(8,128)S(1)}, f32[512,128]{1,0:T(8,128)S(1)}, u32[]{:S(2)}, u32[]{:S(2)}) collective-permute-start(f32[512,128]{1,0:T(8,128)S(1)} %get-tuple-element.49), channel_id=1, source_target_pairs={{0,64},{64,0},{128,192},{192,128},{256,320},{320,256},{384,448},{4... | collective-permute-start | bytes 786440 | tf_op jit(solution)/shard_map/ppermute | solution.py:237
  47.2 9.9 %collective-permute-start.10 = (bf16[128,128]{1,0:T(8,128)(2,1)S(1)}, bf16[128,128]{1,0:T(8,128)(2,1)S(1)}, u32[]{:S(2)}, u32[]{:S(2)}) collective-permute-start(bf16[128,128]{1,0:T(8,128)(2,1)S(1)} %get-tuple-element.52), channel_id=1, source_target_pairs={{0,256},{64,320},{128,384},{192,448},{256,0},{320,64},{384,128},{4... | collective-permute-start | bytes 98312 | tf_op jit(solution)/shard_map/ppermute | solution.py:242
  52.0 5.9 %collective-permute-start.11 = (bf16[128,128]{1,0:T(8,128)(2,1)S(1)}, bf16[128,128]{1,0:T(8,128)(2,1)S(1)}, u32[]{:S(2)}, u32[]{:S(2)}) collective-permute-start(bf16[128,128]{1,0:T(8,128)(2,1)S(1)} %get-tuple-element.53), channel_id=1, source_target_pairs={{0,384},{64,448},{128,256},{192,320},{256,128},{320,192},{384,0},{... | collective-permute-start | bytes 98312 | tf_op jit(solution)/shard_map/ppermute | solution.py:242
  55.0 4.7 %collective-permute-start.9 = (bf16[128,128]{1,0:T(8,128)(2,1)S(1)}, bf16[128,128]{1,0:T(8,128)(2,1)S(1)}, u32[]{:S(2)}, u32[]{:S(2)}) collective-permute-start(bf16[128,128]{1,0:T(8,128)(2,1)S(1)} %get-tuple-element.51), channel_id=1, source_target_pairs={{0,128},{64,192},{128,0},{192,64},{256,384},{320,448},{384,256},{4... | collective-permute-start | bytes 98312 | tf_op jit(solution)/shard_map/ppermute | solution.py:242
  105.0 27.5 %all-to-all-start.4 = ((bf16[8,192,128]{2,1,0:T(8,128)(2,1)}), bf16[8,192,128]{2,1,0:T(8,128)(2,1)S(1)}, u32[]{:S(2)}, u32[]{:S(2)}) async-start(bf16[8,192,128]{2,1,0:T(8,128)(2,1)} %row_pack.1), calls=%async_computation.4 | async-start | bytes 786432 | tf_op jit(solution)/shard_map/all_to_all | solution.py:574
  113.1 5.5 %collective-permute-start.4 = (bf16[3,64,128]{2,1,0:T(8,128)(2,1)S(1)}, bf16[3,64,128]{2,1,0:T(8,128)(2,1)S(1)}, u32[]{:S(2)}, u32[]{:S(2)}) collective-permute-start(bf16[3,64,128]{2,1,0:T(8,128)(2,1)S(1)} %get-tuple-element.69), channel_id=1, source_target_pairs={{0,64},{64,128},{128,192},{192,256},{256,320},{320,384},{384,448},... | collective-permute-start | bytes 147464 | tf_op jit(solution)/shard_map/ppermute | solution.py:562
  116.7 5.5 %collective-permute-start.5 = (bf16[3,64,128]{2,1,0:T(8,128)(2,1)S(1)}, bf16[3,64,128]{2,1,0:T(8,128)(2,1)S(1)}, u32[]{:S(2)}, u32[]{:S(2)}) collective-permute-start(bf16[3,64,128]{2,1,0:T(8,128)(2,1)S(1)} %get-tuple-element.68), channel_id=1, source_target_pairs={{64,0},{128,64},{192,128},{256,192},{320,256},{384,320},{448,384},... | collective-permute-start | bytes 147464 | tf_op jit(solution)/shard_map/ppermute | solution.py:562
  123.1 4.5 %collective-permute-start.6 = (bf16[64,128]{1,0:T(8,128)(2,1)S(1)}, bf16[64,128]{1,0:T(8,128)(2,1)S(1)}, u32[]{:S(2)}, u32[]{:S(2)}) collective-permute-start(bf16[64,128]{1,0:T(8,128)(2,1)S(1)} %get-tuple-element.44), channel_id=1, source_target_pairs={{0,4},{4,8},{8,12},{12,16},{16,20},{20,24},{24,28},{28,32},{32,36}... | collective-permute-start | bytes 49160 | tf_op jit(solution)/shard_map/ppermute | solution.py:562
  125.6 4.5 %collective-permute-start.7 = (bf16[64,128]{1,0:T(8,128)(2,1)S(1)}, bf16[64,128]{1,0:T(8,128)(2,1)S(1)}, u32[]{:S(2)}, u32[]{:S(2)}) collective-permute-start(bf16[64,128]{1,0:T(8,128)(2,1)S(1)} %get-tuple-element.45), channel_id=1, source_target_pairs={{4,0},{8,4},{12,8},{16,12},{20,16},{24,20},{28,24},{32,28},{36,32}... | collective-permute-start | bytes 49160 | tf_op jit(solution)/shard_map/ppermute | solution.py:562

commit v8 on v7

--- a/solution.py
+++ b/solution.py
@@ -416,11 +416,14 @@
     cols, height, _ = out.shape
     part = pieces[0].shape[0] // cols
     per = total.shape[0] // cols
+    pad = height - part - 2 * per
     for c in range(cols):
         at = slice(c * part, (c + 1) * part)
-        out[c, 0:part, :] = sum(x[at, :].astype(f32) for x in pieces)
-        out[c, part : part + per, :] = total[c * per : (c + 1) * per, :]
-        out[c, part + per :, :] = jnp.zeros((height - part - per, LANES), f32)
+        big = sum(x[at, :].astype(f32) for x in pieces)
+        tile = [big, hi_lo(total[c * per : (c + 1) * per, :])]
+        if pad:
+            tile.append(jnp.zeros((pad, LANES), f32))
+        out[c] = jnp.concatenate(tile, axis=0).astype(bf16)
 
 
 def tap_grad(up, mid, down, left, right, grad_mixed, small, pieces, cols):
@@ -429,7 +432,7 @@
     height = part + -(-2 * per // 8) * 8
     return vcall(
         tap_grad_kernel,
-        out_shape=jax.ShapeDtypeStruct((cols, height, LANES), f32),
+        out_shape=jax.ShapeDtypeStruct((cols, height, LANES), bf16),
         scratch_shapes=[pltpu.VMEM((channels, LANES), f32), pltpu.VMEM((channels // 2, LANES), f32)],
         name="tap_grad",
     )(up, mid, down, left, right, grad_mixed, small, *pieces)
@@ -463,11 +466,11 @@
 
 
 def col_pack_kernel(per, recv, out):
-    total = recv[0]
+    total = recv[0].astype(f32)
     for c in range(1, recv.shape[0]):
-        total = total + recv[c]
+        total = total + recv[c].astype(f32)
     part = total.shape[0] - -(-2 * per // 8) * 8
-    tail = hi_lo(total[part : part + per])
+    tail = hi_lo(total[part : part + per] + total[part + per : part + 2 * per])
     pad = total.shape[0] - part - 2 * per
     pieces = [total[0:part], tail] + ([jnp.zeros((pad, LANES), f32)] if pad else [])
     tile = jnp.concatenate(pieces, axis=0).astype(bf16)

time: 134 us -> 133 us (level)
  blocking collectives: 41.8 us -> 40.4 us
    all_to_all x2, blocking collectives: 41.8 us -> 40.4 us  [exchange(): return lax.all_to_all(x, axis, 0, 0)]
where the time goes in v8:
time: 133 us; the launch traced here: 132 us
  starting transfers between devices  51 us (38%)
  blocking collectives  40.4 us (30%)
  waiting for transfers between devices  23.6 us (18%)
  Pallas kernels  12.5 us (9%)
  local copies, waits for them, and re-layouts  3.79 us (3%)
    all_to_all x2, blocking collectives, exchange(): return lax.all_to_all(x, axis, 0, 0)  40.4 us
    ppermute x8, starting transfers between devices, neighbours(): return (lax.ppermute(last, axis, up), lax.ppermute(first, axis, down))  23.3 us
    all_to_all x3, starting transfers between devices, exchange(): return lax.all_to_all(x, axis, 0, 0)  15.7 us
    pallas_call x11, Pallas kernels, call(): pl.pallas_call(kernel, out_shape=out_shape, in_specs=[spec] * len(args),...  12.5 us
    ppermute x8, waiting for transfers between devices, neighbours(): return (lax.ppermute(last, axis, up), lax.ppermute(first, axis, down))  10.2 us
    all_to_all x3, waiting for transfers between devices, exchange(): return lax.all_to_all(x, axis, 0, 0)  9.72 us
    ppermute x3, starting transfers between devices, reduce_rows(): lax.ppermute(chunks[m], 'row', [(i, i ^ 2 * m) for i in range(size)])  9.69 us
    unnamed x17, local copies, waits for them, and re-layouts  3 us
  transfers between devices with their start and end apart: 15, of which 8 were waited for; matrix products, arithmetic and copies ran while one was open for 2% of the time, Pallas kernels for 2%

profile of v8, /device:TPU:1, one launch (start us, length us, event | category | flops | bytes accessed | tf_op | source)
XLA Modules:
  0.0 132.1 jit_solution(655026827757725381)
XLA Ops:
  0.6 0.9 copy.25
  1.5 4.6 %collective-permute-start = (bf16[3,64,128]{2,1,0:T(8,128)(2,1)S(1)}, bf16[3,64,128]{2,1,0:T(8,128)(2,1)S(1)}, u32[]{:S(2)}, u32[]{:S(2)}) collective-permute-start(bf16[3,64,128]{2,1,0:T(8,128)(2,1)S(1)} %get-tuple-element.71), channel_id=1, source_target_pairs={{0,64},{64,128},{128,192},{192,256},{256,320},{320,384},{384,448},... | collective-permute-start | bytes 147464 | tf_op jit(solution)/shard_map/ppermute | solution.py:565
  6.1 5.5 %collective-permute-start.1 = (bf16[3,64,128]{2,1,0:T(8,128)(2,1)S(1)}, bf16[3,64,128]{2,1,0:T(8,128)(2,1)S(1)}, u32[]{:S(2)}, u32[]{:S(2)}) collective-permute-start(bf16[3,64,128]{2,1,0:T(8,128)(2,1)S(1)} %get-tuple-element.70), channel_id=1, source_target_pairs={{64,0},{128,64},{192,128},{256,192},{320,256},{384,320},{448,384},... | collective-permute-start | bytes 147464 | tf_op jit(solution)/shard_map/ppermute | solution.py:565
  11.6 0.0 collective-permute-done.up
  11.6 0.8 collective-permute-done.1.down
  12.4 0.7 copy-done.2
  13.1 0.0 copy-done.3
  13.1 0.4 edges.2
  13.5 2.6 %collective-permute-start.2 = (bf16[64,128]{1,0:T(8,128)(2,1)S(1)}, bf16[64,128]{1,0:T(8,128)(2,1)S(1)}, u32[]{:S(2)}, u32[]{:S(2)}) collective-permute-start(bf16[64,128]{1,0:T(8,128)(2,1)S(1)} %get-tuple-element.34), channel_id=1, source_target_pairs={{0,4},{4,8},{8,12},{12,16},{16,20},{20,24},{24,28},{28,32},{32,36}... | collective-permute-start | bytes 49160 | tf_op jit(solution)/shard_map/ppermute | solution.py:565
  16.2 0.0 copy-start.5
  16.2 1.3 collective-permute-start.3
  17.5 0.1 copy.18.kern
  17.6 0.0 collective-permute-done.2.left
  17.6 3.2 %collective-permute-done.3.right = bf16[64,128]{1,0:T(8,128)(2,1)S(1)} collective-permute-done((bf16[64,128]{1,0:T(8,128)(2,1)S(1)}, bf16[64,128]{1,0:T(8,128)(2,1)S(1)}, u32[]{:S(2)}, u32[]{:S(2)}) %collective-permute-start.3) | collective-permute-done | bytes 16416 | tf_op jit(solution)/shard_map/ppermute | solution.py:565
  20.9 2.6 %forward.1 = (f32[64,512]{1,0:T(8,128)S(1)}, bf16[4,144,512]{2,1,0:T(8,128)(2,1)}) custom-call(bf16[3,64,128]{2,1,0:T(8,128)(2,1)S(1)} %collective-permute-done.up, bf16[4,64,128]{2,1,0:T(8,128)(2,1)S(1)} %bitcast.17, bf16[3,64,128]{2,1,0:T(8,128)(2,1)S(1)} %collective-permute-done.1.down, bf16[64,128]{1,0:T(8,128)(2,1)S(1)} %collective-permute-done.2.left, ...), custom_call_target="tpu_custom_call" | custom-call | tf_op jit(solution)/shard_map/forward/pallas_call | solution.py:28
  23.5 4.1 %all-to-all-start = ((bf16[4,144,512]{2,1,0:T(8,128)(2,1)}), bf16[4,144,512]{2,1,0:T(8,128)(2,1)S(1)}, u32[]{:S(2)}, u32[]{:S(2)}) async-start(bf16[4,144,512]{2,1,0:T(8,128)(2,1)} %get-tuple-element.37), calls=%async_computation | async-start | bytes 1179648 | tf_op jit(solution)/shard_map/all_to_all | solution.py:577
  27.6 0.8 dynamic_slice.3
  28.4 9.7 %all-to-all-done.recv = bf16[4,144,512]{2,1,0:T(8,128)(2,1)S(1)} async-done(((bf16[4,144,512]{2,1,0:T(8,128)(2,1)}), bf16[4,144,512]{2,1,0:T(8,128)(2,1)S(1)}, u32[]{:S(2)}, u32[]{:S(2)}) %all-to-all-start) | async-done | bytes 589856 | tf_op jit(solution)/shard_map/all_to_all | solution.py:577
  38.1 2.1 %mlp.1 = (bf16[4,144,512]{2,1,0:T(8,128)(2,1)}, f32[2,512]{1,0:T(2,128)S(1)}, f32[512,128]{1,0:T(8,128)S(1)}, f32[512,128]{1,0:T(8,128)S(1)}, f32[64,128]{1,0:T(8,128)S(1)}) custom-call(bf16[4,144,512]{2,1,0:T(8,128)(2,1)S(1)} %all-to-all-done.recv, bf16[256,256]{1,0:T(8,128)(2,1)S(1)} %copy-done, f32[1,256]{1,0:T(1,128)S(1)} %bitcast.27, ...), custom_call_target="tpu_custom_call" | custom-call | tf_op jit(solution)/shard_map/mlp/pallas_call | solution.py:28
  40.2 3.5 %all-to-all-start.1 = ((bf16[4,144,512]{2,1,0:T(8,128)(2,1)}), bf16[4,144,512]{2,1,0:T(8,128)(2,1)S(1)}, u32[]{:S(2)}, u32[]{:S(2)}) async-start(bf16[4,144,512]{2,1,0:T(8,128)(2,1)} %get-tuple-element.38), calls=%async_computation.1 | async-start | bytes 1179648 | tf_op jit(solution)/shard_map/all_to_all | solution.py:577
  43.7 2.3 %collective-permute-start.8 = (f32[512,128]{1,0:T(8,128)S(1)}, f32[512,128]{1,0:T(8,128)S(1)}, u32[]{:S(2)}, u32[]{:S(2)}) collective-permute-start(f32[512,128]{1,0:T(8,128)S(1)} %get-tuple-element.49), channel_id=1, source_target_pairs={{0,64},{64,0},{128,192},{192,128},{256,320},{320,256},{384,448},{4... | collective-permute-start | bytes 786440 | tf_op jit(solution)/shard_map/ppermute | solution.py:237
  46.0 1.1 collective-permute-done.8.recv
  47.2 4.8 %collective-permute-start.10 = (bf16[128,128]{1,0:T(8,128)(2,1)S(1)}, bf16[128,128]{1,0:T(8,128)(2,1)S(1)}, u32[]{:S(2)}, u32[]{:S(2)}) collective-permute-start(bf16[128,128]{1,0:T(8,128)(2,1)S(1)} %get-tuple-element.52), channel_id=1, source_target_pairs={{0,256},{64,320},{128,384},{192,448},{256,0},{320,64},{384,128},{4... | collective-permute-start | bytes 98312 | tf_op jit(solution)/shard_map/ppermute | solution.py:242
  52.0 3.0 %collective-permute-start.11 = (bf16[128,128]{1,0:T(8,128)(2,1)S(1)}, bf16[128,128]{1,0:T(8,128)(2,1)S(1)}, u32[]{:S(2)}, u32[]{:S(2)}) collective-permute-start(bf16[128,128]{1,0:T(8,128)(2,1)S(1)} %get-tuple-element.53), channel_id=1, source_target_pairs={{0,384},{64,448},{128,256},{192,320},{256,128},{320,192},{384,0},{... | collective-permute-start | bytes 98312 | tf_op jit(solution)/shard_map/ppermute | solution.py:242
  55.0 1.9 %collective-permute-start.9 = (bf16[128,128]{1,0:T(8,128)(2,1)S(1)}, bf16[128,128]{1,0:T(8,128)(2,1)S(1)}, u32[]{:S(2)}, u32[]{:S(2)}) collective-permute-start(bf16[128,128]{1,0:T(8,128)(2,1)S(1)} %get-tuple-element.51), channel_id=1, source_target_pairs={{0,128},{64,192},{128,0},{192,64},{256,384},{320,448},{384,256},{4... | collective-permute-start | bytes 98312 | tf_op jit(solution)/shard_map/ppermute | solution.py:242
  56.9 0.0 all-to-all-done.1.recv
  56.9 0.1 norm_back.1
  57.1 0.0 collective-permute-done.10.rest_2_
  57.1 0.8 collective-permute-done.11.rest_3_
  57.9 1.8 %collective-permute-done.9.rest_1_ = bf16[128,128]{1,0:T(8,128)(2,1)S(1)} collective-permute-done((bf16[128,128]{1,0:T(8,128)(2,1)S(1)}, bf16[128,128]{1,0:T(8,128)(2,1)S(1)}, u32[]{:S(2)}, u32[]{:S(2)}) %collective-permute-start.9) | collective-permute-done | bytes 32800 | tf_op jit(solution)/shard_map/ppermute | solution.py:242
  59.7 2.8 %tap_grad.1 = bf16[16,16,128]{2,1,0:T(8,128)(2,1)S(1)} custom-call(bf16[3,64,128]{2,1,0:T(8,128)(2,1)S(1)} %collective-permute-done.up, bf16[4,64,128]{2,1,0:T(8,128)(2,1)S(1)} %bitcast.19, bf16[3,64,128]{2,1,0:T(8,128)(2,1)S(1)} %collective-permute-done.1.down, bf16[64,128]{1,0:T(8,128)(2,1)S(1)} %collective-permute-done.2.left, ...), custom_call_target="tpu_custom_call" | custom-call | tf_op jit(solution)/shard_map/tap_grad/pallas_call | solution.py:28
  62.5 26.0 %all_to_all.25.recv = bf16[16,16,128]{2,1,0:T(8,128)(2,1)S(1)} all-to-all(bf16[16,16,128]{2,1,0:T(8,128)(2,1)S(1)} %tap_grad.1), channel_id=1, replica_groups=mesh['row'=8,'col'=16,'ch'=4] {'col'}, dimensions={0} | all-to-all | bytes 131072 | tf_op jit(solution)/shard_map/all_to_all | solution.py:577
  88.5 14.4 %all_to_all.26.recv = bf16[16,16,128]{2,1,0:T(8,128)(2,1)S(1)} all-to-all(bf16[16,16,128]{2,1,0:T(8,128)(2,1)S(1)} %col_pack.1), channel_id=1, replica_groups=mesh['row'=8,'col'=16,'ch'=4] {'col'}, dimensions={0} | all-to-all | bytes 131072 | tf_op jit(solution)/shard_map/all_to_all | solution.py:577
  102.9 0.8 row_pack.1
  103.7 8.1 %all-to-all-start.4 = ((bf16[8,192,128]{2,1,0:T(8,128)(2,1)}), bf16[8,192,128]{2,1,0:T(8,128)(2,1)S(1)}, u32[]{:S(2)}, u32[]{:S(2)}) async-start(bf16[8,192,128]{2,1,0:T(8,128)(2,1)} %row_pack.1), calls=%async_computation.4 | async-start | bytes 786432 | tf_op jit(solution)/shard_map/all_to_all | solution.py:577
  111.8 3.5 %collective-permute-start.4 = (bf16[3,64,128]{2,1,0:T(8,128)(2,1)S(1)}, bf16[3,64,128]{2,1,0:T(8,128)(2,1)S(1)}, u32[]{:S(2)}, u32[]{:S(2)}) collective-permute-start(bf16[3,64,128]{2,1,0:T(8,128)(2,1)S(1)} %get-tuple-element.69), channel_id=1, source_target_pairs={{0,64},{64,128},{128,192},{192,256},{256,320},{320,384},{384,448},... | collective-permute-start | bytes 147464 | tf_op jit(solution)/shard_map/ppermute | solution.py:565
  115.3 1.9 %collective-permute-start.5 = (bf16[3,64,128]{2,1,0:T(8,128)(2,1)S(1)}, bf16[3,64,128]{2,1,0:T(8,128)(2,1)S(1)}, u32[]{:S(2)}, u32[]{:S(2)}) collective-permute-start(bf16[3,64,128]{2,1,0:T(8,128)(2,1)S(1)} %get-tuple-element.68), channel_id=1, source_target_pairs={{64,0},{128,64},{192,128},{256,192},{320,256},{384,320},{448,384},... | collective-permute-start | bytes 147464 | tf_op jit(solution)/shard_map/ppermute | solution.py:565
  117.3 0.0 collective-permute-done.4.up
  117.3 3.6 %collective-permute-done.5.down = bf16[3,64,128]{2,1,0:T(8,128)(2,1)S(1)} collective-permute-done((bf16[3,64,128]{2,1,0:T(8,128)(2,1)S(1)}, bf16[3,64,128]{2,1,0:T(8,128)(2,1)S(1)}, u32[]{:S(2)}, u32[]{:S(2)}) %collective-permute-start.5) | collective-permute-done | bytes 49184 | tf_op jit(solution)/shard_map/ppermute | solution.py:565
  120.8 0.9 edges.3
  121.7 2.5 %collective-permute-start.6 = (bf16[64,128]{1,0:T(8,128)(2,1)S(1)}, bf16[64,128]{1,0:T(8,128)(2,1)S(1)}, u32[]{:S(2)}, u32[]{:S(2)}) collective-permute-start(bf16[64,128]{1,0:T(8,128)(2,1)S(1)} %get-tuple-element.44), channel_id=1, source_target_pairs={{0,4},{4,8},{8,12},{12,16},{16,20},{20,24},{24,28},{28,32},{32,36}... | collective-permute-start | bytes 49160 | tf_op jit(solution)/shard_map/ppermute | solution.py:565
  124.2 1.3 collective-permute-start.7
  125.5 0.7 copy.20
  126.2 0.0 collective-permute-done.6.left
  126.2 2.5 %collective-permute-done.7.right = bf16[64,128]{1,0:T(8,128)(2,1)S(1)} collective-permute-done((bf16[64,128]{1,0:T(8,128)(2,1)S(1)}, bf16[64,128]{1,0:T(8,128)(2,1)S(1)}, u32[]{:S(2)}, u32[]{:S(2)}) %collective-permute-start.7) | collective-permute-done | bytes 16416 | tf_op jit(solution)/shard_map/ppermute | solution.py:565
  128.7 1.7 %backward.1 = bf16[4,64,128]{2,1,0:T(8,128)(2,1)S(1)} custom-call(bf16[3,64,128]{2,1,0:T(8,128)(2,1)S(1)} %collective-permute-done.4.up, bf16[4,64,128]{2,1,0:T(8,128)(2,1)S(1)} %get-tuple-element.43.mid, bf16[3,64,128]{2,1,0:T(8,128)(2,1)S(1)} %collective-permute-done.5.down, bf16[64,128]{1,0:T(8,128)(2,1)S(1)} %collective-permute-done.6.left, ...), custom_call_target="tpu_custom_call" | custom-call | tf_op jit(solution)/shard_map/backward/pallas_call | solution.py:28
  130.4 0.7 copy.21
  131.1 1.0 final.1
  (15 shorter events, 0.1 us)
Async XLA Ops:
  1.5 10.1 %collective-permute-start = (bf16[3,64,128]{2,1,0:T(8,128)(2,1)S(1)}, bf16[3,64,128]{2,1,0:T(8,128)(2,1)S(1)}, u32[]{:S(2)}, u32[]{:S(2)}) collective-permute-start(bf16[3,64,128]{2,1,0:T(8,128)(2,1)S(1)} %get-tuple-element.71), channel_id=1, source_target_pairs={{0,64},{64,128},{128,192},{192,256},{256,320},{320,384},{384,448},... | collective-permute-start | bytes 147464 | tf_op jit(solution)/shard_map/ppermute | solution.py:565
  6.1 6.3 %collective-permute-start.1 = (bf16[3,64,128]{2,1,0:T(8,128)(2,1)S(1)}, bf16[3,64,128]{2,1,0:T(8,128)(2,1)S(1)}, u32[]{:S(2)}, u32[]{:S(2)}) collective-permute-start(bf16[3,64,128]{2,1,0:T(8,128)(2,1)S(1)} %get-tuple-element.70), channel_id=1, source_target_pairs={{64,0},{128,64},{192,128},{256,192},{320,256},{384,320},{448,384},... | collective-permute-start | bytes 147464 | tf_op jit(solution)/shard_map/ppermute | solution.py:565
  12.4 0.7 copy-start.2
  12.4 0.7 copy-start.3
  13.1 4.4 %copy-start.4 = (bf16[64,4,128]{2,1,0:T(4,128)(2,1)S(1)}, bf16[64,4,128]{2,1,0:T(4,128)(2,1)}, u32[]{:S(2)}) copy-start(bf16[64,4,128]{2,1,0:T(4,128)(2,1)} %param.15) | copy-start | bytes 196612
  13.5 4.1 %collective-permute-start.2 = (bf16[64,128]{1,0:T(8,128)(2,1)S(1)}, bf16[64,128]{1,0:T(8,128)(2,1)S(1)}, u32[]{:S(2)}, u32[]{:S(2)}) collective-permute-start(bf16[64,128]{1,0:T(8,128)(2,1)S(1)} %get-tuple-element.34), channel_id=1, source_target_pairs={{0,4},{4,8},{8,12},{12,16},{16,20},{20,24},{24,28},{28,32},{32,36}... | collective-permute-start | bytes 49160 | tf_op jit(solution)/shard_map/ppermute | solution.py:565
  16.2 1.3 %copy-start.5 = (f32[64,49]{0,1:T(8,128)S(1)}, f32[64,49]{0,1:T(8,128)}, u32[]{:S(2)}) copy-start(f32[64,49]{0,1:T(8,128)} %param.9) | copy-start | bytes 37636
  16.2 4.7 %collective-permute-start.3 = (bf16[64,128]{1,0:T(8,128)(2,1)S(1)}, bf16[64,128]{1,0:T(8,128)(2,1)S(1)}, u32[]{:S(2)}, u32[]{:S(2)}) collective-permute-start(bf16[64,128]{1,0:T(8,128)(2,1)S(1)} %get-tuple-element.35), channel_id=1, source_target_pairs={{4,0},{8,4},{12,8},{16,12},{20,16},{24,20},{28,24},{32,28},{36,32}... | collective-permute-start | bytes 49160 | tf_op jit(solution)/shard_map/ppermute | solution.py:565
  23.5 14.6 %copy-start = (bf16[256,256]{1,0:T(8,128)(2,1)S(1)}, bf16[256,256]{1,0:T(8,128)(2,1)}, u32[]{:S(2)}) copy-start(bf16[256,256]{1,0:T(8,128)(2,1)} %w_exp.1) | copy-start | bytes 393220
  23.5 14.6 %copy-start.1 = (bf16[256,256]{1,0:T(8,128)(2,1)S(1)}, bf16[256,256]{1,0:T(8,128)(2,1)}, u32[]{:S(2)}) copy-start(bf16[256,256]{1,0:T(8,128)(2,1)} %w_red.1) | copy-start | bytes 393220
  23.5 14.6 %all-to-all-start = ((bf16[4,144,512]{2,1,0:T(8,128)(2,1)}), bf16[4,144,512]{2,1,0:T(8,128)(2,1)S(1)}, u32[]{:S(2)}, u32[]{:S(2)}) async-start(bf16[4,144,512]{2,1,0:T(8,128)(2,1)} %get-tuple-element.37), calls=%async_computation | async-start | bytes 1179648 | tf_op jit(solution)/shard_map/all_to_all | solution.py:577
  40.2 16.7 %all-to-all-start.1 = ((bf16[4,144,512]{2,1,0:T(8,128)(2,1)}), bf16[4,144,512]{2,1,0:T(8,128)(2,1)S(1)}, u32[]{:S(2)}, u32[]{:S(2)}) async-start(bf16[4,144,512]{2,1,0:T(8,128)(2,1)} %get-tuple-element.38), calls=%async_computation.1 | async-start | bytes 1179648 | tf_op jit(solution)/shard_map/all_to_all | solution.py:577
  43.7 3.5 %collective-permute-start.8 = (f32[512,128]{1,0:T(8,128)S(1)}, f32[512,128]{1,0:T(8,128)S(1)}, u32[]{:S(2)}, u32[]{:S(2)}) collective-permute-start(f32[512,128]{1,0:T(8,128)S(1)} %get-tuple-element.49), channel_id=1, source_target_pairs={{0,64},{64,0},{128,192},{192,128},{256,320},{320,256},{384,448},{4... | collective-permute-start | bytes 786440 | tf_op jit(solution)/shard_map/ppermute | solution.py:237
  47.2 9.9 %collective-permute-start.10 = (bf16[128,128]{1,0:T(8,128)(2,1)S(1)}, bf16[128,128]{1,0:T(8,128)(2,1)S(1)}, u32[]{:S(2)}, u32[]{:S(2)}) collective-permute-start(bf16[128,128]{1,0:T(8,128)(2,1)S(1)} %get-tuple-element.52), channel_id=1, source_target_pairs={{0,256},{64,320},{128,384},{192,448},{256,0},{320,64},{384,128},{4... | collective-permute-start | bytes 98312 | tf_op jit(solution)/shard_map/ppermute | solution.py:242
  52.0 5.9 %collective-permute-start.11 = (bf16[128,128]{1,0:T(8,128)(2,1)S(1)}, bf16[128,128]{1,0:T(8,128)(2,1)S(1)}, u32[]{:S(2)}, u32[]{:S(2)}) collective-permute-start(bf16[128,128]{1,0:T(8,128)(2,1)S(1)} %get-tuple-element.53), channel_id=1, source_target_pairs={{0,384},{64,448},{128,256},{192,320},{256,128},{320,192},{384,0},{... | collective-permute-start | bytes 98312 | tf_op jit(solution)/shard_map/ppermute | solution.py:242
  55.0 4.7 %collective-permute-start.9 = (bf16[128,128]{1,0:T(8,128)(2,1)S(1)}, bf16[128,128]{1,0:T(8,128)(2,1)S(1)}, u32[]{:S(2)}, u32[]{:S(2)}) collective-permute-start(bf16[128,128]{1,0:T(8,128)(2,1)S(1)} %get-tuple-element.51), channel_id=1, source_target_pairs={{0,128},{64,192},{128,0},{192,64},{256,384},{320,448},{384,256},{4... | collective-permute-start | bytes 98312 | tf_op jit(solution)/shard_map/ppermute | solution.py:242
  103.7 27.5 %all-to-all-start.4 = ((bf16[8,192,128]{2,1,0:T(8,128)(2,1)}), bf16[8,192,128]{2,1,0:T(8,128)(2,1)S(1)}, u32[]{:S(2)}, u32[]{:S(2)}) async-start(bf16[8,192,128]{2,1,0:T(8,128)(2,1)} %row_pack.1), calls=%async_computation.4 | async-start | bytes 786432 | tf_op jit(solution)/shard_map/all_to_all | solution.py:577
  111.8 5.5 %collective-permute-start.4 = (bf16[3,64,128]{2,1,0:T(8,128)(2,1)S(1)}, bf16[3,64,128]{2,1,0:T(8,128)(2,1)S(1)}, u32[]{:S(2)}, u32[]{:S(2)}) collective-permute-start(bf16[3,64,128]{2,1,0:T(8,128)(2,1)S(1)} %get-tuple-element.69), channel_id=1, source_target_pairs={{0,64},{64,128},{128,192},{192,256},{256,320},{320,384},{384,448},... | collective-permute-start | bytes 147464 | tf_op jit(solution)/shard_map/ppermute | solution.py:565
  115.3 5.5 %collective-permute-start.5 = (bf16[3,64,128]{2,1,0:T(8,128)(2,1)S(1)}, bf16[3,64,128]{2,1,0:T(8,128)(2,1)S(1)}, u32[]{:S(2)}, u32[]{:S(2)}) collective-permute-start(bf16[3,64,128]{2,1,0:T(8,128)(2,1)S(1)} %get-tuple-element.68), channel_id=1, source_target_pairs={{64,0},{128,64},{192,128},{256,192},{320,256},{384,320},{448,384},... | collective-permute-start | bytes 147464 | tf_op jit(solution)/shard_map/ppermute | solution.py:565
  121.7 4.5 %collective-permute-start.6 = (bf16[64,128]{1,0:T(8,128)(2,1)S(1)}, bf16[64,128]{1,0:T(8,128)(2,1)S(1)}, u32[]{:S(2)}, u32[]{:S(2)}) collective-permute-start(bf16[64,128]{1,0:T(8,128)(2,1)S(1)} %get-tuple-element.44), channel_id=1, source_target_pairs={{0,4},{4,8},{8,12},{12,16},{16,20},{20,24},{24,28},{28,32},{32,36}... | collective-permute-start | bytes 49160 | tf_op jit(solution)/shard_map/ppermute | solution.py:565
  124.2 4.5 %collective-permute-start.7 = (bf16[64,128]{1,0:T(8,128)(2,1)S(1)}, bf16[64,128]{1,0:T(8,128)(2,1)S(1)}, u32[]{:S(2)}, u32[]{:S(2)}) collective-permute-start(bf16[64,128]{1,0:T(8,128)(2,1)S(1)} %get-tuple-element.45), channel_id=1, source_target_pairs={{4,0},{8,4},{12,8},{16,12},{20,16},{24,20},{28,24},{32,28},{36,32}... | collective-permute-start | bytes 49160 | tf_op jit(solution)/shard_map/ppermute | solution.py:565

commit v9 on v8

--- a/solution.py
+++ b/solution.py
@@ -88,8 +88,8 @@
     if s == 0:
         return x
     lane = lane_ids(CT)
-    mask = (lane < -s) if s < 0 else (lane >= LANES - s)
-    return jnp.where(mask, rolled(edge, -s), rolled(x, -s))
+    mask = (lane < s) if s > 0 else (lane >= LANES + s)
+    return rolled(jnp.where(mask, edge, x), -s)
 
 
 def edges_kernel(up, mid, down, gain, shift, first, last, both):
@@ -489,13 +489,12 @@
 def row_pack_kernel(per, recv, out, tile):
     cols, height, _ = recv.shape
     part = height - -(-2 * per // 8) * 8
-    base, size = cols * part, cols * per
+    base = cols * part
     for c in range(cols):
         x = recv[c].astype(f32)
         tile[c * part : (c + 1) * part, :] = x[0:part]
-        tile[base + c * per : base + (c + 1) * per, :] = x[part : part + per]
-        low = base + size + c * per
-        tile[low : low + per, :] = x[part + per : part + 2 * per]
+        small = x[part : part + per] + x[part + per : part + 2 * per]
+        tile[base + c * per : base + (c + 1) * per, :] = small
     x = tile[...].astype(bf16)
     for r in range(out.shape[0]):
         out[r] = x
@@ -503,7 +502,7 @@
 
 def row_pack(recv, rows, per):
     cols, height, _ = recv.shape
-    tall = cols * (height - -(-2 * per // 8) * 8 + 2 * per)
+    tall = cols * (height - -(-2 * per // 8) * 8 + per)
     return vcall(
         functools.partial(row_pack_kernel, per),
         out_shape=jax.ShapeDtypeStruct((rows, tall, LANES), bf16),
@@ -520,7 +519,7 @@
     for r in range(rows):
         x = flat[r].astype(f32) * scale
         block = x[0:size_all]
-        tail = x[size_all : size_all + per] + x[size_all + per : size_all + 2 * per]
+        tail = x[size_all : size_all + per]
         total = tail if r == 0 else total + tail
         start = row_chunk(r, rows) * size_all
         lo = 0

time: 133 us -> 132 us (level)
  no operation moved by 1% of the time
where the time goes in v9:
time: 132 us; the launch traced here: 131 us
  starting transfers between devices  51 us (39%)
  blocking collectives  40.4 us (31%)
  waiting for transfers between devices  23.5 us (18%)
  Pallas kernels  11.3 us (9%)
  local copies, waits for them, and re-layouts  3.79 us (3%)
    all_to_all x2, blocking collectives, exchange(): return lax.all_to_all(x, axis, 0, 0)  40.4 us
    ppermute x8, starting transfers between devices, neighbours(): return (lax.ppermute(last, axis, up), lax.ppermute(first, axis, down))  23.3 us
    all_to_all x3, starting transfers between devices, exchange(): return lax.all_to_all(x, axis, 0, 0)  15.7 us
    pallas_call x11, Pallas kernels, call(): pl.pallas_call(kernel, out_shape=out_shape, in_specs=[spec] * len(args),...  11.3 us
    ppermute x8, waiting for transfers between devices, neighbours(): return (lax.ppermute(last, axis, up), lax.ppermute(first, axis, down))  10.1 us
    all_to_all x3, waiting for transfers between devices, exchange(): return lax.all_to_all(x, axis, 0, 0)  9.72 us
    ppermute x3, starting transfers between devices, reduce_rows(): lax.ppermute(chunks[m], 'row', [(i, i ^ 2 * m) for i in range(size)])  9.69 us
    unnamed x17, local copies, waits for them, and re-layouts  3 us
  transfers between devices with their start and end apart: 15, of which 8 were waited for; matrix products, arithmetic and copies ran while one was open for 2% of the time, Pallas kernels for 2%

profile of v9, /device:TPU:1, one launch (start us, length us, event | category | flops | bytes accessed | tf_op | source)
XLA Modules:
  0.0 130.8 jit_solution(16595048526519283435)
XLA Ops:
  0.6 0.9 copy.25
  1.5 4.6 %collective-permute-start = (bf16[3,64,128]{2,1,0:T(8,128)(2,1)S(1)}, bf16[3,64,128]{2,1,0:T(8,128)(2,1)S(1)}, u32[]{:S(2)}, u32[]{:S(2)}) collective-permute-start(bf16[3,64,128]{2,1,0:T(8,128)(2,1)S(1)} %get-tuple-element.71), channel_id=1, source_target_pairs={{0,64},{64,128},{128,192},{192,256},{256,320},{320,384},{384,448},... | collective-permute-start | bytes 147464 | tf_op jit(solution)/shard_map/ppermute | solution.py:564
  6.1 5.5 %collective-permute-start.1 = (bf16[3,64,128]{2,1,0:T(8,128)(2,1)S(1)}, bf16[3,64,128]{2,1,0:T(8,128)(2,1)S(1)}, u32[]{:S(2)}, u32[]{:S(2)}) collective-permute-start(bf16[3,64,128]{2,1,0:T(8,128)(2,1)S(1)} %get-tuple-element.70), channel_id=1, source_target_pairs={{64,0},{128,64},{192,128},{256,192},{320,256},{384,320},{448,384},... | collective-permute-start | bytes 147464 | tf_op jit(solution)/shard_map/ppermute | solution.py:564
  11.6 0.0 collective-permute-done.up
  11.6 0.8 collective-permute-done.1.down
  12.4 0.7 copy-done.2
  13.1 0.0 copy-done.3
  13.1 0.4 edges.2
  13.5 2.6 %collective-permute-start.2 = (bf16[64,128]{1,0:T(8,128)(2,1)S(1)}, bf16[64,128]{1,0:T(8,128)(2,1)S(1)}, u32[]{:S(2)}, u32[]{:S(2)}) collective-permute-start(bf16[64,128]{1,0:T(8,128)(2,1)S(1)} %get-tuple-element.34), channel_id=1, source_target_pairs={{0,4},{4,8},{8,12},{12,16},{16,20},{20,24},{24,28},{28,32},{32,36}... | collective-permute-start | bytes 49160 | tf_op jit(solution)/shard_map/ppermute | solution.py:564
  16.2 0.0 copy-start.5
  16.2 1.3 collective-permute-start.3
  17.5 0.1 copy.18.kern
  17.6 0.0 collective-permute-done.2.left
  17.6 3.2 %collective-permute-done.3.right = bf16[64,128]{1,0:T(8,128)(2,1)S(1)} collective-permute-done((bf16[64,128]{1,0:T(8,128)(2,1)S(1)}, bf16[64,128]{1,0:T(8,128)(2,1)S(1)}, u32[]{:S(2)}, u32[]{:S(2)}) %collective-permute-start.3) | collective-permute-done | bytes 16416 | tf_op jit(solution)/shard_map/ppermute | solution.py:564
  20.9 2.4 %forward.1 = (f32[64,512]{1,0:T(8,128)S(1)}, bf16[4,144,512]{2,1,0:T(8,128)(2,1)}) custom-call(bf16[3,64,128]{2,1,0:T(8,128)(2,1)S(1)} %collective-permute-done.up, bf16[4,64,128]{2,1,0:T(8,128)(2,1)S(1)} %bitcast.17, bf16[3,64,128]{2,1,0:T(8,128)(2,1)S(1)} %collective-permute-done.1.down, bf16[64,128]{1,0:T(8,128)(2,1)S(1)} %collective-permute-done.2.left, ...), custom_call_target="tpu_custom_call" | custom-call | tf_op jit(solution)/shard_map/forward/pallas_call | solution.py:28
  23.2 4.1 %all-to-all-start = ((bf16[4,144,512]{2,1,0:T(8,128)(2,1)}), bf16[4,144,512]{2,1,0:T(8,128)(2,1)S(1)}, u32[]{:S(2)}, u32[]{:S(2)}) async-start(bf16[4,144,512]{2,1,0:T(8,128)(2,1)} %get-tuple-element.37), calls=%async_computation | async-start | bytes 1179648 | tf_op jit(solution)/shard_map/all_to_all | solution.py:576
  27.4 0.8 dynamic_slice.3
  28.1 9.7 %all-to-all-done.recv = bf16[4,144,512]{2,1,0:T(8,128)(2,1)S(1)} async-done(((bf16[4,144,512]{2,1,0:T(8,128)(2,1)}), bf16[4,144,512]{2,1,0:T(8,128)(2,1)S(1)}, u32[]{:S(2)}, u32[]{:S(2)}) %all-to-all-start) | async-done | bytes 589856 | tf_op jit(solution)/shard_map/all_to_all | solution.py:576
  37.9 2.1 %mlp.1 = (bf16[4,144,512]{2,1,0:T(8,128)(2,1)}, f32[2,512]{1,0:T(2,128)S(1)}, f32[512,128]{1,0:T(8,128)S(1)}, f32[512,128]{1,0:T(8,128)S(1)}, f32[64,128]{1,0:T(8,128)S(1)}) custom-call(bf16[4,144,512]{2,1,0:T(8,128)(2,1)S(1)} %all-to-all-done.recv, bf16[256,256]{1,0:T(8,128)(2,1)S(1)} %copy-done, f32[1,256]{1,0:T(1,128)S(1)} %bitcast.27, ...), custom_call_target="tpu_custom_call" | custom-call | tf_op jit(solution)/shard_map/mlp/pallas_call | solution.py:28
  40.0 3.5 %all-to-all-start.1 = ((bf16[4,144,512]{2,1,0:T(8,128)(2,1)}), bf16[4,144,512]{2,1,0:T(8,128)(2,1)S(1)}, u32[]{:S(2)}, u32[]{:S(2)}) async-start(bf16[4,144,512]{2,1,0:T(8,128)(2,1)} %get-tuple-element.38), calls=%async_computation.1 | async-start | bytes 1179648 | tf_op jit(solution)/shard_map/all_to_all | solution.py:576
  43.5 2.3 %collective-permute-start.8 = (f32[512,128]{1,0:T(8,128)S(1)}, f32[512,128]{1,0:T(8,128)S(1)}, u32[]{:S(2)}, u32[]{:S(2)}) collective-permute-start(f32[512,128]{1,0:T(8,128)S(1)} %get-tuple-element.49), channel_id=1, source_target_pairs={{0,64},{64,0},{128,192},{192,128},{256,320},{320,256},{384,448},{4... | collective-permute-start | bytes 786440 | tf_op jit(solution)/shard_map/ppermute | solution.py:237
  45.8 1.1 collective-permute-done.8.recv
  47.0 4.8 %collective-permute-start.10 = (bf16[128,128]{1,0:T(8,128)(2,1)S(1)}, bf16[128,128]{1,0:T(8,128)(2,1)S(1)}, u32[]{:S(2)}, u32[]{:S(2)}) collective-permute-start(bf16[128,128]{1,0:T(8,128)(2,1)S(1)} %get-tuple-element.52), channel_id=1, source_target_pairs={{0,256},{64,320},{128,384},{192,448},{256,0},{320,64},{384,128},{4... | collective-permute-start | bytes 98312 | tf_op jit(solution)/shard_map/ppermute | solution.py:242
  51.8 3.0 %collective-permute-start.11 = (bf16[128,128]{1,0:T(8,128)(2,1)S(1)}, bf16[128,128]{1,0:T(8,128)(2,1)S(1)}, u32[]{:S(2)}, u32[]{:S(2)}) collective-permute-start(bf16[128,128]{1,0:T(8,128)(2,1)S(1)} %get-tuple-element.53), channel_id=1, source_target_pairs={{0,384},{64,448},{128,256},{192,320},{256,128},{320,192},{384,0},{... | collective-permute-start | bytes 98312 | tf_op jit(solution)/shard_map/ppermute | solution.py:242
  54.8 1.9 %collective-permute-start.9 = (bf16[128,128]{1,0:T(8,128)(2,1)S(1)}, bf16[128,128]{1,0:T(8,128)(2,1)S(1)}, u32[]{:S(2)}, u32[]{:S(2)}) collective-permute-start(bf16[128,128]{1,0:T(8,128)(2,1)S(1)} %get-tuple-element.51), channel_id=1, source_target_pairs={{0,128},{64,192},{128,0},{192,64},{256,384},{320,448},{384,256},{4... | collective-permute-start | bytes 98312 | tf_op jit(solution)/shard_map/ppermute | solution.py:242
  56.7 0.0 all-to-all-done.1.recv
  56.7 0.1 norm_back.1
  56.9 0.0 collective-permute-done.10.rest_2_
  56.9 0.8 collective-permute-done.11.rest_3_
  57.7 1.8 %collective-permute-done.9.rest_1_ = bf16[128,128]{1,0:T(8,128)(2,1)S(1)} collective-permute-done((bf16[128,128]{1,0:T(8,128)(2,1)S(1)}, bf16[128,128]{1,0:T(8,128)(2,1)S(1)}, u32[]{:S(2)}, u32[]{:S(2)}) %collective-permute-start.9) | collective-permute-done | bytes 32800 | tf_op jit(solution)/shard_map/ppermute | solution.py:242
  59.4 2.1 %tap_grad.1 = bf16[16,16,128]{2,1,0:T(8,128)(2,1)S(1)} custom-call(bf16[3,64,128]{2,1,0:T(8,128)(2,1)S(1)} %collective-permute-done.up, bf16[4,64,128]{2,1,0:T(8,128)(2,1)S(1)} %bitcast.19, bf16[3,64,128]{2,1,0:T(8,128)(2,1)S(1)} %collective-permute-done.1.down, bf16[64,128]{1,0:T(8,128)(2,1)S(1)} %collective-permute-done.2.left, ...), custom_call_target="tpu_custom_call" | custom-call | tf_op jit(solution)/shard_map/tap_grad/pallas_call | solution.py:28
  61.5 26.0 %all_to_all.25.recv = bf16[16,16,128]{2,1,0:T(8,128)(2,1)S(1)} all-to-all(bf16[16,16,128]{2,1,0:T(8,128)(2,1)S(1)} %tap_grad.1), channel_id=1, replica_groups=mesh['row'=8,'col'=16,'ch'=4] {'col'}, dimensions={0} | all-to-all | bytes 131072 | tf_op jit(solution)/shard_map/all_to_all | solution.py:576
  87.5 14.4 %all_to_all.26.recv = bf16[16,16,128]{2,1,0:T(8,128)(2,1)S(1)} all-to-all(bf16[16,16,128]{2,1,0:T(8,128)(2,1)S(1)} %col_pack.1), channel_id=1, replica_groups=mesh['row'=8,'col'=16,'ch'=4] {'col'}, dimensions={0} | all-to-all | bytes 131072 | tf_op jit(solution)/shard_map/all_to_all | solution.py:576
  101.9 0.8 row_pack.1
  102.7 8.1 %all-to-all-start.4 = ((bf16[8,160,128]{2,1,0:T(8,128)(2,1)}), bf16[8,160,128]{2,1,0:T(8,128)(2,1)S(1)}, u32[]{:S(2)}, u32[]{:S(2)}) async-start(bf16[8,160,128]{2,1,0:T(8,128)(2,1)} %row_pack.1), calls=%async_computation.4 | async-start | bytes 655360 | tf_op jit(solution)/shard_map/all_to_all | solution.py:576
  110.8 3.5 %collective-permute-start.4 = (bf16[3,64,128]{2,1,0:T(8,128)(2,1)S(1)}, bf16[3,64,128]{2,1,0:T(8,128)(2,1)S(1)}, u32[]{:S(2)}, u32[]{:S(2)}) collective-permute-start(bf16[3,64,128]{2,1,0:T(8,128)(2,1)S(1)} %get-tuple-element.69), channel_id=1, source_target_pairs={{0,64},{64,128},{128,192},{192,256},{256,320},{320,384},{384,448},... | collective-permute-start | bytes 147464 | tf_op jit(solution)/shard_map/ppermute | solution.py:564
  114.3 1.9 %collective-permute-start.5 = (bf16[3,64,128]{2,1,0:T(8,128)(2,1)S(1)}, bf16[3,64,128]{2,1,0:T(8,128)(2,1)S(1)}, u32[]{:S(2)}, u32[]{:S(2)}) collective-permute-start(bf16[3,64,128]{2,1,0:T(8,128)(2,1)S(1)} %get-tuple-element.68), channel_id=1, source_target_pairs={{64,0},{128,64},{192,128},{256,192},{320,256},{384,320},{448,384},... | collective-permute-start | bytes 147464 | tf_op jit(solution)/shard_map/ppermute | solution.py:564
  116.3 0.0 collective-permute-done.4.up
  116.3 3.5 %collective-permute-done.5.down = bf16[3,64,128]{2,1,0:T(8,128)(2,1)S(1)} collective-permute-done((bf16[3,64,128]{2,1,0:T(8,128)(2,1)S(1)}, bf16[3,64,128]{2,1,0:T(8,128)(2,1)S(1)}, u32[]{:S(2)}, u32[]{:S(2)}) %collective-permute-start.5) | collective-permute-done | bytes 49184 | tf_op jit(solution)/shard_map/ppermute | solution.py:564
  119.8 0.9 edges.3
  120.6 2.5 %collective-permute-start.6 = (bf16[64,128]{1,0:T(8,128)(2,1)S(1)}, bf16[64,128]{1,0:T(8,128)(2,1)S(1)}, u32[]{:S(2)}, u32[]{:S(2)}) collective-permute-start(bf16[64,128]{1,0:T(8,128)(2,1)S(1)} %get-tuple-element.44), channel_id=1, source_target_pairs={{0,4},{4,8},{8,12},{12,16},{16,20},{20,24},{24,28},{28,32},{32,36}... | collective-permute-start | bytes 49160 | tf_op jit(solution)/shard_map/ppermute | solution.py:564
  123.2 1.3 collective-permute-start.7
  124.5 0.7 copy.20
  125.2 0.0 collective-permute-done.6.left
  125.2 2.5 %collective-permute-done.7.right = bf16[64,128]{1,0:T(8,128)(2,1)S(1)} collective-permute-done((bf16[64,128]{1,0:T(8,128)(2,1)S(1)}, bf16[64,128]{1,0:T(8,128)(2,1)S(1)}, u32[]{:S(2)}, u32[]{:S(2)}) %collective-permute-start.7) | collective-permute-done | bytes 16416 | tf_op jit(solution)/shard_map/ppermute | solution.py:564
  127.7 1.5 %backward.1 = bf16[4,64,128]{2,1,0:T(8,128)(2,1)S(1)} custom-call(bf16[3,64,128]{2,1,0:T(8,128)(2,1)S(1)} %collective-permute-done.4.up, bf16[4,64,128]{2,1,0:T(8,128)(2,1)S(1)} %get-tuple-element.43.mid, bf16[3,64,128]{2,1,0:T(8,128)(2,1)S(1)} %collective-permute-done.5.down, bf16[64,128]{1,0:T(8,128)(2,1)S(1)} %collective-permute-done.6.left, ...), custom_call_target="tpu_custom_call" | custom-call | tf_op jit(solution)/shard_map/backward/pallas_call | solution.py:28
  129.1 0.7 copy.21
  129.8 1.0 final.1
  (15 shorter events, 0.1 us)
Async XLA Ops:
  1.5 10.1 %collective-permute-start = (bf16[3,64,128]{2,1,0:T(8,128)(2,1)S(1)}, bf16[3,64,128]{2,1,0:T(8,128)(2,1)S(1)}, u32[]{:S(2)}, u32[]{:S(2)}) collective-permute-start(bf16[3,64,128]{2,1,0:T(8,128)(2,1)S(1)} %get-tuple-element.71), channel_id=1, source_target_pairs={{0,64},{64,128},{128,192},{192,256},{256,320},{320,384},{384,448},... | collective-permute-start | bytes 147464 | tf_op jit(solution)/shard_map/ppermute | solution.py:564
  6.1 6.3 %collective-permute-start.1 = (bf16[3,64,128]{2,1,0:T(8,128)(2,1)S(1)}, bf16[3,64,128]{2,1,0:T(8,128)(2,1)S(1)}, u32[]{:S(2)}, u32[]{:S(2)}) collective-permute-start(bf16[3,64,128]{2,1,0:T(8,128)(2,1)S(1)} %get-tuple-element.70), channel_id=1, source_target_pairs={{64,0},{128,64},{192,128},{256,192},{320,256},{384,320},{448,384},... | collective-permute-start | bytes 147464 | tf_op jit(solution)/shard_map/ppermute | solution.py:564
  12.4 0.7 copy-start.2
  12.4 0.7 copy-start.3
  13.1 4.4 %copy-start.4 = (bf16[64,4,128]{2,1,0:T(4,128)(2,1)S(1)}, bf16[64,4,128]{2,1,0:T(4,128)(2,1)}, u32[]{:S(2)}) copy-start(bf16[64,4,128]{2,1,0:T(4,128)(2,1)} %param.15) | copy-start | bytes 196612
  13.5 4.1 %collective-permute-start.2 = (bf16[64,128]{1,0:T(8,128)(2,1)S(1)}, bf16[64,128]{1,0:T(8,128)(2,1)S(1)}, u32[]{:S(2)}, u32[]{:S(2)}) collective-permute-start(bf16[64,128]{1,0:T(8,128)(2,1)S(1)} %get-tuple-element.34), channel_id=1, source_target_pairs={{0,4},{4,8},{8,12},{12,16},{16,20},{20,24},{24,28},{28,32},{32,36}... | collective-permute-start | bytes 49160 | tf_op jit(solution)/shard_map/ppermute | solution.py:564
  16.2 1.3 %copy-start.5 = (f32[64,49]{0,1:T(8,128)S(1)}, f32[64,49]{0,1:T(8,128)}, u32[]{:S(2)}) copy-start(f32[64,49]{0,1:T(8,128)} %param.9) | copy-start | bytes 37636
  16.2 4.7 %collective-permute-start.3 = (bf16[64,128]{1,0:T(8,128)(2,1)S(1)}, bf16[64,128]{1,0:T(8,128)(2,1)S(1)}, u32[]{:S(2)}, u32[]{:S(2)}) collective-permute-start(bf16[64,128]{1,0:T(8,128)(2,1)S(1)} %get-tuple-element.35), channel_id=1, source_target_pairs={{4,0},{8,4},{12,8},{16,12},{20,16},{24,20},{28,24},{32,28},{36,32}... | collective-permute-start | bytes 49160 | tf_op jit(solution)/shard_map/ppermute | solution.py:564
  23.2 14.6 %copy-start = (bf16[256,256]{1,0:T(8,128)(2,1)S(1)}, bf16[256,256]{1,0:T(8,128)(2,1)}, u32[]{:S(2)}) copy-start(bf16[256,256]{1,0:T(8,128)(2,1)} %w_exp.1) | copy-start | bytes 393220
  23.2 14.6 %copy-start.1 = (bf16[256,256]{1,0:T(8,128)(2,1)S(1)}, bf16[256,256]{1,0:T(8,128)(2,1)}, u32[]{:S(2)}) copy-start(bf16[256,256]{1,0:T(8,128)(2,1)} %w_red.1) | copy-start | bytes 393220
  23.2 14.6 %all-to-all-start = ((bf16[4,144,512]{2,1,0:T(8,128)(2,1)}), bf16[4,144,512]{2,1,0:T(8,128)(2,1)S(1)}, u32[]{:S(2)}, u32[]{:S(2)}) async-start(bf16[4,144,512]{2,1,0:T(8,128)(2,1)} %get-tuple-element.37), calls=%async_computation | async-start | bytes 1179648 | tf_op jit(solution)/shard_map/all_to_all | solution.py:576
  40.0 16.7 %all-to-all-start.1 = ((bf16[4,144,512]{2,1,0:T(8,128)(2,1)}), bf16[4,144,512]{2,1,0:T(8,128)(2,1)S(1)}, u32[]{:S(2)}, u32[]{:S(2)}) async-start(bf16[4,144,512]{2,1,0:T(8,128)(2,1)} %get-tuple-element.38), calls=%async_computation.1 | async-start | bytes 1179648 | tf_op jit(solution)/shard_map/all_to_all | solution.py:576
  43.5 3.5 %collective-permute-start.8 = (f32[512,128]{1,0:T(8,128)S(1)}, f32[512,128]{1,0:T(8,128)S(1)}, u32[]{:S(2)}, u32[]{:S(2)}) collective-permute-start(f32[512,128]{1,0:T(8,128)S(1)} %get-tuple-element.49), channel_id=1, source_target_pairs={{0,64},{64,0},{128,192},{192,128},{256,320},{320,256},{384,448},{4... | collective-permute-start | bytes 786440 | tf_op jit(solution)/shard_map/ppermute | solution.py:237
  47.0 9.9 %collective-permute-start.10 = (bf16[128,128]{1,0:T(8,128)(2,1)S(1)}, bf16[128,128]{1,0:T(8,128)(2,1)S(1)}, u32[]{:S(2)}, u32[]{:S(2)}) collective-permute-start(bf16[128,128]{1,0:T(8,128)(2,1)S(1)} %get-tuple-element.52), channel_id=1, source_target_pairs={{0,256},{64,320},{128,384},{192,448},{256,0},{320,64},{384,128},{4... | collective-permute-start | bytes 98312 | tf_op jit(solution)/shard_map/ppermute | solution.py:242
  51.8 5.9 %collective-permute-start.11 = (bf16[128,128]{1,0:T(8,128)(2,1)S(1)}, bf16[128,128]{1,0:T(8,128)(2,1)S(1)}, u32[]{:S(2)}, u32[]{:S(2)}) collective-permute-start(bf16[128,128]{1,0:T(8,128)(2,1)S(1)} %get-tuple-element.53), channel_id=1, source_target_pairs={{0,384},{64,448},{128,256},{192,320},{256,128},{320,192},{384,0},{... | collective-permute-start | bytes 98312 | tf_op jit(solution)/shard_map/ppermute | solution.py:242
  54.8 4.7 %collective-permute-start.9 = (bf16[128,128]{1,0:T(8,128)(2,1)S(1)}, bf16[128,128]{1,0:T(8,128)(2,1)S(1)}, u32[]{:S(2)}, u32[]{:S(2)}) collective-permute-start(bf16[128,128]{1,0:T(8,128)(2,1)S(1)} %get-tuple-element.51), channel_id=1, source_target_pairs={{0,128},{64,192},{128,0},{192,64},{256,384},{320,448},{384,256},{4... | collective-permute-start | bytes 98312 | tf_op jit(solution)/shard_map/ppermute | solution.py:242
  102.7 27.1 %all-to-all-start.4 = ((bf16[8,160,128]{2,1,0:T(8,128)(2,1)}), bf16[8,160,128]{2,1,0:T(8,128)(2,1)S(1)}, u32[]{:S(2)}, u32[]{:S(2)}) async-start(bf16[8,160,128]{2,1,0:T(8,128)(2,1)} %row_pack.1), calls=%async_computation.4 | async-start | bytes 655360 | tf_op jit(solution)/shard_map/all_to_all | solution.py:576
  110.8 5.5 %collective-permute-start.4 = (bf16[3,64,128]{2,1,0:T(8,128)(2,1)S(1)}, bf16[3,64,128]{2,1,0:T(8,128)(2,1)S(1)}, u32[]{:S(2)}, u32[]{:S(2)}) collective-permute-start(bf16[3,64,128]{2,1,0:T(8,128)(2,1)S(1)} %get-tuple-element.69), channel_id=1, source_target_pairs={{0,64},{64,128},{128,192},{192,256},{256,320},{320,384},{384,448},... | collective-permute-start | bytes 147464 | tf_op jit(solution)/shard_map/ppermute | solution.py:564
  114.3 5.4 %collective-permute-start.5 = (bf16[3,64,128]{2,1,0:T(8,128)(2,1)S(1)}, bf16[3,64,128]{2,1,0:T(8,128)(2,1)S(1)}, u32[]{:S(2)}, u32[]{:S(2)}) collective-permute-start(bf16[3,64,128]{2,1,0:T(8,128)(2,1)S(1)} %get-tuple-element.68), channel_id=1, source_target_pairs={{64,0},{128,64},{192,128},{256,192},{320,256},{384,320},{448,384},... | collective-permute-start | bytes 147464 | tf_op jit(solution)/shard_map/ppermute | solution.py:564
  120.6 4.5 %collective-permute-start.6 = (bf16[64,128]{1,0:T(8,128)(2,1)S(1)}, bf16[64,128]{1,0:T(8,128)(2,1)S(1)}, u32[]{:S(2)}, u32[]{:S(2)}) collective-permute-start(bf16[64,128]{1,0:T(8,128)(2,1)S(1)} %get-tuple-element.44), channel_id=1, source_target_pairs={{0,4},{4,8},{8,12},{12,16},{16,20},{20,24},{24,28},{28,32},{32,36}... | collective-permute-start | bytes 49160 | tf_op jit(solution)/shard_map/ppermute | solution.py:564
  123.2 4.5 %collective-permute-start.7 = (bf16[64,128]{1,0:T(8,128)(2,1)S(1)}, bf16[64,128]{1,0:T(8,128)(2,1)S(1)}, u32[]{:S(2)}, u32[]{:S(2)}) collective-permute-start(bf16[64,128]{1,0:T(8,128)(2,1)S(1)} %get-tuple-element.45), channel_id=1, source_target_pairs={{4,0},{8,4},{12,8},{16,12},{20,16},{24,20},{28,24},{32,28},{36,32}... | collective-permute-start | bytes 49160 | tf_op jit(solution)/shard_map/ppermute | solution.py:564

commit v10 on v9

--- a/solution.py
+++ b/solution.py
@@ -238,10 +238,10 @@
     if size == 2:
         return [keep, recv]
     chunks = spread(keep, recv, size // 2)
-    return [chunks[0]] + [
-        lax.ppermute(chunks[m], "row", [(i, i ^ (2 * m)) for i in range(size)])
-        for m in range(1, size // 2)
-    ]
+    out = [chunks[0]]
+    for m in range(1, size // 2):
+        out.append(lax.ppermute(chunks[m], "row", [(i, i ^ (2 * m)) for i in range(size)]))
+    return out
 
 
 def mlp_kernel(recv, w_exp, bias, w_red, payload, stats_out, send, keep, off, grads, s_norm, s_act, s_cot, s_gh):

time: 132 us -> 132 us (level)
  no operation moved by 1% of the time
where the time goes in v10:
time: 132 us; the launch traced here: 131 us
  starting transfers between devices  51 us (39%)
  blocking collectives  40.4 us (31%)
  waiting for transfers between devices  23.5 us (18%)
  Pallas kernels  11.3 us (9%)
  local copies, waits for them, and re-layouts  3.79 us (3%)
    all_to_all x2, blocking collectives, exchange(): return lax.all_to_all(x, axis, 0, 0)  40.4 us
    ppermute x8, starting transfers between devices, neighbours(): return (lax.ppermute(last, axis, up), lax.ppermute(first, axis, down))  23.3 us
    all_to_all x3, starting transfers between devices, exchange(): return lax.all_to_all(x, axis, 0, 0)  15.7 us
    pallas_call x11, Pallas kernels, call(): pl.pallas_call(kernel, out_shape=out_shape, in_specs=[spec] * len(args),...  11.3 us
    ppermute x8, waiting for transfers between devices, neighbours(): return (lax.ppermute(last, axis, up), lax.ppermute(first, axis, down))  10.1 us
    all_to_all x3, waiting for transfers between devices, exchange(): return lax.all_to_all(x, axis, 0, 0)  9.72 us
    ppermute x3, starting transfers between devices, reduce_rows(): lax.ppermute(chunks[m], 'row', [(i, i ^ 2 * m) for i in range(size)])  9.69 us
    unnamed x17, local copies, waits for them, and re-layouts  3 us
  transfers between devices with their start and end apart: 15, of which 8 were waited for; matrix products, arithmetic and copies ran while one was open for 2% of the time, Pallas kernels for 2%

profile of v10, /device:TPU:1, one launch (start us, length us, event | category | flops | bytes accessed | tf_op | source)
XLA Modules:
  0.0 130.8 jit_solution(16595048526519283435)
XLA Ops:
  0.6 0.9 copy.25
  1.5 4.6 %collective-permute-start = (bf16[3,64,128]{2,1,0:T(8,128)(2,1)S(1)}, bf16[3,64,128]{2,1,0:T(8,128)(2,1)S(1)}, u32[]{:S(2)}, u32[]{:S(2)}) collective-permute-start(bf16[3,64,128]{2,1,0:T(8,128)(2,1)S(1)} %get-tuple-element.71), channel_id=1, source_target_pairs={{0,64},{64,128},{128,192},{192,256},{256,320},{320,384},{384,448},... | collective-permute-start | bytes 147464 | tf_op jit(solution)/shard_map/ppermute | solution.py:564
  6.1 5.5 %collective-permute-start.1 = (bf16[3,64,128]{2,1,0:T(8,128)(2,1)S(1)}, bf16[3,64,128]{2,1,0:T(8,128)(2,1)S(1)}, u32[]{:S(2)}, u32[]{:S(2)}) collective-permute-start(bf16[3,64,128]{2,1,0:T(8,128)(2,1)S(1)} %get-tuple-element.70), channel_id=1, source_target_pairs={{64,0},{128,64},{192,128},{256,192},{320,256},{384,320},{448,384},... | collective-permute-start | bytes 147464 | tf_op jit(solution)/shard_map/ppermute | solution.py:564
  11.6 0.0 collective-permute-done.up
  11.6 0.8 collective-permute-done.1.down
  12.4 0.7 copy-done.2
  13.1 0.0 copy-done.3
  13.1 0.4 edges.2
  13.5 2.6 %collective-permute-start.2 = (bf16[64,128]{1,0:T(8,128)(2,1)S(1)}, bf16[64,128]{1,0:T(8,128)(2,1)S(1)}, u32[]{:S(2)}, u32[]{:S(2)}) collective-permute-start(bf16[64,128]{1,0:T(8,128)(2,1)S(1)} %get-tuple-element.34), channel_id=1, source_target_pairs={{0,4},{4,8},{8,12},{12,16},{16,20},{20,24},{24,28},{28,32},{32,36}... | collective-permute-start | bytes 49160 | tf_op jit(solution)/shard_map/ppermute | solution.py:564
  16.2 0.0 copy-start.5
  16.2 1.3 collective-permute-start.3
  17.5 0.1 copy.18.kern
  17.6 0.0 collective-permute-done.2.left
  17.6 3.2 %collective-permute-done.3.right = bf16[64,128]{1,0:T(8,128)(2,1)S(1)} collective-permute-done((bf16[64,128]{1,0:T(8,128)(2,1)S(1)}, bf16[64,128]{1,0:T(8,128)(2,1)S(1)}, u32[]{:S(2)}, u32[]{:S(2)}) %collective-permute-start.3) | collective-permute-done | bytes 16416 | tf_op jit(solution)/shard_map/ppermute | solution.py:564
  20.9 2.4 %forward.1 = (f32[64,512]{1,0:T(8,128)S(1)}, bf16[4,144,512]{2,1,0:T(8,128)(2,1)}) custom-call(bf16[3,64,128]{2,1,0:T(8,128)(2,1)S(1)} %collective-permute-done.up, bf16[4,64,128]{2,1,0:T(8,128)(2,1)S(1)} %bitcast.17, bf16[3,64,128]{2,1,0:T(8,128)(2,1)S(1)} %collective-permute-done.1.down, bf16[64,128]{1,0:T(8,128)(2,1)S(1)} %collective-permute-done.2.left, ...), custom_call_target="tpu_custom_call" | custom-call | tf_op jit(solution)/shard_map/forward/pallas_call | solution.py:28
  23.2 4.1 %all-to-all-start = ((bf16[4,144,512]{2,1,0:T(8,128)(2,1)}), bf16[4,144,512]{2,1,0:T(8,128)(2,1)S(1)}, u32[]{:S(2)}, u32[]{:S(2)}) async-start(bf16[4,144,512]{2,1,0:T(8,128)(2,1)} %get-tuple-element.37), calls=%async_computation | async-start | bytes 1179648 | tf_op jit(solution)/shard_map/all_to_all | solution.py:576
  27.4 0.8 dynamic_slice.3
  28.1 9.7 %all-to-all-done.recv = bf16[4,144,512]{2,1,0:T(8,128)(2,1)S(1)} async-done(((bf16[4,144,512]{2,1,0:T(8,128)(2,1)}), bf16[4,144,512]{2,1,0:T(8,128)(2,1)S(1)}, u32[]{:S(2)}, u32[]{:S(2)}) %all-to-all-start) | async-done | bytes 589856 | tf_op jit(solution)/shard_map/all_to_all | solution.py:576
  37.9 2.1 %mlp.1 = (bf16[4,144,512]{2,1,0:T(8,128)(2,1)}, f32[2,512]{1,0:T(2,128)S(1)}, f32[512,128]{1,0:T(8,128)S(1)}, f32[512,128]{1,0:T(8,128)S(1)}, f32[64,128]{1,0:T(8,128)S(1)}) custom-call(bf16[4,144,512]{2,1,0:T(8,128)(2,1)S(1)} %all-to-all-done.recv, bf16[256,256]{1,0:T(8,128)(2,1)S(1)} %copy-done, f32[1,256]{1,0:T(1,128)S(1)} %bitcast.27, ...), custom_call_target="tpu_custom_call" | custom-call | tf_op jit(solution)/shard_map/mlp/pallas_call | solution.py:28
  40.0 3.5 %all-to-all-start.1 = ((bf16[4,144,512]{2,1,0:T(8,128)(2,1)}), bf16[4,144,512]{2,1,0:T(8,128)(2,1)S(1)}, u32[]{:S(2)}, u32[]{:S(2)}) async-start(bf16[4,144,512]{2,1,0:T(8,128)(2,1)} %get-tuple-element.38), calls=%async_computation.1 | async-start | bytes 1179648 | tf_op jit(solution)/shard_map/all_to_all | solution.py:576
  43.5 2.3 %collective-permute-start.8 = (f32[512,128]{1,0:T(8,128)S(1)}, f32[512,128]{1,0:T(8,128)S(1)}, u32[]{:S(2)}, u32[]{:S(2)}) collective-permute-start(f32[512,128]{1,0:T(8,128)S(1)} %get-tuple-element.49), channel_id=1, source_target_pairs={{0,64},{64,0},{128,192},{192,128},{256,320},{320,256},{384,448},{4... | collective-permute-start | bytes 786440 | tf_op jit(solution)/shard_map/ppermute | solution.py:237
  45.8 1.1 collective-permute-done.8.recv
  47.0 4.8 %collective-permute-start.10 = (bf16[128,128]{1,0:T(8,128)(2,1)S(1)}, bf16[128,128]{1,0:T(8,128)(2,1)S(1)}, u32[]{:S(2)}, u32[]{:S(2)}) collective-permute-start(bf16[128,128]{1,0:T(8,128)(2,1)S(1)} %get-tuple-element.52), channel_id=1, source_target_pairs={{0,256},{64,320},{128,384},{192,448},{256,0},{320,64},{384,128},{4... | collective-permute-start | bytes 98312 | tf_op jit(solution)/shard_map/ppermute | solution.py:243
  51.8 3.0 %collective-permute-start.11 = (bf16[128,128]{1,0:T(8,128)(2,1)S(1)}, bf16[128,128]{1,0:T(8,128)(2,1)S(1)}, u32[]{:S(2)}, u32[]{:S(2)}) collective-permute-start(bf16[128,128]{1,0:T(8,128)(2,1)S(1)} %get-tuple-element.53), channel_id=1, source_target_pairs={{0,384},{64,448},{128,256},{192,320},{256,128},{320,192},{384,0},{... | collective-permute-start | bytes 98312 | tf_op jit(solution)/shard_map/ppermute | solution.py:243
  54.8 1.9 %collective-permute-start.9 = (bf16[128,128]{1,0:T(8,128)(2,1)S(1)}, bf16[128,128]{1,0:T(8,128)(2,1)S(1)}, u32[]{:S(2)}, u32[]{:S(2)}) collective-permute-start(bf16[128,128]{1,0:T(8,128)(2,1)S(1)} %get-tuple-element.51), channel_id=1, source_target_pairs={{0,128},{64,192},{128,0},{192,64},{256,384},{320,448},{384,256},{4... | collective-permute-start | bytes 98312 | tf_op jit(solution)/shard_map/ppermute | solution.py:243
  56.7 0.0 all-to-all-done.1.recv
  56.7 0.1 norm_back.1
  56.9 0.0 collective-permute-done.10.rest_2_
  56.9 0.8 collective-permute-done.11.rest_3_
  57.7 1.8 %collective-permute-done.9.rest_1_ = bf16[128,128]{1,0:T(8,128)(2,1)S(1)} collective-permute-done((bf16[128,128]{1,0:T(8,128)(2,1)S(1)}, bf16[128,128]{1,0:T(8,128)(2,1)S(1)}, u32[]{:S(2)}, u32[]{:S(2)}) %collective-permute-start.9) | collective-permute-done | bytes 32800 | tf_op jit(solution)/shard_map/ppermute | solution.py:243
  59.4 2.1 %tap_grad.1 = bf16[16,16,128]{2,1,0:T(8,128)(2,1)S(1)} custom-call(bf16[3,64,128]{2,1,0:T(8,128)(2,1)S(1)} %collective-permute-done.up, bf16[4,64,128]{2,1,0:T(8,128)(2,1)S(1)} %bitcast.19, bf16[3,64,128]{2,1,0:T(8,128)(2,1)S(1)} %collective-permute-done.1.down, bf16[64,128]{1,0:T(8,128)(2,1)S(1)} %collective-permute-done.2.left, ...), custom_call_target="tpu_custom_call" | custom-call | tf_op jit(solution)/shard_map/tap_grad/pallas_call | solution.py:28
  61.5 26.0 %all_to_all.25.recv = bf16[16,16,128]{2,1,0:T(8,128)(2,1)S(1)} all-to-all(bf16[16,16,128]{2,1,0:T(8,128)(2,1)S(1)} %tap_grad.1), channel_id=1, replica_groups=mesh['row'=8,'col'=16,'ch'=4] {'col'}, dimensions={0} | all-to-all | bytes 131072 | tf_op jit(solution)/shard_map/all_to_all | solution.py:576
  87.5 14.4 %all_to_all.26.recv = bf16[16,16,128]{2,1,0:T(8,128)(2,1)S(1)} all-to-all(bf16[16,16,128]{2,1,0:T(8,128)(2,1)S(1)} %col_pack.1), channel_id=1, replica_groups=mesh['row'=8,'col'=16,'ch'=4] {'col'}, dimensions={0} | all-to-all | bytes 131072 | tf_op jit(solution)/shard_map/all_to_all | solution.py:576
  101.9 0.8 row_pack.1
  102.7 8.1 %all-to-all-start.4 = ((bf16[8,160,128]{2,1,0:T(8,128)(2,1)}), bf16[8,160,128]{2,1,0:T(8,128)(2,1)S(1)}, u32[]{:S(2)}, u32[]{:S(2)}) async-start(bf16[8,160,128]{2,1,0:T(8,128)(2,1)} %row_pack.1), calls=%async_computation.4 | async-start | bytes 655360 | tf_op jit(solution)/shard_map/all_to_all | solution.py:576
  110.8 3.5 %collective-permute-start.4 = (bf16[3,64,128]{2,1,0:T(8,128)(2,1)S(1)}, bf16[3,64,128]{2,1,0:T(8,128)(2,1)S(1)}, u32[]{:S(2)}, u32[]{:S(2)}) collective-permute-start(bf16[3,64,128]{2,1,0:T(8,128)(2,1)S(1)} %get-tuple-element.69), channel_id=1, source_target_pairs={{0,64},{64,128},{128,192},{192,256},{256,320},{320,384},{384,448},... | collective-permute-start | bytes 147464 | tf_op jit(solution)/shard_map/ppermute | solution.py:564
  114.3 1.9 %collective-permute-start.5 = (bf16[3,64,128]{2,1,0:T(8,128)(2,1)S(1)}, bf16[3,64,128]{2,1,0:T(8,128)(2,1)S(1)}, u32[]{:S(2)}, u32[]{:S(2)}) collective-permute-start(bf16[3,64,128]{2,1,0:T(8,128)(2,1)S(1)} %get-tuple-element.68), channel_id=1, source_target_pairs={{64,0},{128,64},{192,128},{256,192},{320,256},{384,320},{448,384},... | collective-permute-start | bytes 147464 | tf_op jit(solution)/shard_map/ppermute | solution.py:564
  116.3 0.0 collective-permute-done.4.up
  116.3 3.5 %collective-permute-done.5.down = bf16[3,64,128]{2,1,0:T(8,128)(2,1)S(1)} collective-permute-done((bf16[3,64,128]{2,1,0:T(8,128)(2,1)S(1)}, bf16[3,64,128]{2,1,0:T(8,128)(2,1)S(1)}, u32[]{:S(2)}, u32[]{:S(2)}) %collective-permute-start.5) | collective-permute-done | bytes 49184 | tf_op jit(solution)/shard_map/ppermute | solution.py:564
  119.8 0.9 edges.3
  120.6 2.5 %collective-permute-start.6 = (bf16[64,128]{1,0:T(8,128)(2,1)S(1)}, bf16[64,128]{1,0:T(8,128)(2,1)S(1)}, u32[]{:S(2)}, u32[]{:S(2)}) collective-permute-start(bf16[64,128]{1,0:T(8,128)(2,1)S(1)} %get-tuple-element.44), channel_id=1, source_target_pairs={{0,4},{4,8},{8,12},{12,16},{16,20},{20,24},{24,28},{28,32},{32,36}... | collective-permute-start | bytes 49160 | tf_op jit(solution)/shard_map/ppermute | solution.py:564
  123.2 1.3 collective-permute-start.7
  124.5 0.7 copy.20
  125.2 0.0 collective-permute-done.6.left
  125.2 2.5 %collective-permute-done.7.right = bf16[64,128]{1,0:T(8,128)(2,1)S(1)} collective-permute-done((bf16[64,128]{1,0:T(8,128)(2,1)S(1)}, bf16[64,128]{1,0:T(8,128)(2,1)S(1)}, u32[]{:S(2)}, u32[]{:S(2)}) %collective-permute-start.7) | collective-permute-done | bytes 16416 | tf_op jit(solution)/shard_map/ppermute | solution.py:564
  127.7 1.5 %backward.1 = bf16[4,64,128]{2,1,0:T(8,128)(2,1)S(1)} custom-call(bf16[3,64,128]{2,1,0:T(8,128)(2,1)S(1)} %collective-permute-done.4.up, bf16[4,64,128]{2,1,0:T(8,128)(2,1)S(1)} %get-tuple-element.43.mid, bf16[3,64,128]{2,1,0:T(8,128)(2,1)S(1)} %collective-permute-done.5.down, bf16[64,128]{1,0:T(8,128)(2,1)S(1)} %collective-permute-done.6.left, ...), custom_call_target="tpu_custom_call" | custom-call | tf_op jit(solution)/shard_map/backward/pallas_call | solution.py:28
  129.1 0.7 copy.21
  129.8 1.0 final.1
  (15 shorter events, 0.1 us)
Async XLA Ops:
  1.5 10.1 %collective-permute-start = (bf16[3,64,128]{2,1,0:T(8,128)(2,1)S(1)}, bf16[3,64,128]{2,1,0:T(8,128)(2,1)S(1)}, u32[]{:S(2)}, u32[]{:S(2)}) collective-permute-start(bf16[3,64,128]{2,1,0:T(8,128)(2,1)S(1)} %get-tuple-element.71), channel_id=1, source_target_pairs={{0,64},{64,128},{128,192},{192,256},{256,320},{320,384},{384,448},... | collective-permute-start | bytes 147464 | tf_op jit(solution)/shard_map/ppermute | solution.py:564
  6.1 6.3 %collective-permute-start.1 = (bf16[3,64,128]{2,1,0:T(8,128)(2,1)S(1)}, bf16[3,64,128]{2,1,0:T(8,128)(2,1)S(1)}, u32[]{:S(2)}, u32[]{:S(2)}) collective-permute-start(bf16[3,64,128]{2,1,0:T(8,128)(2,1)S(1)} %get-tuple-element.70), channel_id=1, source_target_pairs={{64,0},{128,64},{192,128},{256,192},{320,256},{384,320},{448,384},... | collective-permute-start | bytes 147464 | tf_op jit(solution)/shard_map/ppermute | solution.py:564
  12.4 0.7 copy-start.2
  12.4 0.7 copy-start.3
  13.1 4.4 %copy-start.4 = (bf16[64,4,128]{2,1,0:T(4,128)(2,1)S(1)}, bf16[64,4,128]{2,1,0:T(4,128)(2,1)}, u32[]{:S(2)}) copy-start(bf16[64,4,128]{2,1,0:T(4,128)(2,1)} %param.15) | copy-start | bytes 196612
  13.5 4.1 %collective-permute-start.2 = (bf16[64,128]{1,0:T(8,128)(2,1)S(1)}, bf16[64,128]{1,0:T(8,128)(2,1)S(1)}, u32[]{:S(2)}, u32[]{:S(2)}) collective-permute-start(bf16[64,128]{1,0:T(8,128)(2,1)S(1)} %get-tuple-element.34), channel_id=1, source_target_pairs={{0,4},{4,8},{8,12},{12,16},{16,20},{20,24},{24,28},{28,32},{32,36}... | collective-permute-start | bytes 49160 | tf_op jit(solution)/shard_map/ppermute | solution.py:564
  16.2 1.3 %copy-start.5 = (f32[64,49]{0,1:T(8,128)S(1)}, f32[64,49]{0,1:T(8,128)}, u32[]{:S(2)}) copy-start(f32[64,49]{0,1:T(8,128)} %param.9) | copy-start | bytes 37636
  16.2 4.7 %collective-permute-start.3 = (bf16[64,128]{1,0:T(8,128)(2,1)S(1)}, bf16[64,128]{1,0:T(8,128)(2,1)S(1)}, u32[]{:S(2)}, u32[]{:S(2)}) collective-permute-start(bf16[64,128]{1,0:T(8,128)(2,1)S(1)} %get-tuple-element.35), channel_id=1, source_target_pairs={{4,0},{8,4},{12,8},{16,12},{20,16},{24,20},{28,24},{32,28},{36,32}... | collective-permute-start | bytes 49160 | tf_op jit(solution)/shard_map/ppermute | solution.py:564
  23.2 14.6 %copy-start = (bf16[256,256]{1,0:T(8,128)(2,1)S(1)}, bf16[256,256]{1,0:T(8,128)(2,1)}, u32[]{:S(2)}) copy-start(bf16[256,256]{1,0:T(8,128)(2,1)} %w_exp.1) | copy-start | bytes 393220
  23.2 14.6 %copy-start.1 = (bf16[256,256]{1,0:T(8,128)(2,1)S(1)}, bf16[256,256]{1,0:T(8,128)(2,1)}, u32[]{:S(2)}) copy-start(bf16[256,256]{1,0:T(8,128)(2,1)} %w_red.1) | copy-start | bytes 393220
  23.2 14.6 %all-to-all-start = ((bf16[4,144,512]{2,1,0:T(8,128)(2,1)}), bf16[4,144,512]{2,1,0:T(8,128)(2,1)S(1)}, u32[]{:S(2)}, u32[]{:S(2)}) async-start(bf16[4,144,512]{2,1,0:T(8,128)(2,1)} %get-tuple-element.37), calls=%async_computation | async-start | bytes 1179648 | tf_op jit(solution)/shard_map/all_to_all | solution.py:576
  40.0 16.7 %all-to-all-start.1 = ((bf16[4,144,512]{2,1,0:T(8,128)(2,1)}), bf16[4,144,512]{2,1,0:T(8,128)(2,1)S(1)}, u32[]{:S(2)}, u32[]{:S(2)}) async-start(bf16[4,144,512]{2,1,0:T(8,128)(2,1)} %get-tuple-element.38), calls=%async_computation.1 | async-start | bytes 1179648 | tf_op jit(solution)/shard_map/all_to_all | solution.py:576
  43.5 3.5 %collective-permute-start.8 = (f32[512,128]{1,0:T(8,128)S(1)}, f32[512,128]{1,0:T(8,128)S(1)}, u32[]{:S(2)}, u32[]{:S(2)}) collective-permute-start(f32[512,128]{1,0:T(8,128)S(1)} %get-tuple-element.49), channel_id=1, source_target_pairs={{0,64},{64,0},{128,192},{192,128},{256,320},{320,256},{384,448},{4... | collective-permute-start | bytes 786440 | tf_op jit(solution)/shard_map/ppermute | solution.py:237
  47.0 9.9 %collective-permute-start.10 = (bf16[128,128]{1,0:T(8,128)(2,1)S(1)}, bf16[128,128]{1,0:T(8,128)(2,1)S(1)}, u32[]{:S(2)}, u32[]{:S(2)}) collective-permute-start(bf16[128,128]{1,0:T(8,128)(2,1)S(1)} %get-tuple-element.52), channel_id=1, source_target_pairs={{0,256},{64,320},{128,384},{192,448},{256,0},{320,64},{384,128},{4... | collective-permute-start | bytes 98312 | tf_op jit(solution)/shard_map/ppermute | solution.py:243
  51.8 5.9 %collective-permute-start.11 = (bf16[128,128]{1,0:T(8,128)(2,1)S(1)}, bf16[128,128]{1,0:T(8,128)(2,1)S(1)}, u32[]{:S(2)}, u32[]{:S(2)}) collective-permute-start(bf16[128,128]{1,0:T(8,128)(2,1)S(1)} %get-tuple-element.53), channel_id=1, source_target_pairs={{0,384},{64,448},{128,256},{192,320},{256,128},{320,192},{384,0},{... | collective-permute-start | bytes 98312 | tf_op jit(solution)/shard_map/ppermute | solution.py:243
  54.8 4.7 %collective-permute-start.9 = (bf16[128,128]{1,0:T(8,128)(2,1)S(1)}, bf16[128,128]{1,0:T(8,128)(2,1)S(1)}, u32[]{:S(2)}, u32[]{:S(2)}) collective-permute-start(bf16[128,128]{1,0:T(8,128)(2,1)S(1)} %get-tuple-element.51), channel_id=1, source_target_pairs={{0,128},{64,192},{128,0},{192,64},{256,384},{320,448},{384,256},{4... | collective-permute-start | bytes 98312 | tf_op jit(solution)/shard_map/ppermute | solution.py:243
  102.7 27.1 %all-to-all-start.4 = ((bf16[8,160,128]{2,1,0:T(8,128)(2,1)}), bf16[8,160,128]{2,1,0:T(8,128)(2,1)S(1)}, u32[]{:S(2)}, u32[]{:S(2)}) async-start(bf16[8,160,128]{2,1,0:T(8,128)(2,1)} %row_pack.1), calls=%async_computation.4 | async-start | bytes 655360 | tf_op jit(solution)/shard_map/all_to_all | solution.py:576
  110.8 5.5 %collective-permute-start.4 = (bf16[3,64,128]{2,1,0:T(8,128)(2,1)S(1)}, bf16[3,64,128]{2,1,0:T(8,128)(2,1)S(1)}, u32[]{:S(2)}, u32[]{:S(2)}) collective-permute-start(bf16[3,64,128]{2,1,0:T(8,128)(2,1)S(1)} %get-tuple-element.69), channel_id=1, source_target_pairs={{0,64},{64,128},{128,192},{192,256},{256,320},{320,384},{384,448},... | collective-permute-start | bytes 147464 | tf_op jit(solution)/shard_map/ppermute | solution.py:564
  114.3 5.4 %collective-permute-start.5 = (bf16[3,64,128]{2,1,0:T(8,128)(2,1)S(1)}, bf16[3,64,128]{2,1,0:T(8,128)(2,1)S(1)}, u32[]{:S(2)}, u32[]{:S(2)}) collective-permute-start(bf16[3,64,128]{2,1,0:T(8,128)(2,1)S(1)} %get-tuple-element.68), channel_id=1, source_target_pairs={{64,0},{128,64},{192,128},{256,192},{320,256},{384,320},{448,384},... | collective-permute-start | bytes 147464 | tf_op jit(solution)/shard_map/ppermute | solution.py:564
  120.6 4.5 %collective-permute-start.6 = (bf16[64,128]{1,0:T(8,128)(2,1)S(1)}, bf16[64,128]{1,0:T(8,128)(2,1)S(1)}, u32[]{:S(2)}, u32[]{:S(2)}) collective-permute-start(bf16[64,128]{1,0:T(8,128)(2,1)S(1)} %get-tuple-element.44), channel_id=1, source_target_pairs={{0,4},{4,8},{8,12},{12,16},{16,20},{20,24},{24,28},{28,32},{32,36}... | collective-permute-start | bytes 49160 | tf_op jit(solution)/shard_map/ppermute | solution.py:564
  123.2 4.5 %collective-permute-start.7 = (bf16[64,128]{1,0:T(8,128)(2,1)S(1)}, bf16[64,128]{1,0:T(8,128)(2,1)S(1)}, u32[]{:S(2)}, u32[]{:S(2)}) collective-permute-start(bf16[64,128]{1,0:T(8,128)(2,1)S(1)} %get-tuple-element.45), channel_id=1, source_target_pairs={{4,0},{8,4},{12,8},{16,12},{20,16},{24,20},{28,24},{32,28},{36,32}... | collective-permute-start | bytes 49160 | tf_op jit(solution)/shard_map/ppermute | solution.py:564
